TPU v7x, 128 devices: a whole 4x4x4 slice. The times are simulated.
128 devices in a mesh: lon: 16 (over y, x_hi, core), lat: 8 (over x_lo, z).
Axes of the slice: x: 4 (x_hi: 2, x_lo: 2; x = x_hi * 2 + x_lo), y: 4, z: 4, core: 2. Of those that a mesh axis runs over, the one named last changes fastest.
Arguments:
- coarse: bfloat16 [12, 16, 16384], P(None, None, ('lon', 'lat')), may hold values from -6 to 6
- target: float32 [4, 16, 16384], P(None, 'lat', 'lon'), may hold values from -6 to 6
- noise: float32 [4, 16, 16384], P(None, 'lat', 'lon'), may hold values from -6 to 6
- land_mask: int32 [16, 16384], P('lat', 'lon'), may hold values 0 or 1
- level_index: int32 [8, 16], P('lat', 'lon'), may hold values from 0 to 31
- frozen_first: bfloat16 [3, 3, 128, 12], replicated, may hold values from -0.625 to 0.625
- frozen_middle: bfloat16 [3, 3, 128, 128], replicated, may hold values from -0.1875 to 0.1875
- frozen_last: bfloat16 [3, 3, 4, 128], replicated, may hold values from -0.1875 to 0.1875
- diffuse_in: bfloat16 [3, 3, 128, 20], replicated, may hold values from -0.4375 to 0.4375
- diffuse_down: bfloat16 [3, 3, 256, 128], replicated, may hold values from -0.1875 to 0.1875
- diffuse_up: bfloat16 [3, 3, 128, 256], replicated, may hold values from -0.125 to 0.125
- diffuse_out: bfloat16 [3, 3, 4, 128], replicated, may hold values from -0.1875 to 0.1875
Outputs:
- denoised: float32 [4, 16, 16384], P(None, 'lat', 'lon')
- grad_in: float32 [3, 3, 128, 20], replicated
- grad_down: float32 [3, 3, 256, 128], replicated
- grad_up: float32 [3, 3, 128, 256], replicated
- grad_last: float32 [3, 3, 4, 128], replicated
All inputs are finite; a program needn't handle non-finite values. No bound on the sum of `land_mask` on one device may be relied on, other than what follows from the above.
Results may differ from a plain program's by a relative error of at most 0.0044.
Values may be sent and summed in bfloat16 or wider, within the bound.
No kernel may reach another device: no remote copies, remote signals or barrier semaphores. Data moves between devices by JAX's collectives and lax.ppermute only.
A program may use at most 128 MiB of HBM per device.

v0:
```python
import math

import jax
import jax.numpy as jnp
from jax import lax
from jax.experimental import pallas as pl
from jax.experimental.pallas import tpu as pltpu
from jax.sharding import Mesh
from jax.sharding import PartitionSpec as P

LEVELS = 32
ROWS = 16
LOW = ROWS // 2
OWN = 128
HALO = 16
WIDE = OWN + 2 * HALO
WLOW = WIDE // 2
LANES = 256
HID1 = 128
HID2 = 256
BF = jnp.bfloat16
F32 = jnp.float32

LON = ("y", "x_hi", "core")
LAT = ("x_lo", "z")
CHIPS = ("y", "x_hi", "x_lo", "z")
STRIPS = LON + LAT

FIELDS = 24
UP_ROWS = 9 * HID1
DOWN_ROWS = 9 * HID2
BIG_ROWS = 2304
LAST_ROWS = 72
IN_ROWS = 9 * FIELDS
HALF_ROWS = 2560


def mm(x, w):
    return lax.dot_general(x, w, (((1,), (0,)), ((), ())), preferred_element_type=F32)


def mm_nt(x, w):
    return lax.dot_general(x, w, (((1,), (1,)), ((), ())), preferred_element_type=F32)


def mm_tn(x, w):
    return lax.dot_general(x, w, (((0,), (0,)), ((), ())), preferred_element_type=F32)


def back(x, axis):
    return pltpu.roll(x, x.shape[axis] - 1, axis)


def ahead(x, axis):
    return pltpu.roll(x, 1, axis)


def with_halo(own, left, right):
    lane = lax.broadcasted_iota(jnp.int32, own.shape, 1)
    halo = jnp.where(lane < HALO, right, jnp.where(lane >= OWN - HALO, left, 0.0))
    return jnp.concatenate([own, halo], axis=1)


def to_cells(stack):
    pad = OWN - stack.shape[0]
    if pad:
        stack = jnp.concatenate([stack, jnp.zeros((pad, LANES), F32)], axis=0)
    cells = stack.T
    return jnp.concatenate([cells[: OWN + HALO], cells[LANES - HALO :]], axis=0).astype(BF)


def to_lanes(cells):
    gap = jnp.zeros((LANES - WIDE, cells.shape[1]), cells.dtype)
    return jnp.concatenate([cells[: OWN + HALO], gap, cells[OWN + HALO :]], axis=0)


def lon_shifts(field):
    return jnp.concatenate([ahead(field, 1), field, back(field, 1)], axis=0)


def three_rows(ref, start, count):
    width = ref.shape[1]
    return jnp.concatenate(
        [ref[pl.ds(start + a, count)].reshape(count * width, ref.shape[2]) for a in range(3)], axis=1
    )


def lon_sum(taps, count, width, out):
    first, second, third = (
        taps[:, b * out : (b + 1) * out].reshape(count, width, out) for b in range(3)
    )
    return ahead(first, 1) + second + back(third, 1)


def four_channels(ref, row):
    sums = []
    for b in range(3):
        at = [(a * 3 + b) * 8 for a in range(3)]
        sums.append(
            ref[row, at[0] : at[0] + 8]
            + ref[row + 1, at[1] : at[1] + 8]
            + ref[row + 2, at[2] : at[2] + 8]
        )
    return ahead(sums[0], 1) + sums[1] + back(sums[2], 1)


def zero_edges(ref):
    edge = jnp.zeros(ref.shape[1:], ref.dtype)
    ref[0] = edge
    ref[ref.shape[0] - 1] = edge


def each(count, body, unroll=1):
    def step(i, carry):
        body(i)
        return carry

    lax.fori_loop(0, count, step, 0, unroll=unroll)


def pack_kernel(target, noise, land_mask, level, packed):
    power = level[...].astype(F32) / (LEVELS - 1)
    sigma = jnp.broadcast_to(0.02 * jnp.exp(power * math.log(4000.0)), (1, OWN))
    weight = 1.0 + land_mask[...].astype(F32)
    for p in range(packed.shape[0]):
        lanes = slice(p * OWN, (p + 1) * OWN)
        for r in range(2):
            packed[p, r, 0:1] = weight[r : r + 1, lanes]
            packed[p, r, 1:2] = sigma
            packed[p, r, 2:4] = jnp.zeros((2, OWN), F32)
            packed[p, r, 4:8] = target[:, r, lanes]
            packed[p, r, 8:12] = jnp.zeros((4, OWN), F32)
            packed[p, r, 12:16] = noise[:, r, lanes]


def stack_inputs(ref, weight, room):
    ref[...] = jnp.zeros_like(ref)
    count = weight.shape[2]
    for a in range(3):
        for b in range(3):
            ref[a, b * room : b * room + count] = weight[a, b].astype(F32)
    return ref[...].astype(BF).reshape(3 * OWN, OWN)


def stack_outputs(ref, weight):
    ref[...] = jnp.zeros_like(ref)
    for a in range(3):
        for b in range(3):
            at = (a * 3 + b) * 8 + 4
            ref[at : at + 4] = weight[a, b].astype(F32)
    return ref[...].astype(BF)


def step_kernel(
    scale,
    place,
    own,
    left,
    right,
    w_first,
    w_middle,
    w_last,
    w_in,
    w_down,
    w_up,
    w_out,
    grads,
    *rest,
):
    lats = 8
    tiles, scratch = rest[:lats], rest[lats:]
    (
        stack,
        stack_o,
        field,
        net,
        hid,
        act_c,
        taps,
        residuals,
        noisies,
        slope_a,
        act_a,
        pairs,
        pooled,
        act_b,
        slope_b,
        up_taps,
        phases,
        slope_c,
        grad_f,
        spread_f,
        back_c,
        grad_c,
        blocks,
        grad_b,
        grad_a,
        last_sum,
        den,
    ) = scratch
    for ref in (net, hid, pooled, up_taps, taps, grad_f, grad_c, grad_b):
        zero_edges(ref)
    first_w = stack_inputs(stack, w_first, 16)

    def gather(r):
        wide = with_halo(own[r], left[r], right[r])
        field[r] = wide
        net[r + 1] = to_cells(lon_shifts(wide[8:24]))

    each(ROWS, gather, 4)

    def first(i):
        pre = mm(three_rows(net, 4 * i, 4), first_w)
        hid[pl.ds(4 * i + 1, 4)] = jax.nn.silu(pre).astype(BF).reshape(4, WIDE, HID1)

    each(ROWS // 4, first)
    middle_w = jnp.concatenate([w_middle[a] for a in range(3)], axis=1)

    def second(i):
        pre = lon_sum(mm_nt(three_rows(hid, 4 * i, 4), middle_w), 4, WIDE, HID1)
        act_c[pl.ds(4 * i, 4)] = jax.nn.silu(pre).astype(BF)

    each(ROWS // 4, second)
    last_w = stack_outputs(stack_o, w_last)[0:72]

    def mean_taps(r):
        taps[r + 1] = mm_nt(last_w, to_lanes(act_c[r]))

    each(ROWS, mean_taps, 4)
    in_w = stack_inputs(stack, w_in, FIELDS)
    lane = lax.broadcasted_iota(jnp.int32, (8, LANES), 1)
    held = (lane < OWN + HALO) | (lane >= LANES - HALO)
    low_half = lax.broadcasted_iota(jnp.int32, (8, LANES), 0) < 4

    def enter(r):
        mean_r = four_channels(taps, r).astype(BF).astype(F32)
        sigma = jnp.where(held, jnp.broadcast_to(field[r, 1:2], (8, LANES)), 1.0)
        residual = field[r, 0:8] - mean_r
        noisy = residual + sigma * field[r, 16:24]
        variance = sigma * sigma + 0.25
        residuals[r] = residual
        noisies[r] = noisy
        scaled = (lax.rsqrt(variance) * noisy).astype(BF).astype(F32)
        both = jnp.where(low_half, pltpu.roll(mean_r, 4, 0), scaled)
        net[r + 1] = to_cells(lon_shifts(jnp.concatenate([both, field[r, 8:24]], axis=0)))

    each(ROWS, enter, 4)

    def level_one(i):
        pre = mm(three_rows(net, 4 * i, 4), in_w)
        gate = jax.nn.sigmoid(pre)
        slope_a[pl.ds(4 * i, 4)] = (gate * (1.0 + pre * (1.0 - gate))).reshape(4, WIDE, HID1)
        act = (pre * gate).astype(BF).reshape(4, WIDE, HID1)
        act_a[pl.ds(4 * i, 4)] = act
        wide = act.astype(F32)
        for k in range(2):
            pairs[k] = wide[2 * k] + wide[2 * k + 1]
            total = pairs[k, pl.ds(0, WLOW, stride=2)] + pairs[k, pl.ds(1, WLOW, stride=2)]
            pooled[2 * i + k + 1] = (0.25 * total).astype(BF)

    each(ROWS // 4, level_one)
    down_w = jnp.concatenate([w_down[a] for a in range(3)], axis=1)

    def level_two(i):
        pre = lon_sum(mm_nt(three_rows(pooled, 2 * i, 2), down_w), 2, WLOW, HID2)
        gate = jax.nn.sigmoid(pre)
        slope_b[pl.ds(2 * i, 2)] = gate * (1.0 + pre * (1.0 - gate))
        act_b[pl.ds(2 * i, 2)] = (pre * gate).astype(BF)

    each(LOW // 2, level_two)

    def up_products(i):
        low = act_b[pl.ds(2 * i, 2)].reshape(2 * WLOW, HID2)
        up_taps[pl.ds(2 * i + 1, 2)] = mm_nt(low, w_up[...]).reshape(2, WLOW, 9 * HID1)

    each(LOW // 2, up_products)

    def level_three(i):
        for pi in range(2):
            sums = []
            for b in range(3):
                total = None
                for a in range(3):
                    row = i + 1 + (pi + a - 1) // 2
                    at = (a * 3 + b) * HID1
                    part = up_taps[row, :, at : at + HID1]
                    total = part if total is None else total + part
                sums.append(total)
            phases[pi, pl.ds(0, WLOW, stride=2)] = ahead(sums[0], 0) + sums[1] + sums[2]
            phases[pi, pl.ds(1, WLOW, stride=2)] = sums[0] + sums[1] + back(sums[2], 0)
            row = 2 * i + pi
            pre = phases[pi]
            gate = jax.nn.sigmoid(pre)
            act_c[row] = (pre * gate + act_a[row].astype(F32)).astype(BF)
            slope_c[row] = gate * (1.0 + pre * (1.0 - gate))

    each(LOW, level_three)
    out_w = stack_outputs(stack_o, w_out)

    def field_taps(r):
        taps[r + 1] = mm_nt(out_w[0:72], to_lanes(act_c[r]))

    each(ROWS, field_taps, 4)

    def loss(r):
        value = four_channels(taps, r)
        sigma = jnp.where(held, jnp.broadcast_to(field[r, 1:2], (8, LANES)), 1.0)
        weight = jnp.broadcast_to(field[r, 0:1], (8, LANES))
        variance = sigma * sigma + 0.25
        c_out = 0.5 * sigma * lax.rsqrt(variance)
        lam = variance / (0.25 * sigma * sigma)
        denoised = (0.25 / variance) * noisies[r] + c_out * value
        den[r] = denoised[4:8, :OWN]
        loss_grad = (2.0 * scale) * weight * lam * (denoised - residuals[r])
        cot = (c_out * loss_grad).astype(BF).astype(F32)
        grad_f[r + 1] = jnp.where(low_half, 0.0, cot)

    each(ROWS, loss, 4)
    lat = place[1]
    for k in range(lats):
        tiles[k][...] = den[pl.ds(2 * lax.rem(lat + k, lats), 2)]
    last_sum[...] = jnp.zeros_like(last_sum)

    def last_grads(r):
        parts = []
        for a in range(3):
            cot = grad_f[r + 2 - a]
            parts += [back(cot, 1), cot, ahead(cot, 1)]
        cots = jnp.concatenate(parts + [jnp.zeros((8, LANES), F32)], axis=0)
        last_sum[...] += mm(cots[:, :OWN].astype(BF), act_c[r, 0:OWN])
        spread_f[r] = to_cells(cots)

    each(ROWS, last_grads, 4)
    near, far = place[0], 1 - place[0]

    def keep(half, at, value):
        grads[pl.ds(half, 1), at : at + value.shape[0]] = value.astype(BF)[None]

    keep(near, BIG_ROWS, last_sum[0:LAST_ROWS])
    keep(near, BIG_ROWS + LAST_ROWS, jnp.zeros((HALF_ROWS - BIG_ROWS - LAST_ROWS, OWN), F32))

    def back_three(i):
        wide = mm(spread_f[pl.ds(4 * i, 4)].reshape(4 * WIDE, OWN), out_w)
        wide = wide.reshape(4, WIDE, HID1)
        back_c[pl.ds(4 * i, 4)] = wide
        grad_c[pl.ds(4 * i + 1, 4)] = wide * slope_c[pl.ds(4 * i, 4)]

    each(ROWS // 4, back_three)

    def block_sums(i):
        even = [grad_c[2 * i + k, pl.ds(0, WLOW, stride=2)] for k in range(4)]
        odd = [grad_c[2 * i + k, pl.ds(1, WLOW, stride=2)] for k in range(4)]
        for a in range(3):
            e, o = even[2 - a] + even[3 - a], odd[2 - a] + odd[3 - a]
            for b, total in enumerate((o + back(e, 0), e + o, ahead(o, 0) + e)):
                at = (a * 3 + b) * HID1
                blocks[i, :, at : at + HID1] = total.astype(BF)

    each(LOW, block_sums)

    def back_two(i):
        low = mm(blocks[pl.ds(2 * i, 2)].reshape(2 * WLOW, 9 * HID1), w_up[...])
        cot = low.reshape(2, WLOW, HID2) * slope_b[pl.ds(2 * i, 2)]
        shifts = jnp.concatenate([back(cot, 1), cot, ahead(cot, 1)], axis=2)
        grad_b[pl.ds(2 * i + 1, 2)] = shifts.astype(BF)

    each(LOW // 2, back_two)
    own_low = lax.broadcasted_iota(jnp.int32, (LOW, WLOW, HID2), 1) < OWN // 2
    low_b = jnp.where(own_low, act_b[...].astype(F32), 0.0).astype(BF).reshape(LOW * WLOW, HID2)
    for k in range(3):
        left_side = blocks[:, :, 3 * HID1 * k : 3 * HID1 * (k + 1)].reshape(LOW * WLOW, 3 * HID1)
        up = mm_tn(left_side, low_b)
        keep(near, 3 * HID1 * k, up[:, :HID1])
        keep(near, 3 * HID1 * k + UP_ROWS, up[:, HID1:])
    own_one = lax.broadcasted_iota(jnp.int32, (LOW, WLOW, HID1), 1) < OWN // 2
    low_a = jnp.concatenate(
        [
            jnp.where(own_one, pooled[a : a + LOW].astype(F32), 0.0).astype(BF).reshape(LOW * WLOW, HID1)
            for a in range(3)
        ],
        axis=1,
    )
    for b in range(3):
        left_side = grad_b[1 : LOW + 1, :, HID2 * b : HID2 * (b + 1)].reshape(LOW * WLOW, HID2)
        down = mm_tn(left_side, low_a)
        for a in range(3):
            keep(far, (a * 3 + b) * HID2, down[:, HID1 * a : HID1 * (a + 1)])
    own_wide = lax.broadcasted_iota(jnp.int32, (WIDE, HID1), 0) < OWN

    def back_one(i):
        total = None
        for a in range(3):
            cot = grad_b[pl.ds(2 * i + 2 - a, 2)].reshape(2 * WLOW, 3 * HID2)
            part = mm(cot, w_down[a])
            total = part if total is None else total + part
        low = (0.25 * total).reshape(2, WLOW, HID1)
        for k in range(2):
            phases[k, pl.ds(0, WLOW, stride=2)] = low[k]
            phases[k, pl.ds(1, WLOW, stride=2)] = low[k]
            for pi in range(2):
                row = 4 * i + 2 * k + pi
                cot = (back_c[row] + phases[k]) * slope_a[row]
                grad_a[row] = jnp.where(own_wide, cot, 0.0).astype(BF)

    each(LOW // 2, back_one)
    inputs = mm_tn(three_rows(net, 0, ROWS), grad_a[...].reshape(ROWS * WIDE, HID1))
    for a in range(3):
        keep(far, BIG_ROWS + a * 3 * FIELDS, inputs[a * OWN : a * OWN + 3 * FIELDS])
    keep(far, BIG_ROWS + IN_ROWS, jnp.zeros((HALF_ROWS - BIG_ROWS - IN_ROWS, OWN), F32))


def unpack_kernel(place, mine, other, *rest):
    tiles, (tile, first, down, up, last) = rest[:8], rest[8:]
    a = pl.program_id(0)
    even = place[0] == 0

    def half(k, at, count):
        rows = pl.ds(pl.multiple_of(at, 8), count)
        if k == 0:
            return jnp.where(even, mine[rows].astype(F32), other[rows].astype(F32))
        return jnp.where(even, other[rows].astype(F32), mine[rows].astype(F32))

    low = half(0, a * (3 * HID1), 3 * HID1).reshape(3, HID1, HID1)
    high = half(0, a * (3 * HID1) + UP_ROWS, 3 * HID1).reshape(3, HID1, HID1)
    up[0] = jnp.concatenate([low, high], axis=2)
    down[0] = half(1, a * (3 * HID2), 3 * HID2).reshape(3, HID2, HID1)
    firsts = half(1, BIG_ROWS + a * (3 * FIELDS), 3 * FIELDS)
    lasts = half(0, BIG_ROWS + a * FIELDS, FIELDS)
    for b in range(3):
        first[0, b] = firsts[b * FIELDS : b * FIELDS + 20]
        last[0, b] = lasts[b * 8 + 4 : b * 8 + 8]

    @pl.when(a == 0)
    def _():
        for k in range(8):
            at = pl.multiple_of(lax.rem(place[1] + 8 - k, 8) * OWN, OWN)
            for r in range(2):
                tile[:, r, pl.ds(at, OWN)] = tiles[k][r]


def in_vmem(count):
    return [pl.BlockSpec(memory_space=pltpu.MemorySpace.VMEM) for _ in range(count)]


def in_smem():
    return pl.BlockSpec(memory_space=pltpu.MemorySpace.SMEM)


def pack(target, noise, land_mask, level_index):
    lats = target.shape[2] // OWN
    return pl.pallas_call(
        pack_kernel,
        out_shape=jax.ShapeDtypeStruct((lats, 2, 16, OWN), F32),
        in_specs=in_vmem(4),
        out_specs=in_vmem(1)[0],
        name="pack",
    )(target, noise, land_mask, level_index)


def step(scale, *operands):
    def kernel(*refs):
        step_kernel(scale, *refs)

    return pl.pallas_call(
        kernel,
        out_shape=(
            jax.ShapeDtypeStruct((2, HALF_ROWS, OWN), BF),
            *([jax.ShapeDtypeStruct((2, 4, OWN), F32)] * 8),
        ),
        in_specs=[in_smem(), *in_vmem(10)],
        out_specs=tuple(in_vmem(9)),
        scratch_shapes=[
            pltpu.VMEM((3, OWN, OWN), F32),
            pltpu.VMEM((OWN, OWN), F32),
            pltpu.VMEM((ROWS, FIELDS, LANES), F32),
            pltpu.VMEM((ROWS + 2, WIDE, OWN), BF),
            pltpu.VMEM((ROWS + 2, WIDE, HID1), BF),
            pltpu.VMEM((ROWS, WIDE, HID1), BF),
            pltpu.VMEM((ROWS + 2, 72, LANES), F32),
            pltpu.VMEM((ROWS, 8, LANES), F32),
            pltpu.VMEM((ROWS, 8, LANES), F32),
            pltpu.VMEM((ROWS, WIDE, HID1), F32),
            pltpu.VMEM((ROWS, WIDE, HID1), BF),
            pltpu.VMEM((2, WIDE, HID1), F32),
            pltpu.VMEM((LOW + 2, WLOW, HID1), BF),
            pltpu.VMEM((LOW, WLOW, HID2), BF),
            pltpu.VMEM((LOW, WLOW, HID2), F32),
            pltpu.VMEM((LOW + 2, WLOW, 9 * HID1), F32),
            pltpu.VMEM((2, WIDE, HID1), F32),
            pltpu.VMEM((ROWS, WIDE, HID1), F32),
            pltpu.VMEM((ROWS + 2, 8, LANES), F32),
            pltpu.VMEM((ROWS, WIDE, OWN), BF),
            pltpu.VMEM((ROWS, WIDE, HID1), F32),
            pltpu.VMEM((ROWS + 2, WIDE, HID1), F32),
            pltpu.VMEM((LOW, WLOW, 9 * HID1), BF),
            pltpu.VMEM((LOW + 2, WLOW, 3 * HID2), BF),
            pltpu.VMEM((ROWS, WIDE, HID1), BF),
            pltpu.VMEM((80, HID1), F32),
            pltpu.VMEM((ROWS, 4, OWN), F32),
        ],
        name="step",
    )(*operands)


def unpack(place, mine, other, tiles):
    whole = pl.BlockSpec((HALF_ROWS, OWN), lambda a: (0, 0))
    part = pl.BlockSpec((2, 4, OWN), lambda a: (0, 0, 0))

    def taps(rows, lanes):
        return pl.BlockSpec((1, 3, rows, lanes), lambda a: (a, 0, 0, 0))

    return pl.pallas_call(
        unpack_kernel,
        grid=(3,),
        out_shape=(
            jax.ShapeDtypeStruct((4, 2, 8 * OWN), F32),
            jax.ShapeDtypeStruct((3, 3, 20, HID1), F32),
            jax.ShapeDtypeStruct((3, 3, HID2, HID1), F32),
            jax.ShapeDtypeStruct((3, 3, HID1, HID2), F32),
            jax.ShapeDtypeStruct((3, 3, 4, HID1), F32),
        ),
        in_specs=[in_smem(), whole, whole, *([part] * 8)],
        out_specs=(
            pl.BlockSpec((4, 2, 8 * OWN), lambda a: (0, 0, 0)),
            taps(20, HID1),
            taps(HID2, HID1),
            taps(HID1, HID2),
            taps(4, HID1),
        ),
        name="unpack",
    )(place, mine, other, *tiles)


def all_to_all(value, axes):
    return lax.all_to_all(value, axes, split_axis=0, concat_axis=0, tiled=True)


def shift_by(value, axes, step):
    count = lax.axis_size(axes)
    return lax.ppermute(value, axes, [(i, (i + step) % count) for i in range(count)])


def local(
    coarse,
    target,
    noise,
    land_mask,
    level_index,
    frozen_first,
    frozen_middle,
    frozen_last,
    diffuse_in,
    diffuse_down,
    diffuse_up,
    diffuse_out,
):
    scale = 1.0 / (target.shape[0] * math.sqrt(target.shape[1] * target.shape[2] * lax.axis_size(STRIPS)))
    place = jnp.stack([lax.axis_index("core"), lax.axis_index(LAT)]).astype(jnp.int32)
    packed = all_to_all(pack(target, noise, land_mask, level_index), LAT).reshape(ROWS, 16, OWN)
    fields = jnp.concatenate([packed[:, :8], coarse.transpose(1, 0, 2).astype(F32), packed[:, 12:]], axis=1)
    grads, *tiles = step(
        scale,
        place,
        fields,
        shift_by(fields, STRIPS, 1),
        shift_by(fields, STRIPS, -1),
        frozen_first.transpose(0, 1, 3, 2),
        frozen_middle.reshape(3, 3 * HID1, HID1),
        frozen_last,
        diffuse_in.transpose(0, 1, 3, 2),
        diffuse_down.reshape(3, 3 * HID2, HID1),
        diffuse_up.reshape(9 * HID1, HID2),
        diffuse_out,
    )
    chips = lax.axis_size(CHIPS)
    half = grads[0].astype(F32) + shift_by(grads[1], "core", 1).astype(F32)
    with jax.named_scope("scatter"):
        parts = all_to_all(half.astype(BF).reshape(chips, HALF_ROWS // chips, OWN), CHIPS)
    with jax.named_scope("tiles"):
        tiles = [tiles[0], *(shift_by(tiles[k], LAT, k) for k in range(1, 8))]
    total = parts.astype(F32).sum(0).astype(BF)
    with jax.named_scope("spread"):
        mine = all_to_all(jnp.broadcast_to(total[None], parts.shape), CHIPS).reshape(HALF_ROWS, OWN)
    tile, first, down, up, last = unpack(place, mine, shift_by(mine, "core", 1), tiles)
    return (tile, first.transpose(0, 1, 3, 2), down, up, last)


def solution(mesh):
    fine = Mesh(mesh.devices.reshape(4, 2, 2, 2, 4), LON + LAT)
    tile = P(None, LAT, LON)
    return jax.shard_map(
        local,
        mesh=fine,
        in_specs=(
            P(None, None, STRIPS),
            tile,
            tile,
            P(LAT, LON),
            P(LAT, LON),
            *([P()] * 7),
        ),
        out_specs=(tile, P(), P(), P(), P()),
        check_vma=False,
    )
```

profile of v0, /device:TPU:1, one launch (start us, length us, event | category | flops | bytes accessed | tf_op | source)
XLA Modules:
  0.0 109.6 jit_solution(11766774447005787389)
XLA Ops:
  1.3 1.5 %pack.1 = f32[8,2,16,128]{3,2,1,0:T(8,128)} custom-call(f32[4,2,1024]{2,1,0:T(2,128)} %target.1, f32[4,2,1024]{2,1,0:T(2,128)} %noise.1, s32[2,1024]{1,0:T(2,128)} %land_mask.1, s32[1,1]{1,0:T(1,128)S(6)} %copy.21.level), custom_call_target="tpu_custom_call" | custom-call | tf_op jit(solution)/shard_map/pack/pallas_call | solution.py:451
  2.8 6.8 %all-to-all-start = ((f32[8,2,16,128]{3,2,1,0:T(8,128)}), f32[8,2,16,128]{3,2,1,0:T(8,128)S(1)}, u32[]{:S(2)}, u32[]{:S(2)}) async-start(f32[8,2,16,128]{3,2,1,0:T(8,128)} %pack.1), calls=%async_computation | async-start | bytes 262144 | tf_op jit(solution)/shard_map/all_to_all | solution.py:535
  9.6 0.8 copy.20
  10.4 4.6 %all-to-all-done = f32[8,2,16,128]{3,2,1,0:T(8,128)S(1)} async-done(((f32[8,2,16,128]{3,2,1,0:T(8,128)}), f32[8,2,16,128]{3,2,1,0:T(8,128)S(1)}, u32[]{:S(2)}, u32[]{:S(2)}) %all-to-all-start) | async-done | bytes 131104 | tf_op jit(solution)/shard_map/all_to_all | solution.py:535
  15.1 3.2 %collective-permute-start.1 = (f32[16,24,128]{2,1,0:T(8,128)S(1)}, f32[16,24,128]{2,1,0:T(8,128)S(1)}, u32[]{:S(2)}, u32[]{:S(2)}) collective-permute-start(f32[16,24,128]{2,1,0:T(8,128)S(1)} %pad_maximum_fusion.refs_1_), channel_id=1, source_target_pairs={{0,127},{1,0},{2,1},{3,2},{4,3},{5,4},{6,5},{7,6},{8,7},{9,8},{10,... | collective-permute-start | bytes 589832 | tf_op jit(solution)/shard_map/ppermute | solution.py:540
  18.3 0.6 pad_add_fusion.refs_0_.place
  18.9 3.1 %collective-permute-done.1.refs_3_ = f32[16,24,128]{2,1,0:T(8,128)S(1)} collective-permute-done((f32[16,24,128]{2,1,0:T(8,128)S(1)}, f32[16,24,128]{2,1,0:T(8,128)S(1)}, u32[]{:S(2)}, u32[]{:S(2)}) %collective-permute-start.1) | collective-permute-done | bytes 196640 | tf_op jit(solution)/shard_map/ppermute | solution.py:540
  22.0 3.5 %collective-permute-done.refs_2_ = f32[16,24,128]{2,1,0:T(8,128)S(1)} collective-permute-done((f32[16,24,128]{2,1,0:T(8,128)S(1)}, f32[16,24,128]{2,1,0:T(8,128)S(1)}, u32[]{:S(2)}, u32[]{:S(2)}) %collective-permute-start) | collective-permute-done | bytes 196640 | tf_op jit(solution)/shard_map/ppermute | solution.py:540
  25.5 0.7 copy-done.5
  26.2 22.2 %step.1 = (bf16[2,2560,128]{2,1,0:T(8,128)(2,1)}, f32[2,4,128]{2,1,0:T(4,128)}, f32[2,4,128]{2,1,0:T(4,128)}, f32[2,4,128]{2,1,0:T(4,128)}, f32[2,4,128]{2,1,0:T...) custom-call(s32[2]{0:T(128)} %pad_add_fusion.refs_0_.place, ...), custom_call_target="tpu_custom_call" | custom-call | tf_op jit(solution)/shard_map/step/pallas_call | solution.py:464
  48.5 1.2 %slice_bitcast_fusion = bf16[2560,128]{1,0:T(8,128)(2,1)S(1)} fusion(bf16[2,2560,128]{2,1,0:T(8,128)(2,1)} %get-tuple-element.19), kind=kLoop, calls=%fused_computation.2 | loop fusion | bytes 1310720 | tf_op jit(solution)/shard_map/squeeze | solution.py:576
  49.7 5.6 %collective-permute-start.2 = (bf16[2560,128]{1,0:T(8,128)(2,1)S(1)}, bf16[2560,128]{1,0:T(8,128)(2,1)S(1)}, u32[]{:S(2)}, u32[]{:S(2)}) collective-permute-start(bf16[2560,128]{1,0:T(8,128)(2,1)S(1)} %slice_bitcast_fusion), channel_id=1, source_target_pairs={{0,8},{8,0},{1,9},{9,1},{2,10},{10,2},{3,11},{11,3},{4,12},{12,4},... | collective-permute-start | bytes 1966088 | tf_op jit(solution)/shard_map/ppermute | solution.py:540
  55.3 1.7 %collective-permute-done.2 = bf16[2560,128]{1,0:T(8,128)(2,1)S(1)} collective-permute-done((bf16[2560,128]{1,0:T(8,128)(2,1)S(1)}, bf16[2560,128]{1,0:T(8,128)(2,1)S(1)}, u32[]{:S(2)}, u32[]{:S(2)}) %collective-permute-start.2) | collective-permute-done | bytes 655392 | tf_op jit(solution)/shard_map/ppermute | solution.py:540
  57.0 0.2 fusion
  57.2 17.7 %all_to_all.15 = bf16[64,40,128]{2,1,0:T(8,128)(2,1)S(1)} all-to-all(bf16[64,40,128]{2,1,0:T(8,128)(2,1)S(1)} %bitcast.21), channel_id=1, replica_groups=mesh['y'=4,'x_hi'=2,'core'=2,'x_lo'=2,'z'=4] {'y','x_hi','x_lo','z'}, dimensions={0} | all-to-all | bytes 1310720 | tf_op jit(solution)/shard_map/scatter/all_to_all | solution.py:535
  74.9 0.1 reduce_sum.12
  75.1 0.1 broadcast_in_dim.2
  75.1 17.1 %all_to_all.16 = bf16[64,40,128]{2,1,0:T(8,128)(2,1)S(1)} all-to-all(bf16[64,40,128]{2,1,0:T(8,128)(2,1)S(1)} %broadcast_in_dim.2), channel_id=1, replica_groups=mesh['y'=4,'x_hi'=2,'core'=2,'x_lo'=2,'z'=4] {'y','x_hi','x_lo','z'}, dimensions={0} | all-to-all | bytes 1310720 | tf_op jit(solution)/shard_map/spread/all_to_all | solution.py:535
  92.3 3.0 %collective-permute-start.3 = (bf16[2560,128]{1,0:T(8,128)(2,1)S(1)}, bf16[2560,128]{1,0:T(8,128)(2,1)S(1)}, u32[]{:S(2)}, u32[]{:S(2)}) collective-permute-start(bf16[2560,128]{1,0:T(8,128)(2,1)S(1)} %bitcast.19), channel_id=1, source_target_pairs={{0,8},{8,0},{1,9},{9,1},{2,10},{10,2},{3,11},{11,3},{4,12},{12,4},... | collective-permute-start | bytes 1966088 | tf_op jit(solution)/shard_map/ppermute | solution.py:540
  95.2 0.4 collective-permute-start.4
  95.6 1.1 collective-permute-start.5
  96.7 1.3 %collective-permute-start.6 = (f32[2,4,128]{2,1,0:T(4,128)S(1)}, f32[2,4,128]{2,1,0:T(4,128)S(1)}, u32[]{:S(2)}, u32[]{:S(2)}) collective-permute-start(f32[2,4,128]{2,1,0:T(4,128)S(1)} %copy-done.17), channel_id=1, source_target_pairs={{0,3},{1,4},{2,5},{3,6},{4,7},{5,0},{6,1},{7,2},{8,11},{9,12},{10,... | collective-permute-start | bytes 12296 | tf_op jit(solution)/shard_map/tiles/ppermute | solution.py:540
  98.0 1.3 %collective-permute-start.7 = (f32[2,4,128]{2,1,0:T(4,128)S(1)}, f32[2,4,128]{2,1,0:T(4,128)S(1)}, u32[]{:S(2)}, u32[]{:S(2)}) collective-permute-start(f32[2,4,128]{2,1,0:T(4,128)S(1)} %copy-done.16), channel_id=1, source_target_pairs={{0,4},{1,5},{2,6},{3,7},{4,0},{5,1},{6,2},{7,3},{8,12},{9,13},{10,... | collective-permute-start | bytes 12296 | tf_op jit(solution)/shard_map/tiles/ppermute | solution.py:540
  99.3 0.5 collective-permute-done.4.rest_1_
  99.8 0.1 collective-permute-start.8
  99.9 0.6 collective-permute-done.5.rest_2_
  100.5 2.0 %collective-permute-start.9 = (f32[2,4,128]{2,1,0:T(4,128)S(1)}, f32[2,4,128]{2,1,0:T(4,128)S(1)}, u32[]{:S(2)}, u32[]{:S(2)}) collective-permute-start(f32[2,4,128]{2,1,0:T(4,128)S(1)} %copy-done.14), channel_id=1, source_target_pairs={{0,6},{1,7},{2,0},{3,1},{4,2},{5,3},{6,4},{7,5},{8,14},{9,15},{10,... | collective-permute-start | bytes 12296 | tf_op jit(solution)/shard_map/tiles/ppermute | solution.py:540
  102.6 2.1 %collective-permute-start.10 = (f32[2,4,128]{2,1,0:T(4,128)S(1)}, f32[2,4,128]{2,1,0:T(4,128)S(1)}, u32[]{:S(2)}, u32[]{:S(2)}) collective-permute-start(f32[2,4,128]{2,1,0:T(4,128)S(1)} %copy-done.13), channel_id=1, source_target_pairs={{0,7},{1,0},{2,1},{3,2},{4,3},{5,4},{6,5},{7,6},{8,15},{9,8},{10,9... | collective-permute-start | bytes 12296 | tf_op jit(solution)/shard_map/tiles/ppermute | solution.py:540
  104.7 0.7 collective-permute-done.10.rest_7_
  105.5 0.5 copy-done.12
  106.0 0.3 copy-done.3
  106.3 3.3 %unpack.1 = (f32[4,2,1024]{2,1,0:T(2,128)}, f32[3,3,20,128]{3,2,1,0:T(8,128)}, f32[3,3,256,128]{3,2,1,0:T(8,128)}, f32[3,3,128,256]{3,2,1,0:T(8,128)}, f32[3,3,4,128]{3,2,1,0:T(4,128)}) custom-call(s32[2]{0:T(128)} %pad_add_fusion.refs_0_.place, bf16[2560,128]{1,0:T(8,128)(2,1)} %bitcast.20, bf16[2560,128]{1,0:T(8,128)(2,1)} %copy-done.3, ...), custom_call_target="tpu_custom_call" | custom-call | tf_op jit(solution)/shard_map/unpack/pallas_call | solution.py:512
  (46 shorter events, 0.1 us)
Async XLA Ops:
  2.8 12.2 %all-to-all-start = ((f32[8,2,16,128]{3,2,1,0:T(8,128)}), f32[8,2,16,128]{3,2,1,0:T(8,128)S(1)}, u32[]{:S(2)}, u32[]{:S(2)}) async-start(f32[8,2,16,128]{3,2,1,0:T(8,128)} %pack.1), calls=%async_computation | async-start | bytes 262144 | tf_op jit(solution)/shard_map/all_to_all | solution.py:535
  15.1 10.4 %copy-start.2 = (f32[16,24,128]{2,1,0:T(8,128)}, f32[16,24,128]{2,1,0:T(8,128)S(1)}, u32[]{:S(2)}) copy-start(f32[16,24,128]{2,1,0:T(8,128)S(1)} %pad_maximum_fusion.refs_1_) | copy-start | bytes 589828
  15.1 6.9 %collective-permute-start.1 = (f32[16,24,128]{2,1,0:T(8,128)S(1)}, f32[16,24,128]{2,1,0:T(8,128)S(1)}, u32[]{:S(2)}, u32[]{:S(2)}) collective-permute-start(f32[16,24,128]{2,1,0:T(8,128)S(1)} %pad_maximum_fusion.refs_1_), channel_id=1, source_target_pairs={{0,127},{1,0},{2,1},{3,2},{4,3},{5,4},{6,5},{7,6},{8,7},{9,8},{10,... | collective-permute-start | bytes 589832 | tf_op jit(solution)/shard_map/ppermute | solution.py:540
  18.3 7.2 %collective-permute-start = (f32[16,24,128]{2,1,0:T(8,128)S(1)}, f32[16,24,128]{2,1,0:T(8,128)S(1)}, u32[]{:S(2)}, u32[]{:S(2)}) collective-permute-start(f32[16,24,128]{2,1,0:T(8,128)S(1)} %pad_maximum_fusion.refs_1_), channel_id=1, source_target_pairs={{0,1},{1,2},{2,3},{3,4},{4,5},{5,6},{6,7},{7,8},{8,9},{9,10},{10,1... | collective-permute-start | bytes 589832 | tf_op jit(solution)/shard_map/ppermute | solution.py:540
  22.0 3.5 %copy-start.4 = (f32[16,24,128]{2,1,0:T(8,128)}, f32[16,24,128]{2,1,0:T(8,128)S(1)}, u32[]{:S(2)}) copy-start(f32[16,24,128]{2,1,0:T(8,128)S(1)} %collective-permute-done.1.refs_3_) | copy-start | bytes 589828
  25.5 0.7 copy-start.5
  48.5 8.6 %copy-start.1 = (bf16[2,2560,128]{2,1,0:T(8,128)(2,1)S(1)}, bf16[2,2560,128]{2,1,0:T(8,128)(2,1)}, u32[]{:S(2)}) copy-start(bf16[2,2560,128]{2,1,0:T(8,128)(2,1)} %get-tuple-element.19) | copy-start | bytes 3932164
  49.7 7.3 %collective-permute-start.2 = (bf16[2560,128]{1,0:T(8,128)(2,1)S(1)}, bf16[2560,128]{1,0:T(8,128)(2,1)S(1)}, u32[]{:S(2)}, u32[]{:S(2)}) collective-permute-start(bf16[2560,128]{1,0:T(8,128)(2,1)S(1)} %slice_bitcast_fusion), channel_id=1, source_target_pairs={{0,8},{8,0},{1,9},{9,1},{2,10},{10,2},{3,11},{11,3},{4,12},{12,4},... | collective-permute-start | bytes 1966088 | tf_op jit(solution)/shard_map/ppermute | solution.py:540
  74.9 20.4 %copy-start.19 = (f32[2,4,128]{2,1,0:T(4,128)S(1)}, f32[2,4,128]{2,1,0:T(4,128)}, u32[]{:S(2)}) copy-start(f32[2,4,128]{2,1,0:T(4,128)} %get-tuple-element.21) | copy-start | bytes 12292
  74.9 20.8 %copy-start.18 = (f32[2,4,128]{2,1,0:T(4,128)S(1)}, f32[2,4,128]{2,1,0:T(4,128)}, u32[]{:S(2)}) copy-start(f32[2,4,128]{2,1,0:T(4,128)} %get-tuple-element.22) | copy-start | bytes 12292
  74.9 21.8 %copy-start.17 = (f32[2,4,128]{2,1,0:T(4,128)S(1)}, f32[2,4,128]{2,1,0:T(4,128)}, u32[]{:S(2)}) copy-start(f32[2,4,128]{2,1,0:T(4,128)} %get-tuple-element.23) | copy-start | bytes 12292
  74.9 23.1 %copy-start.16 = (f32[2,4,128]{2,1,0:T(4,128)S(1)}, f32[2,4,128]{2,1,0:T(4,128)}, u32[]{:S(2)}) copy-start(f32[2,4,128]{2,1,0:T(4,128)} %get-tuple-element.24) | copy-start | bytes 12292
  74.9 24.9 %copy-start.15 = (f32[2,4,128]{2,1,0:T(4,128)S(1)}, f32[2,4,128]{2,1,0:T(4,128)}, u32[]{:S(2)}) copy-start(f32[2,4,128]{2,1,0:T(4,128)} %get-tuple-element.25) | copy-start | bytes 12292
  74.9 25.6 %copy-start.14 = (f32[2,4,128]{2,1,0:T(4,128)S(1)}, f32[2,4,128]{2,1,0:T(4,128)}, u32[]{:S(2)}) copy-start(f32[2,4,128]{2,1,0:T(4,128)} %get-tuple-element.26) | copy-start | bytes 12292
  74.9 27.6 %copy-start.13 = (f32[2,4,128]{2,1,0:T(4,128)S(1)}, f32[2,4,128]{2,1,0:T(4,128)}, u32[]{:S(2)}) copy-start(f32[2,4,128]{2,1,0:T(4,128)} %get-tuple-element.27) | copy-start | bytes 12292
  92.3 13.2 %copy-start = (bf16[64,40,128]{2,1,0:T(8,128)(2,1)}, bf16[64,40,128]{2,1,0:T(8,128)(2,1)S(1)}, u32[]{:S(2)}) copy-start(bf16[64,40,128]{2,1,0:T(8,128)(2,1)S(1)} %all_to_all.16) | copy-start | bytes 1966084
  92.3 13.2 %collective-permute-start.3 = (bf16[2560,128]{1,0:T(8,128)(2,1)S(1)}, bf16[2560,128]{1,0:T(8,128)(2,1)S(1)}, u32[]{:S(2)}, u32[]{:S(2)}) collective-permute-start(bf16[2560,128]{1,0:T(8,128)(2,1)S(1)} %bitcast.19), channel_id=1, source_target_pairs={{0,8},{8,0},{1,9},{9,1},{2,10},{10,2},{3,11},{11,3},{4,12},{12,4},... | collective-permute-start | bytes 1966088 | tf_op jit(solution)/shard_map/ppermute | solution.py:540
  95.2 4.6 %collective-permute-start.4 = (f32[2,4,128]{2,1,0:T(4,128)S(1)}, f32[2,4,128]{2,1,0:T(4,128)S(1)}, u32[]{:S(2)}, u32[]{:S(2)}) collective-permute-start(f32[2,4,128]{2,1,0:T(4,128)S(1)} %copy-done.19), channel_id=1, source_target_pairs={{0,1},{1,2},{2,3},{3,4},{4,5},{5,6},{6,7},{7,0},{8,9},{9,10},{10,1... | collective-permute-start | bytes 12296 | tf_op jit(solution)/shard_map/tiles/ppermute | solution.py:540
  95.6 4.9 %collective-permute-start.5 = (f32[2,4,128]{2,1,0:T(4,128)S(1)}, f32[2,4,128]{2,1,0:T(4,128)S(1)}, u32[]{:S(2)}, u32[]{:S(2)}) collective-permute-start(f32[2,4,128]{2,1,0:T(4,128)S(1)} %copy-done.18), channel_id=1, source_target_pairs={{0,2},{1,3},{2,4},{3,5},{4,6},{5,7},{6,0},{7,1},{8,10},{9,11},{10,... | collective-permute-start | bytes 12296 | tf_op jit(solution)/shard_map/tiles/ppermute | solution.py:540
  96.7 5.8 %collective-permute-start.6 = (f32[2,4,128]{2,1,0:T(4,128)S(1)}, f32[2,4,128]{2,1,0:T(4,128)S(1)}, u32[]{:S(2)}, u32[]{:S(2)}) collective-permute-start(f32[2,4,128]{2,1,0:T(4,128)S(1)} %copy-done.17), channel_id=1, source_target_pairs={{0,3},{1,4},{2,5},{3,6},{4,7},{5,0},{6,1},{7,2},{8,11},{9,12},{10,... | collective-permute-start | bytes 12296 | tf_op jit(solution)/shard_map/tiles/ppermute | solution.py:540
  98.0 6.7 %collective-permute-start.7 = (f32[2,4,128]{2,1,0:T(4,128)S(1)}, f32[2,4,128]{2,1,0:T(4,128)S(1)}, u32[]{:S(2)}, u32[]{:S(2)}) collective-permute-start(f32[2,4,128]{2,1,0:T(4,128)S(1)} %copy-done.16), channel_id=1, source_target_pairs={{0,4},{1,5},{2,6},{3,7},{4,0},{5,1},{6,2},{7,3},{8,12},{9,13},{10,... | collective-permute-start | bytes 12296 | tf_op jit(solution)/shard_map/tiles/ppermute | solution.py:540
  99.8 5.7 %copy-start.6 = (f32[2,4,128]{2,1,0:T(4,128)}, f32[2,4,128]{2,1,0:T(4,128)S(1)}, u32[]{:S(2)}) copy-start(f32[2,4,128]{2,1,0:T(4,128)S(1)} %collective-permute-done.4.rest_1_) | copy-start | bytes 12292
  99.8 4.9 %collective-permute-start.8 = (f32[2,4,128]{2,1,0:T(4,128)S(1)}, f32[2,4,128]{2,1,0:T(4,128)S(1)}, u32[]{:S(2)}, u32[]{:S(2)}) collective-permute-start(f32[2,4,128]{2,1,0:T(4,128)S(1)} %copy-done.15), channel_id=1, source_target_pairs={{0,5},{1,6},{2,7},{3,0},{4,1},{5,2},{6,3},{7,4},{8,13},{9,14},{10,... | collective-permute-start | bytes 12296 | tf_op jit(solution)/shard_map/tiles/ppermute | solution.py:540
  100.5 5.0 %copy-start.7 = (f32[2,4,128]{2,1,0:T(4,128)}, f32[2,4,128]{2,1,0:T(4,128)S(1)}, u32[]{:S(2)}) copy-start(f32[2,4,128]{2,1,0:T(4,128)S(1)} %collective-permute-done.5.rest_2_) | copy-start | bytes 12292
  100.5 4.2 %collective-permute-start.9 = (f32[2,4,128]{2,1,0:T(4,128)S(1)}, f32[2,4,128]{2,1,0:T(4,128)S(1)}, u32[]{:S(2)}, u32[]{:S(2)}) collective-permute-start(f32[2,4,128]{2,1,0:T(4,128)S(1)} %copy-done.14), channel_id=1, source_target_pairs={{0,6},{1,7},{2,0},{3,1},{4,2},{5,3},{6,4},{7,5},{8,14},{9,15},{10,... | collective-permute-start | bytes 12296 | tf_op jit(solution)/shard_map/tiles/ppermute | solution.py:540
  102.6 2.9 %copy-start.8 = (f32[2,4,128]{2,1,0:T(4,128)}, f32[2,4,128]{2,1,0:T(4,128)S(1)}, u32[]{:S(2)}) copy-start(f32[2,4,128]{2,1,0:T(4,128)S(1)} %collective-permute-done.6.rest_3_) | copy-start | bytes 12292
  102.6 2.9 %collective-permute-start.10 = (f32[2,4,128]{2,1,0:T(4,128)S(1)}, f32[2,4,128]{2,1,0:T(4,128)S(1)}, u32[]{:S(2)}, u32[]{:S(2)}) collective-permute-start(f32[2,4,128]{2,1,0:T(4,128)S(1)} %copy-done.13), channel_id=1, source_target_pairs={{0,7},{1,0},{2,1},{3,2},{4,3},{5,4},{6,5},{7,6},{8,15},{9,8},{10,9... | collective-permute-start | bytes 12296 | tf_op jit(solution)/shard_map/tiles/ppermute | solution.py:540
  104.7 0.8 copy-start.9
  104.7 0.8 copy-start.10
  104.7 0.8 copy-start.11
  105.4 0.6 copy-start.12
  105.5 0.9 copy-start.3
where the time goes:
time: 112 us; the launch traced here: 110 us
  blocking collectives  34.8 us (31%)
  Pallas kernels  27.1 us (24%)
  starting transfers between devices  26.9 us (24%)
  waiting for transfers between devices  14.8 us (13%)
  local copies, waits for them, and re-layouts  3.7 us (3%)
  between operations  1.46 us (1%)
    all_to_all x2, blocking collectives, all_to_all(): return lax.all_to_all(value, axes, split_axis=0, concat_axis=0, tiled=True)  34.8 us
    pallas_call x1, Pallas kernels, step(): pl.pallas_call(kernel, out_shape=(jax.ShapeDtypeStruct((2, HALF_ROWS, OWN...  22.2 us
    ppermute x11, starting transfers between devices, shift_by(): lax.ppermute(value, axes, [(i, (i + step) % count) for i in range(count)])  20.1 us
    ppermute x11, waiting for transfers between devices, shift_by(): lax.ppermute(value, axes, [(i, (i + step) % count) for i in range(count)])  10.2 us
    all_to_all x1, starting transfers between devices, all_to_all(): return lax.all_to_all(value, axes, split_axis=0, concat_axis=0, tiled=True)  6.78 us
    all_to_all x1, waiting for transfers between devices, all_to_all(): return lax.all_to_all(value, axes, split_axis=0, concat_axis=0, tiled=True)  4.63 us
    pallas_call x1, Pallas kernels, unpack(): pl.pallas_call(unpack_kernel, grid=(3,), out_shape=(jax.ShapeDtypeStruct(...  3.31 us
  transfers between devices with their start and end apart: 12, of which 7 were waited for; matrix products, arithmetic and copies ran while one was open for 1% of the time, Pallas kernels for 0%

commit v1 on v0

--- a/solution.py
+++ b/solution.py
@@ -33,6 +33,19 @@
 LAST_ROWS = 72
 IN_ROWS = 9 * FIELDS
 HALF_ROWS = 2560
+CELL_ROWS = 8
+CHUNK = {
+    "first": (4, 1),
+    "second": (4, 1),
+    "one": (4, 1),
+    "two": (2, 1),
+    "up": (2, 1),
+    "back_three": (4, 1),
+    "back_two": (2, 1),
+    "back_one": (2, 1),
+    "three": 1,
+    "blocks": 1,
+}
 
 
 def mm(x, w):
@@ -165,10 +178,9 @@
     w_up,
     w_out,
     grads,
-    *rest,
+    tiles,
+    *scratch,
 ):
-    lats = 8
-    tiles, scratch = rest[:lats], rest[lats:]
     (
         stack,
         stack_o,
@@ -209,18 +221,22 @@
 
     each(ROWS, gather, 4)
 
+    n1, u1 = CHUNK["first"]
+
     def first(i):
-        pre = mm(three_rows(net, 4 * i, 4), first_w)
-        hid[pl.ds(4 * i + 1, 4)] = jax.nn.silu(pre).astype(BF).reshape(4, WIDE, HID1)
-
-    each(ROWS // 4, first)
+        pre = mm(three_rows(net, n1 * i, n1), first_w)
+        hid[pl.ds(n1 * i + 1, n1)] = jax.nn.silu(pre).astype(BF).reshape(n1, WIDE, HID1)
+
+    each(ROWS // n1, first, u1)
     middle_w = jnp.concatenate([w_middle[a] for a in range(3)], axis=1)
 
+    n2, u2 = CHUNK["second"]
+
     def second(i):
-        pre = lon_sum(mm_nt(three_rows(hid, 4 * i, 4), middle_w), 4, WIDE, HID1)
-        act_c[pl.ds(4 * i, 4)] = jax.nn.silu(pre).astype(BF)
-
-    each(ROWS // 4, second)
+        pre = lon_sum(mm_nt(three_rows(hid, n2 * i, n2), middle_w), n2, WIDE, HID1)
+        act_c[pl.ds(n2 * i, n2)] = jax.nn.silu(pre).astype(BF)
+
+    each(ROWS // n2, second, u2)
     last_w = stack_outputs(stack_o, w_last)[0:72]
 
     def mean_taps(r):
@@ -246,34 +262,40 @@
 
     each(ROWS, enter, 4)
 
+    n3, u3 = CHUNK["one"]
+
     def level_one(i):
-        pre = mm(three_rows(net, 4 * i, 4), in_w)
+        pre = mm(three_rows(net, n3 * i, n3), in_w)
         gate = jax.nn.sigmoid(pre)
-        slope_a[pl.ds(4 * i, 4)] = (gate * (1.0 + pre * (1.0 - gate))).reshape(4, WIDE, HID1)
-        act = (pre * gate).astype(BF).reshape(4, WIDE, HID1)
-        act_a[pl.ds(4 * i, 4)] = act
+        slope_a[pl.ds(n3 * i, n3)] = (gate * (1.0 + pre * (1.0 - gate))).reshape(n3, WIDE, HID1)
+        act = (pre * gate).astype(BF).reshape(n3, WIDE, HID1)
+        act_a[pl.ds(n3 * i, n3)] = act
         wide = act.astype(F32)
-        for k in range(2):
-            pairs[k] = wide[2 * k] + wide[2 * k + 1]
-            total = pairs[k, pl.ds(0, WLOW, stride=2)] + pairs[k, pl.ds(1, WLOW, stride=2)]
-            pooled[2 * i + k + 1] = (0.25 * total).astype(BF)
-
-    each(ROWS // 4, level_one)
+        for k in range(n3 // 2):
+            row = (n3 // 2) * i + k
+            pairs[row] = wide[2 * k] + wide[2 * k + 1]
+            total = pairs[row, pl.ds(0, WLOW, stride=2)] + pairs[row, pl.ds(1, WLOW, stride=2)]
+            pooled[row + 1] = (0.25 * total).astype(BF)
+
+    each(ROWS // n3, level_one, u3)
     down_w = jnp.concatenate([w_down[a] for a in range(3)], axis=1)
 
+    n4, u4 = CHUNK["two"]
+
     def level_two(i):
-        pre = lon_sum(mm_nt(three_rows(pooled, 2 * i, 2), down_w), 2, WLOW, HID2)
+        pre = lon_sum(mm_nt(three_rows(pooled, n4 * i, n4), down_w), n4, WLOW, HID2)
         gate = jax.nn.sigmoid(pre)
-        slope_b[pl.ds(2 * i, 2)] = gate * (1.0 + pre * (1.0 - gate))
-        act_b[pl.ds(2 * i, 2)] = (pre * gate).astype(BF)
-
-    each(LOW // 2, level_two)
+        slope_b[pl.ds(n4 * i, n4)] = gate * (1.0 + pre * (1.0 - gate))
+        act_b[pl.ds(n4 * i, n4)] = (pre * gate).astype(BF)
+
+    each(LOW // n4, level_two, u4)
+    n5, u5 = CHUNK["up"]
 
     def up_products(i):
-        low = act_b[pl.ds(2 * i, 2)].reshape(2 * WLOW, HID2)
-        up_taps[pl.ds(2 * i + 1, 2)] = mm_nt(low, w_up[...]).reshape(2, WLOW, 9 * HID1)
-
-    each(LOW // 2, up_products)
+        low = act_b[pl.ds(n5 * i, n5)].reshape(n5 * WLOW, HID2)
+        up_taps[pl.ds(n5 * i + 1, n5)] = mm_nt(low, w_up[...]).reshape(n5, WLOW, 9 * HID1)
+
+    each(LOW // n5, up_products, u5)
 
     def level_three(i):
         for pi in range(2):
@@ -286,15 +308,15 @@
                     part = up_taps[row, :, at : at + HID1]
                     total = part if total is None else total + part
                 sums.append(total)
-            phases[pi, pl.ds(0, WLOW, stride=2)] = ahead(sums[0], 0) + sums[1] + sums[2]
-            phases[pi, pl.ds(1, WLOW, stride=2)] = sums[0] + sums[1] + back(sums[2], 0)
             row = 2 * i + pi
-            pre = phases[pi]
+            phases[row, pl.ds(0, WLOW, stride=2)] = ahead(sums[0], 0) + sums[1] + sums[2]
+            phases[row, pl.ds(1, WLOW, stride=2)] = sums[0] + sums[1] + back(sums[2], 0)
+            pre = phases[row]
             gate = jax.nn.sigmoid(pre)
             act_c[row] = (pre * gate + act_a[row].astype(F32)).astype(BF)
             slope_c[row] = gate * (1.0 + pre * (1.0 - gate))
 
-    each(LOW, level_three)
+    each(LOW, level_three, CHUNK["three"])
     out_w = stack_outputs(stack_o, w_out)
 
     def field_taps(r):
@@ -302,23 +324,23 @@
 
     each(ROWS, field_taps, 4)
 
-    def loss(r):
-        value = four_channels(taps, r)
-        sigma = jnp.where(held, jnp.broadcast_to(field[r, 1:2], (8, LANES)), 1.0)
-        weight = jnp.broadcast_to(field[r, 0:1], (8, LANES))
-        variance = sigma * sigma + 0.25
-        c_out = 0.5 * sigma * lax.rsqrt(variance)
-        lam = variance / (0.25 * sigma * sigma)
-        denoised = (0.25 / variance) * noisies[r] + c_out * value
-        den[r] = denoised[4:8, :OWN]
-        loss_grad = (2.0 * scale) * weight * lam * (denoised - residuals[r])
-        cot = (c_out * loss_grad).astype(BF).astype(F32)
-        grad_f[r + 1] = jnp.where(low_half, 0.0, cot)
-
-    each(ROWS, loss, 4)
-    lat = place[1]
-    for k in range(lats):
-        tiles[k][...] = den[pl.ds(2 * lax.rem(lat + k, lats), 2)]
+    def loss(i):
+        for k in range(2):
+            r = 2 * i + k
+            value = four_channels(taps, r)
+            sigma = jnp.where(held, jnp.broadcast_to(field[r, 1:2], (8, LANES)), 1.0)
+            weight = jnp.broadcast_to(field[r, 0:1], (8, LANES))
+            variance = sigma * sigma + 0.25
+            c_out = 0.5 * sigma * lax.rsqrt(variance)
+            lam = variance / (0.25 * sigma * sigma)
+            denoised = (0.25 / variance) * noisies[r] + c_out * value
+            den[i, 4 * k : 4 * k + 4] = denoised[4:8, :OWN]
+            loss_grad = (2.0 * scale) * weight * lam * (denoised - residuals[r])
+            cot = (c_out * loss_grad).astype(BF).astype(F32)
+            grad_f[r + 1] = jnp.where(low_half, 0.0, cot)
+
+    each(LOW, loss, 2)
+    tiles[...] = den[...].astype(BF)
     last_sum[...] = jnp.zeros_like(last_sum)
 
     def last_grads(r):
@@ -339,13 +361,15 @@
     keep(near, BIG_ROWS, last_sum[0:LAST_ROWS])
     keep(near, BIG_ROWS + LAST_ROWS, jnp.zeros((HALF_ROWS - BIG_ROWS - LAST_ROWS, OWN), F32))
 
+    n6, u6 = CHUNK["back_three"]
+
     def back_three(i):
-        wide = mm(spread_f[pl.ds(4 * i, 4)].reshape(4 * WIDE, OWN), out_w)
-        wide = wide.reshape(4, WIDE, HID1)
-        back_c[pl.ds(4 * i, 4)] = wide
-        grad_c[pl.ds(4 * i + 1, 4)] = wide * slope_c[pl.ds(4 * i, 4)]
-
-    each(ROWS // 4, back_three)
+        wide = mm(spread_f[pl.ds(n6 * i, n6)].reshape(n6 * WIDE, OWN), out_w)
+        wide = wide.reshape(n6, WIDE, HID1)
+        back_c[pl.ds(n6 * i, n6)] = wide
+        grad_c[pl.ds(n6 * i + 1, n6)] = wide * slope_c[pl.ds(n6 * i, n6)]
+
+    each(ROWS // n6, back_three, u6)
 
     def block_sums(i):
         even = [grad_c[2 * i + k, pl.ds(0, WLOW, stride=2)] for k in range(4)]
@@ -356,61 +380,63 @@
                 at = (a * 3 + b) * HID1
                 blocks[i, :, at : at + HID1] = total.astype(BF)
 
-    each(LOW, block_sums)
+    each(LOW, block_sums, CHUNK["blocks"])
+
+    n7, u7 = CHUNK["back_two"]
 
     def back_two(i):
-        low = mm(blocks[pl.ds(2 * i, 2)].reshape(2 * WLOW, 9 * HID1), w_up[...])
-        cot = low.reshape(2, WLOW, HID2) * slope_b[pl.ds(2 * i, 2)]
+        low = mm(blocks[pl.ds(n7 * i, n7)].reshape(n7 * WLOW, 9 * HID1), w_up[...])
+        cot = low.reshape(n7, WLOW, HID2) * slope_b[pl.ds(n7 * i, n7)]
         shifts = jnp.concatenate([back(cot, 1), cot, ahead(cot, 1)], axis=2)
-        grad_b[pl.ds(2 * i + 1, 2)] = shifts.astype(BF)
-
-    each(LOW // 2, back_two)
-    own_low = lax.broadcasted_iota(jnp.int32, (LOW, WLOW, HID2), 1) < OWN // 2
-    low_b = jnp.where(own_low, act_b[...].astype(F32), 0.0).astype(BF).reshape(LOW * WLOW, HID2)
+        grad_b[pl.ds(n7 * i + 1, n7)] = shifts.astype(BF)
+
+    each(LOW // n7, back_two, u7)
+    held_low = OWN // 2
+    cells = LOW * held_low
+    low_b = act_b[:, :held_low].reshape(cells, HID2)
     for k in range(3):
-        left_side = blocks[:, :, 3 * HID1 * k : 3 * HID1 * (k + 1)].reshape(LOW * WLOW, 3 * HID1)
-        up = mm_tn(left_side, low_b)
-        keep(near, 3 * HID1 * k, up[:, :HID1])
-        keep(near, 3 * HID1 * k + UP_ROWS, up[:, HID1:])
-    own_one = lax.broadcasted_iota(jnp.int32, (LOW, WLOW, HID1), 1) < OWN // 2
+        at = 3 * HID1 * k
+        up = mm_tn(blocks[:, :held_low, at : at + 3 * HID1].reshape(cells, 3 * HID1), low_b)
+        keep(near, at, up[:, :HID1])
+        keep(near, at + UP_ROWS, up[:, HID1:])
     low_a = jnp.concatenate(
-        [
-            jnp.where(own_one, pooled[a : a + LOW].astype(F32), 0.0).astype(BF).reshape(LOW * WLOW, HID1)
-            for a in range(3)
-        ],
-        axis=1,
+        [pooled[a : a + LOW, :held_low].reshape(cells, HID1) for a in range(3)], axis=1
     )
     for b in range(3):
-        left_side = grad_b[1 : LOW + 1, :, HID2 * b : HID2 * (b + 1)].reshape(LOW * WLOW, HID2)
-        down = mm_tn(left_side, low_a)
+        at = HID2 * b
+        down = mm_tn(grad_b[1 : LOW + 1, :held_low, at : at + HID2].reshape(cells, HID2), low_a)
         for a in range(3):
             keep(far, (a * 3 + b) * HID2, down[:, HID1 * a : HID1 * (a + 1)])
-    own_wide = lax.broadcasted_iota(jnp.int32, (WIDE, HID1), 0) < OWN
+    n8, u8 = CHUNK["back_one"]
 
     def back_one(i):
         total = None
         for a in range(3):
-            cot = grad_b[pl.ds(2 * i + 2 - a, 2)].reshape(2 * WLOW, 3 * HID2)
+            cot = grad_b[pl.ds(n8 * i + 2 - a, n8)].reshape(n8 * WLOW, 3 * HID2)
             part = mm(cot, w_down[a])
             total = part if total is None else total + part
-        low = (0.25 * total).reshape(2, WLOW, HID1)
-        for k in range(2):
-            phases[k, pl.ds(0, WLOW, stride=2)] = low[k]
-            phases[k, pl.ds(1, WLOW, stride=2)] = low[k]
+        low = (0.25 * total).reshape(n8, WLOW, HID1)
+        for k in range(n8):
+            row = n8 * i + k
+            phases[row, pl.ds(0, WLOW, stride=2)] = low[k]
+            phases[row, pl.ds(1, WLOW, stride=2)] = low[k]
+            spread = phases[row, 0:OWN]
             for pi in range(2):
-                row = 4 * i + 2 * k + pi
-                cot = (back_c[row] + phases[k]) * slope_a[row]
-                grad_a[row] = jnp.where(own_wide, cot, 0.0).astype(BF)
-
-    each(LOW // 2, back_one)
-    inputs = mm_tn(three_rows(net, 0, ROWS), grad_a[...].reshape(ROWS * WIDE, HID1))
+                r = 2 * row + pi
+                grad_a[r] = ((back_c[r, 0:OWN] + spread) * slope_a[r, 0:OWN]).astype(BF)
+
+    each(LOW // n8, back_one, u8)
+    near_cells = jnp.concatenate(
+        [net[a : a + ROWS, :OWN].reshape(ROWS * OWN, OWN) for a in range(3)], axis=1
+    )
+    inputs = mm_tn(grad_a[...].reshape(ROWS * OWN, HID1), near_cells)
     for a in range(3):
-        keep(far, BIG_ROWS + a * 3 * FIELDS, inputs[a * OWN : a * OWN + 3 * FIELDS])
+        part = inputs[:, a * OWN : (a + 1) * OWN].T
+        keep(far, BIG_ROWS + a * 3 * FIELDS, part[: 3 * FIELDS])
     keep(far, BIG_ROWS + IN_ROWS, jnp.zeros((HALF_ROWS - BIG_ROWS - IN_ROWS, OWN), F32))
 
 
-def unpack_kernel(place, mine, other, *rest):
-    tiles, (tile, first, down, up, last) = rest[:8], rest[8:]
+def unpack_kernel(place, mine, other, tiles, tile, first, down, up, last):
     a = pl.program_id(0)
     even = place[0] == 0
 
@@ -432,10 +458,10 @@
 
     @pl.when(a == 0)
     def _():
+        blocks = tiles[...].astype(F32)
         for k in range(8):
-            at = pl.multiple_of(lax.rem(place[1] + 8 - k, 8) * OWN, OWN)
             for r in range(2):
-                tile[:, r, pl.ds(at, OWN)] = tiles[k][r]
+                tile[:, r, k * OWN : (k + 1) * OWN] = blocks[k, 4 * r : 4 * r + 4]
 
 
 def in_vmem(count):
@@ -465,10 +491,10 @@
         kernel,
         out_shape=(
             jax.ShapeDtypeStruct((2, HALF_ROWS, OWN), BF),
-            *([jax.ShapeDtypeStruct((2, 4, OWN), F32)] * 8),
+            jax.ShapeDtypeStruct((LOW, CELL_ROWS, OWN), BF),
         ),
         in_specs=[in_smem(), *in_vmem(10)],
-        out_specs=tuple(in_vmem(9)),
+        out_specs=tuple(in_vmem(2)),
         scratch_shapes=[
             pltpu.VMEM((3, OWN, OWN), F32),
             pltpu.VMEM((OWN, OWN), F32),
@@ -481,12 +507,12 @@
             pltpu.VMEM((ROWS, 8, LANES), F32),
             pltpu.VMEM((ROWS, WIDE, HID1), F32),
             pltpu.VMEM((ROWS, WIDE, HID1), BF),
-            pltpu.VMEM((2, WIDE, HID1), F32),
+            pltpu.VMEM((LOW, WIDE, HID1), F32),
             pltpu.VMEM((LOW + 2, WLOW, HID1), BF),
             pltpu.VMEM((LOW, WLOW, HID2), BF),
             pltpu.VMEM((LOW, WLOW, HID2), F32),
             pltpu.VMEM((LOW + 2, WLOW, 9 * HID1), F32),
-            pltpu.VMEM((2, WIDE, HID1), F32),
+            pltpu.VMEM((ROWS, WIDE, HID1), F32),
             pltpu.VMEM((ROWS, WIDE, HID1), F32),
             pltpu.VMEM((ROWS + 2, 8, LANES), F32),
             pltpu.VMEM((ROWS, WIDE, OWN), BF),
@@ -494,9 +520,9 @@
             pltpu.VMEM((ROWS + 2, WIDE, HID1), F32),
             pltpu.VMEM((LOW, WLOW, 9 * HID1), BF),
             pltpu.VMEM((LOW + 2, WLOW, 3 * HID2), BF),
-            pltpu.VMEM((ROWS, WIDE, HID1), BF),
+            pltpu.VMEM((ROWS, OWN, HID1), BF),
             pltpu.VMEM((80, HID1), F32),
-            pltpu.VMEM((ROWS, 4, OWN), F32),
+            pltpu.VMEM((LOW, CELL_ROWS, OWN), F32),
         ],
         name="step",
     )(*operands)
@@ -504,7 +530,7 @@
 
 def unpack(place, mine, other, tiles):
     whole = pl.BlockSpec((HALF_ROWS, OWN), lambda a: (0, 0))
-    part = pl.BlockSpec((2, 4, OWN), lambda a: (0, 0, 0))
+    cells = pl.BlockSpec((8, CELL_ROWS, OWN), lambda a: (0, 0, 0))
 
     def taps(rows, lanes):
         return pl.BlockSpec((1, 3, rows, lanes), lambda a: (a, 0, 0, 0))
@@ -519,7 +545,7 @@
             jax.ShapeDtypeStruct((3, 3, HID1, HID2), F32),
             jax.ShapeDtypeStruct((3, 3, 4, HID1), F32),
         ),
-        in_specs=[in_smem(), whole, whole, *([part] * 8)],
+        in_specs=[in_smem(), whole, whole, cells],
         out_specs=(
             pl.BlockSpec((4, 2, 8 * OWN), lambda a: (0, 0, 0)),
             taps(20, HID1),
@@ -528,7 +554,7 @@
             taps(4, HID1),
         ),
         name="unpack",
-    )(place, mine, other, *tiles)
+    )(place, mine, other, tiles)
 
 
 def all_to_all(value, axes):
@@ -555,10 +581,10 @@
     diffuse_out,
 ):
     scale = 1.0 / (target.shape[0] * math.sqrt(target.shape[1] * target.shape[2] * lax.axis_size(STRIPS)))
-    place = jnp.stack([lax.axis_index("core"), lax.axis_index(LAT)]).astype(jnp.int32)
+    place = lax.axis_index("core").astype(jnp.int32)[None]
     packed = all_to_all(pack(target, noise, land_mask, level_index), LAT).reshape(ROWS, 16, OWN)
     fields = jnp.concatenate([packed[:, :8], coarse.transpose(1, 0, 2).astype(F32), packed[:, 12:]], axis=1)
-    grads, *tiles = step(
+    grads, tiles = step(
         scale,
         place,
         fields,
@@ -573,14 +599,17 @@
         diffuse_out,
     )
     chips = lax.axis_size(CHIPS)
+    rows = HALF_ROWS // chips
+    lats = tiles.shape[0]
     half = grads[0].astype(F32) + shift_by(grads[1], "core", 1).astype(F32)
-    with jax.named_scope("scatter"):
-        parts = all_to_all(half.astype(BF).reshape(chips, HALF_ROWS // chips, OWN), CHIPS)
-    with jax.named_scope("tiles"):
-        tiles = [tiles[0], *(shift_by(tiles[k], LAT, k) for k in range(1, 8))]
-    total = parts.astype(F32).sum(0).astype(BF)
+    blocks = jnp.broadcast_to(tiles[None], (chips // lats, *tiles.shape)).reshape(chips, CELL_ROWS, OWN)
+    sent = jnp.concatenate([half.astype(BF).reshape(chips, rows, OWN), blocks], axis=1)
+    parts = all_to_all(sent, CHIPS)
+    total = parts[:, :rows].astype(F32).sum(0).astype(BF)
+    seats = parts.reshape(chips // lats, lats, rows + CELL_ROWS, OWN)[:, :, rows:]
+    tiles = lax.dynamic_index_in_dim(seats, lax.axis_index(("y", "x_hi")), 0, False)
     with jax.named_scope("spread"):
-        mine = all_to_all(jnp.broadcast_to(total[None], parts.shape), CHIPS).reshape(HALF_ROWS, OWN)
+        mine = all_to_all(jnp.broadcast_to(total[None], (chips, rows, OWN)), CHIPS).reshape(HALF_ROWS, OWN)
     tile, first, down, up, last = unpack(place, mine, shift_by(mine, "core", 1), tiles)
     return (tile, first.transpose(0, 1, 3, 2), down, up, last)
 

time: 112 us -> 102 us (0.911); the launches traced: 110 us -> 102 us
  starting transfers between devices: 26.9 us -> 18.6 us
  blocking collectives: 34.8 us -> 36.1 us
    ppermute x11 -> x4, starting transfers between devices: 20.1 us -> 11.8 us  [shift_by(): lax.ppermute(value, axes, [(i, (i + step) % count) for i in range(count)])]
    all_to_all x2, blocking collectives: 34.8 us -> 36.1 us  [all_to_all(): return lax.all_to_all(value, axes, split_axis=0, concat_axis=0, tiled=True)]
    ppermute x11 -> x4, waiting for transfers between devices: 10.2 us -> 10 us  [shift_by(): lax.ppermute(value, axes, [(i, (i + step) % count) for i in range(count)])]
  transfers between devices with their start and end apart: 12 -> 5, of which waited for: 7 -> 5; matrix products, arithmetic and copies ran while one was open for 1% -> 1% of each run, Pallas kernels for 0% -> 0%
where the time goes in v1:
time: 102 us
  blocking collectives  36.1 us (35%)
  Pallas kernels  26.6 us (26%)
  starting transfers between devices  18.6 us (18%)
  waiting for transfers between devices  14.6 us (14%)
  local copies, waits for them, and re-layouts  4.36 us (4%)
  between operations  1.37 us (1%)
    all_to_all x2, blocking collectives, all_to_all(): return lax.all_to_all(value, axes, split_axis=0, concat_axis=0, tiled=True)  36.1 us
    pallas_call x1, Pallas kernels, step(): pl.pallas_call(kernel, out_shape=(jax.ShapeDtypeStruct((2, HALF_ROWS, OWN...  21.8 us
    ppermute x4, starting transfers between devices, shift_by(): lax.ppermute(value, axes, [(i, (i + step) % count) for i in range(count)])  11.8 us
    ppermute x4, waiting for transfers between devices, shift_by(): lax.ppermute(value, axes, [(i, (i + step) % count) for i in range(count)])  10 us
    all_to_all x1, starting transfers between devices, all_to_all(): return lax.all_to_all(value, axes, split_axis=0, concat_axis=0, tiled=True)  6.78 us
    all_to_all x1, waiting for transfers between devices, all_to_all(): return lax.all_to_all(value, axes, split_axis=0, concat_axis=0, tiled=True)  4.63 us
    pallas_call x1, Pallas kernels, unpack(): pl.pallas_call(unpack_kernel, grid=(3,), out_shape=(jax.ShapeDtypeStruct(...  3.26 us
  transfers between devices with their start and end apart: 5, of which 5 were waited for; matrix products, arithmetic and copies ran while one was open for 1% of the time, Pallas kernels for 0%

profile of v1, /device:TPU:1, one launch (start us, length us, event | category | flops | bytes accessed | tf_op | source)
XLA Modules:
  0.0 102.0 jit_solution(4904139655585284076)
XLA Ops:
  1.3 1.5 %pack.1 = f32[8,2,16,128]{3,2,1,0:T(8,128)} custom-call(f32[4,2,1024]{2,1,0:T(2,128)} %target.1, f32[4,2,1024]{2,1,0:T(2,128)} %noise.1, s32[2,1024]{1,0:T(2,128)} %land_mask.1, s32[1,1]{1,0:T(1,128)S(6)} %copy.21.level), custom_call_target="tpu_custom_call" | custom-call | tf_op jit(solution)/shard_map/pack/pallas_call | solution.py:477
  2.8 6.8 %all-to-all-start = ((f32[8,2,16,128]{3,2,1,0:T(8,128)}), f32[8,2,16,128]{3,2,1,0:T(8,128)S(1)}, u32[]{:S(2)}, u32[]{:S(2)}) async-start(f32[8,2,16,128]{3,2,1,0:T(8,128)} %pack.1), calls=%async_computation | async-start | bytes 262144 | tf_op jit(solution)/shard_map/all_to_all | solution.py:561
  9.6 0.8 copy.20
  10.4 4.6 %all-to-all-done = f32[8,2,16,128]{3,2,1,0:T(8,128)S(1)} async-done(((f32[8,2,16,128]{3,2,1,0:T(8,128)}), f32[8,2,16,128]{3,2,1,0:T(8,128)S(1)}, u32[]{:S(2)}, u32[]{:S(2)}) %all-to-all-start) | async-done | bytes 131104 | tf_op jit(solution)/shard_map/all_to_all | solution.py:561
  15.1 0.0 copy-start.2
  15.1 3.2 %collective-permute-start.1 = (f32[16,24,128]{2,1,0:T(8,128)S(1)}, f32[16,24,128]{2,1,0:T(8,128)S(1)}, u32[]{:S(2)}, u32[]{:S(2)}) collective-permute-start(f32[16,24,128]{2,1,0:T(8,128)S(1)} %pad_maximum_fusion.1.refs_1_), channel_id=1, source_target_pairs={{0,127},{1,0},{2,1},{3,2},{4,3},{5,4},{6,5},{7,6},{8,7},{9,8},{10,... | collective-permute-start | bytes 589832 | tf_op jit(solution)/shard_map/ppermute | solution.py:566
  18.3 0.0 collective-permute-start
  18.3 3.7 %collective-permute-done.1.refs_3_ = f32[16,24,128]{2,1,0:T(8,128)S(1)} collective-permute-done((f32[16,24,128]{2,1,0:T(8,128)S(1)}, f32[16,24,128]{2,1,0:T(8,128)S(1)}, u32[]{:S(2)}, u32[]{:S(2)}) %collective-permute-start.1) | collective-permute-done | bytes 196640 | tf_op jit(solution)/shard_map/ppermute | solution.py:566
  22.0 0.0 copy-start.4
  22.0 3.5 %collective-permute-done.refs_2_ = f32[16,24,128]{2,1,0:T(8,128)S(1)} collective-permute-done((f32[16,24,128]{2,1,0:T(8,128)S(1)}, f32[16,24,128]{2,1,0:T(8,128)S(1)}, u32[]{:S(2)}, u32[]{:S(2)}) %collective-permute-start) | collective-permute-done | bytes 196640 | tf_op jit(solution)/shard_map/ppermute | solution.py:566
  25.5 0.0 copy-done.2
  25.5 0.0 copy-done.4
  25.5 0.7 copy-done.5
  26.2 21.8 %step.1 = (bf16[2,2560,128]{2,1,0:T(8,128)(2,1)}, bf16[8,8,128]{2,1,0:T(8,128)(2,1)}) custom-call(s32[1]{0:T(128)} %bitcast.refs_0_.place, f32[16,24,128]{2,1,0:T(8,128)} %copy-done.2, f32[16,24,128]{2,1,0:T(8,128)} %copy-done.5, f32[16,24,128]{2,1,0:T(8,128)} %copy-done.4, bf16[3,3,12,128]{3,2,1,0:T(8,128)(2,1)} %bitcast.34, bf16[3,384,128]{2,1,0:T(8,128)(2,1)} %bitcast.32, ...), custom_call_target="tpu_custom_call" | custom-call | tf_op jit(solution)/shard_map/step/pallas_call | solution.py:490
  48.0 1.2 %slice_bitcast_fusion = bf16[2560,128]{1,0:T(8,128)(2,1)S(1)} fusion(bf16[2,2560,128]{2,1,0:T(8,128)(2,1)} %get-tuple-element.12), kind=kLoop, calls=%fused_computation.4 | loop fusion | bytes 1310720 | tf_op jit(solution)/shard_map/squeeze | solution.py:604
  49.3 0.0 copy-start.6
  49.3 5.6 %collective-permute-start.2 = (bf16[2560,128]{1,0:T(8,128)(2,1)S(1)}, bf16[2560,128]{1,0:T(8,128)(2,1)S(1)}, u32[]{:S(2)}, u32[]{:S(2)}) collective-permute-start(bf16[2560,128]{1,0:T(8,128)(2,1)S(1)} %slice_bitcast_fusion), channel_id=1, source_target_pairs={{0,8},{8,0},{1,9},{9,1},{2,10},{10,2},{3,11},{11,3},{4,12},{12,4},... | collective-permute-start | bytes 1966088 | tf_op jit(solution)/shard_map/ppermute | solution.py:566
  54.9 1.7 %collective-permute-done.2 = bf16[2560,128]{1,0:T(8,128)(2,1)S(1)} collective-permute-done((bf16[2560,128]{1,0:T(8,128)(2,1)S(1)}, bf16[2560,128]{1,0:T(8,128)(2,1)S(1)}, u32[]{:S(2)}, u32[]{:S(2)}) %collective-permute-start.2) | collective-permute-done | bytes 655392 | tf_op jit(solution)/shard_map/ppermute | solution.py:566
  56.6 0.0 copy-done.1
  56.6 0.2 fusion
  56.8 0.0 copy-done.6
  56.8 0.1 pad_maximum_fusion
  56.9 19.0 %all_to_all.15 = bf16[64,48,128]{2,1,0:T(8,128)(2,1)S(1)} all-to-all(bf16[64,48,128]{2,1,0:T(8,128)(2,1)S(1)} %pad_maximum_fusion), channel_id=1, replica_groups=mesh['y'=4,'x_hi'=2,'core'=2,'x_lo'=2,'z'=4] {'y','x_hi','x_lo','z'}, dimensions={0} | all-to-all | bytes 1572864 | tf_op jit(solution)/shard_map/all_to_all | solution.py:561
  75.9 0.1 slice_reduce_fusion
  76.0 0.1 broadcast_in_dim.8
  76.1 17.1 %all_to_all.16 = bf16[64,40,128]{2,1,0:T(8,128)(2,1)S(1)} all-to-all(bf16[64,40,128]{2,1,0:T(8,128)(2,1)S(1)} %broadcast_in_dim.8), channel_id=1, replica_groups=mesh['y'=4,'x_hi'=2,'core'=2,'x_lo'=2,'z'=4] {'y','x_hi','x_lo','z'}, dimensions={0} | all-to-all | bytes 1310720 | tf_op jit(solution)/shard_map/spread/all_to_all | solution.py:561
  93.2 3.0 %collective-permute-start.3 = (bf16[2560,128]{1,0:T(8,128)(2,1)S(1)}, bf16[2560,128]{1,0:T(8,128)(2,1)S(1)}, u32[]{:S(2)}, u32[]{:S(2)}) collective-permute-start(bf16[2560,128]{1,0:T(8,128)(2,1)S(1)} %bitcast.23), channel_id=1, source_target_pairs={{0,8},{8,0},{1,9},{9,1},{2,10},{10,2},{3,11},{11,3},{4,12},{12,4},... | collective-permute-start | bytes 1966088 | tf_op jit(solution)/shard_map/ppermute | solution.py:566
  96.2 0.6 dynamic-slice_bitcast_fusion.tiles
  96.8 1.1 %collective-permute-done.3.other = bf16[2560,128]{1,0:T(8,128)(2,1)S(1)} collective-permute-done((bf16[2560,128]{1,0:T(8,128)(2,1)S(1)}, bf16[2560,128]{1,0:T(8,128)(2,1)S(1)}, u32[]{:S(2)}, u32[]{:S(2)}) %collective-permute-start.3) | collective-permute-done | bytes 655392 | tf_op jit(solution)/shard_map/ppermute | solution.py:566
  97.9 0.0 copy-done
  97.9 0.9 copy-done.3
  98.7 3.3 %unpack.1 = (f32[4,2,1024]{2,1,0:T(2,128)}, f32[3,3,20,128]{3,2,1,0:T(8,128)}, f32[3,3,256,128]{3,2,1,0:T(8,128)}, f32[3,3,128,256]{3,2,1,0:T(8,128)}, f32[3,3,4,128]{3,2,1,0:T(4,128)}) custom-call(s32[1]{0:T(128)} %bitcast.refs_0_.place, bf16[2560,128]{1,0:T(8,128)(2,1)} %bitcast.24, bf16[2560,128]{1,0:T(8,128)(2,1)} %copy-done.3, ...), custom_call_target="tpu_custom_call" | custom-call | tf_op jit(solution)/shard_map/unpack/pallas_call | solution.py:538
  (9 shorter events, 0.1 us)
Async XLA Ops:
  2.8 12.2 %all-to-all-start = ((f32[8,2,16,128]{3,2,1,0:T(8,128)}), f32[8,2,16,128]{3,2,1,0:T(8,128)S(1)}, u32[]{:S(2)}, u32[]{:S(2)}) async-start(f32[8,2,16,128]{3,2,1,0:T(8,128)} %pack.1), calls=%async_computation | async-start | bytes 262144 | tf_op jit(solution)/shard_map/all_to_all | solution.py:561
  15.1 10.4 %copy-start.2 = (f32[16,24,128]{2,1,0:T(8,128)}, f32[16,24,128]{2,1,0:T(8,128)S(1)}, u32[]{:S(2)}) copy-start(f32[16,24,128]{2,1,0:T(8,128)S(1)} %pad_maximum_fusion.1.refs_1_) | copy-start | bytes 589828
  15.1 6.9 %collective-permute-start.1 = (f32[16,24,128]{2,1,0:T(8,128)S(1)}, f32[16,24,128]{2,1,0:T(8,128)S(1)}, u32[]{:S(2)}, u32[]{:S(2)}) collective-permute-start(f32[16,24,128]{2,1,0:T(8,128)S(1)} %pad_maximum_fusion.1.refs_1_), channel_id=1, source_target_pairs={{0,127},{1,0},{2,1},{3,2},{4,3},{5,4},{6,5},{7,6},{8,7},{9,8},{10,... | collective-permute-start | bytes 589832 | tf_op jit(solution)/shard_map/ppermute | solution.py:566
  18.3 7.2 %collective-permute-start = (f32[16,24,128]{2,1,0:T(8,128)S(1)}, f32[16,24,128]{2,1,0:T(8,128)S(1)}, u32[]{:S(2)}, u32[]{:S(2)}) collective-permute-start(f32[16,24,128]{2,1,0:T(8,128)S(1)} %pad_maximum_fusion.1.refs_1_), channel_id=1, source_target_pairs={{0,1},{1,2},{2,3},{3,4},{4,5},{5,6},{6,7},{7,8},{8,9},{9,10},{10,1... | collective-permute-start | bytes 589832 | tf_op jit(solution)/shard_map/ppermute | solution.py:566
  22.0 3.5 %copy-start.4 = (f32[16,24,128]{2,1,0:T(8,128)}, f32[16,24,128]{2,1,0:T(8,128)S(1)}, u32[]{:S(2)}) copy-start(f32[16,24,128]{2,1,0:T(8,128)S(1)} %collective-permute-done.1.refs_3_) | copy-start | bytes 589828
  25.5 0.7 copy-start.5
  48.0 8.6 %copy-start.1 = (bf16[2,2560,128]{2,1,0:T(8,128)(2,1)S(1)}, bf16[2,2560,128]{2,1,0:T(8,128)(2,1)}, u32[]{:S(2)}) copy-start(bf16[2,2560,128]{2,1,0:T(8,128)(2,1)} %get-tuple-element.12) | copy-start | bytes 3932164
  49.3 7.5 %copy-start.6 = (bf16[8,8,128]{2,1,0:T(8,128)(2,1)S(1)}, bf16[8,8,128]{2,1,0:T(8,128)(2,1)}, u32[]{:S(2)}) copy-start(bf16[8,8,128]{2,1,0:T(8,128)(2,1)} %get-tuple-element.13) | copy-start | bytes 49156
  49.3 7.3 %collective-permute-start.2 = (bf16[2560,128]{1,0:T(8,128)(2,1)S(1)}, bf16[2560,128]{1,0:T(8,128)(2,1)S(1)}, u32[]{:S(2)}, u32[]{:S(2)}) collective-permute-start(bf16[2560,128]{1,0:T(8,128)(2,1)S(1)} %slice_bitcast_fusion), channel_id=1, source_target_pairs={{0,8},{8,0},{1,9},{9,1},{2,10},{10,2},{3,11},{11,3},{4,12},{12,4},... | collective-permute-start | bytes 1966088 | tf_op jit(solution)/shard_map/ppermute | solution.py:566
  93.2 4.7 %copy-start = (bf16[64,40,128]{2,1,0:T(8,128)(2,1)}, bf16[64,40,128]{2,1,0:T(8,128)(2,1)S(1)}, u32[]{:S(2)}) copy-start(bf16[64,40,128]{2,1,0:T(8,128)(2,1)S(1)} %all_to_all.16) | copy-start | bytes 1966084
  93.2 4.7 %collective-permute-start.3 = (bf16[2560,128]{1,0:T(8,128)(2,1)S(1)}, bf16[2560,128]{1,0:T(8,128)(2,1)S(1)}, u32[]{:S(2)}, u32[]{:S(2)}) collective-permute-start(bf16[2560,128]{1,0:T(8,128)(2,1)S(1)} %bitcast.23), channel_id=1, source_target_pairs={{0,8},{8,0},{1,9},{9,1},{2,10},{10,2},{3,11},{11,3},{4,12},{12,4},... | collective-permute-start | bytes 1966088 | tf_op jit(solution)/shard_map/ppermute | solution.py:566
  97.9 0.9 copy-start.3

commit v2 on v1

--- a/solution.py
+++ b/solution.py
@@ -35,17 +35,18 @@
 HALF_ROWS = 2560
 CELL_ROWS = 8
 CHUNK = {
-    "first": (4, 1),
-    "second": (4, 1),
-    "one": (4, 1),
-    "two": (2, 1),
-    "up": (2, 1),
-    "back_three": (4, 1),
-    "back_two": (2, 1),
-    "back_one": (2, 1),
-    "three": 1,
-    "blocks": 1,
+    "first": (8, 1),
+    "second": (4, 2),
+    "one": (8, 1),
+    "two": (4, 2),
+    "up": (8, 1),
+    "back_three": (8, 1),
+    "back_two": (2, 2),
+    "back_one": (4, 1),
+    "three": 2,
+    "blocks": 4,
 }
+EDGE_ROWS = OWN // HALO
 
 
 def mm(x, w):
@@ -146,6 +147,25 @@
             packed[p, r, 12:16] = noise[:, r, lanes]
 
 
+def edges_kernel(packed, coarse, fields, first_columns, last_columns):
+    lane = lax.broadcasted_iota(jnp.int32, (FIELDS, OWN), 1)
+    for g in range(ROWS // EDGE_ROWS):
+        firsts = lasts = jnp.zeros((FIELDS, OWN), F32)
+        for j in range(EDGE_ROWS):
+            r = g * EDGE_ROWS + j
+            fields[r, 0:8] = packed[r, 0:8]
+            fields[r, 8:20] = coarse[r]
+            fields[r, 20:24] = packed[r, 12:16]
+            row = fields[r]
+            here = (lane >= j * HALO) & (lane < (j + 1) * HALO)
+            at = j * HALO
+            firsts = jnp.where(here, pltpu.roll(row, at, 1) if at else row, firsts)
+            at = (j + 1) * HALO % OWN
+            lasts = jnp.where(here, pltpu.roll(row, at, 1) if at else row, lasts)
+        first_columns[g] = firsts
+        last_columns[g] = lasts
+
+
 def stack_inputs(ref, weight, room):
     ref[...] = jnp.zeros_like(ref)
     count = weight.shape[2]
@@ -177,7 +197,8 @@
     w_down,
     w_up,
     w_out,
-    grads,
+    mine,
+    other,
     tiles,
     *scratch,
 ):
@@ -209,17 +230,25 @@
         grad_a,
         last_sum,
         den,
+        halves,
+        sems,
     ) = scratch
     for ref in (net, hid, pooled, up_taps, taps, grad_f, grad_c, grad_b):
         zero_edges(ref)
     first_w = stack_inputs(stack, w_first, 16)
 
-    def gather(r):
-        wide = with_halo(own[r], left[r], right[r])
-        field[r] = wide
-        net[r + 1] = to_cells(lon_shifts(wide[8:24]))
-
-    each(ROWS, gather, 4)
+    def gather(g):
+        from_left, from_right = left[g], right[g]
+        for j in range(EDGE_ROWS):
+            r = g * EDGE_ROWS + j
+            at = OWN - HALO - j * HALO
+            before = pltpu.roll(from_left, at, 1) if at else from_left
+            after = pltpu.roll(from_right, OWN - j * HALO, 1) if j else from_right
+            wide = with_halo(own[r], before, after)
+            field[r] = wide
+            net[r + 1] = to_cells(lon_shifts(wide[8:24]))
+
+    each(ROWS // EDGE_ROWS, gather)
 
     n1, u1 = CHUNK["first"]
 
@@ -353,10 +382,17 @@
         spread_f[r] = to_cells(cots)
 
     each(ROWS, last_grads, 4)
-    near, far = place[0], 1 - place[0]
+    near, far = 0, 1
 
     def keep(half, at, value):
-        grads[pl.ds(half, 1), at : at + value.shape[0]] = value.astype(BF)[None]
+        halves[half, at : at + value.shape[0]] = value.astype(BF)
+
+    def send(half):
+        for core, target in ((half, mine), (1 - half, other)):
+
+            @pl.when(place[0] == core)
+            def _():
+                pltpu.make_async_copy(halves.at[half], target, sems.at[half]).start()
 
     keep(near, BIG_ROWS, last_sum[0:LAST_ROWS])
     keep(near, BIG_ROWS + LAST_ROWS, jnp.zeros((HALF_ROWS - BIG_ROWS - LAST_ROWS, OWN), F32))
@@ -399,6 +435,7 @@
         up = mm_tn(blocks[:, :held_low, at : at + 3 * HID1].reshape(cells, 3 * HID1), low_b)
         keep(near, at, up[:, :HID1])
         keep(near, at + UP_ROWS, up[:, HID1:])
+    send(near)
     low_a = jnp.concatenate(
         [pooled[a : a + LOW, :held_low].reshape(cells, HID1) for a in range(3)], axis=1
     )
@@ -434,6 +471,9 @@
         part = inputs[:, a * OWN : (a + 1) * OWN].T
         keep(far, BIG_ROWS + a * 3 * FIELDS, part[: 3 * FIELDS])
     keep(far, BIG_ROWS + IN_ROWS, jnp.zeros((HALF_ROWS - BIG_ROWS - IN_ROWS, OWN), F32))
+    send(far)
+    for half in (near, far):
+        pltpu.make_async_copy(halves.at[half], mine, sems.at[half]).wait()
 
 
 def unpack_kernel(place, mine, other, tiles, tile, first, down, up, last):
@@ -483,6 +523,17 @@
     )(target, noise, land_mask, level_index)
 
 
+def edges(packed, coarse):
+    columns = jax.ShapeDtypeStruct((ROWS // EDGE_ROWS, FIELDS, OWN), F32)
+    return pl.pallas_call(
+        edges_kernel,
+        out_shape=(jax.ShapeDtypeStruct((ROWS, FIELDS, OWN), F32), columns, columns),
+        in_specs=in_vmem(2),
+        out_specs=tuple(in_vmem(3)),
+        name="edges",
+    )(packed, coarse)
+
+
 def step(scale, *operands):
     def kernel(*refs):
         step_kernel(scale, *refs)
@@ -490,11 +541,12 @@
     return pl.pallas_call(
         kernel,
         out_shape=(
-            jax.ShapeDtypeStruct((2, HALF_ROWS, OWN), BF),
+            jax.ShapeDtypeStruct((HALF_ROWS, OWN), BF),
+            jax.ShapeDtypeStruct((HALF_ROWS, OWN), BF),
             jax.ShapeDtypeStruct((LOW, CELL_ROWS, OWN), BF),
         ),
         in_specs=[in_smem(), *in_vmem(10)],
-        out_specs=tuple(in_vmem(2)),
+        out_specs=(*[pl.BlockSpec(memory_space=pl.ANY)] * 2, *in_vmem(1)),
         scratch_shapes=[
             pltpu.VMEM((3, OWN, OWN), F32),
             pltpu.VMEM((OWN, OWN), F32),
@@ -523,6 +575,8 @@
             pltpu.VMEM((ROWS, OWN, HID1), BF),
             pltpu.VMEM((80, HID1), F32),
             pltpu.VMEM((LOW, CELL_ROWS, OWN), F32),
+            pltpu.VMEM((2, HALF_ROWS, OWN), BF),
+            pltpu.SemaphoreType.DMA((2,)),
         ],
         name="step",
     )(*operands)
@@ -583,13 +637,13 @@
     scale = 1.0 / (target.shape[0] * math.sqrt(target.shape[1] * target.shape[2] * lax.axis_size(STRIPS)))
     place = lax.axis_index("core").astype(jnp.int32)[None]
     packed = all_to_all(pack(target, noise, land_mask, level_index), LAT).reshape(ROWS, 16, OWN)
-    fields = jnp.concatenate([packed[:, :8], coarse.transpose(1, 0, 2).astype(F32), packed[:, 12:]], axis=1)
-    grads, tiles = step(
+    fields, first_columns, last_columns = edges(packed, coarse.transpose(1, 0, 2).astype(F32))
+    grads, partner, tiles = step(
         scale,
         place,
         fields,
-        shift_by(fields, STRIPS, 1),
-        shift_by(fields, STRIPS, -1),
+        shift_by(last_columns, STRIPS, 1),
+        shift_by(first_columns, STRIPS, -1),
         frozen_first.transpose(0, 1, 3, 2),
         frozen_middle.reshape(3, 3 * HID1, HID1),
         frozen_last,
@@ -601,7 +655,7 @@
     chips = lax.axis_size(CHIPS)
     rows = HALF_ROWS // chips
     lats = tiles.shape[0]
-    half = grads[0].astype(F32) + shift_by(grads[1], "core", 1).astype(F32)
+    half = grads.astype(F32) + shift_by(partner, "core", 1).astype(F32)
     blocks = jnp.broadcast_to(tiles[None], (chips // lats, *tiles.shape)).reshape(chips, CELL_ROWS, OWN)
     sent = jnp.concatenate([half.astype(BF).reshape(chips, rows, OWN), blocks], axis=1)
     parts = all_to_all(sent, CHIPS)

time: 102 us -> 102 us (level)
  waiting for transfers between devices: 14.6 us -> 8.72 us
  blocking collectives: 36.1 us -> 41.5 us
  Pallas kernels: 26.6 us -> 25.2 us
  other arithmetic: 0.39 us -> 1.46 us
    all_to_all x2, blocking collectives: 36.1 us -> 41.5 us  [all_to_all(): return lax.all_to_all(value, axes, split_axis=0, concat_axis=0, tiled=True)]
    ppermute x4, waiting for transfers between devices: 10 us -> 4.74 us  [shift_by(): lax.ppermute(value, axes, [(i, (i + step) % count) for i in range(count)])]
    pallas_call x1 -> x2, Pallas kernels: 21.8 us -> 20.4 us  [the longest x1 18.7 us: step(): pl.pallas_call(kernel, out_shape=(jax.ShapeDtypeStruct((HALF_ROWS, OWN),...]
    squeeze x1 -> x0, local copies, waits for them, and re-layouts: 1.23 us -> none  [local(): half = grads[0].astype(F32) + shift_by(grads[1], 'core', 1).astype(F32)]
    convert_element_type x1, other arithmetic: 0.17 us -> 1.26 us  [local(): half.astype(BF).reshape(chips, rows, OWN)]
    unnamed x14 -> x12, local copies, waits for them, and re-layouts: 1.56 us -> 2.14 us
  transfers between devices with their start and end apart: 5 -> 5, of which waited for: 5 -> 4; matrix products, arithmetic and copies ran while one was open for 1% -> 2% of each run, Pallas kernels for 0% -> 0%
where the time goes in v2:
time: 102 us
  blocking collectives  41.5 us (41%)
  Pallas kernels  25.2 us (25%)
  starting transfers between devices  19.1 us (19%)
  waiting for transfers between devices  8.72 us (9%)
  local copies, waits for them, and re-layouts  4.34 us (4%)
  other arithmetic  1.46 us (1%)
  between operations  1.34 us (1%)
    all_to_all x2, blocking collectives, all_to_all(): return lax.all_to_all(value, axes, split_axis=0, concat_axis=0, tiled=True)  41.5 us
    pallas_call x1, Pallas kernels, step(): pl.pallas_call(kernel, out_shape=(jax.ShapeDtypeStruct((HALF_ROWS, OWN),...  18.7 us
    ppermute x4, starting transfers between devices, shift_by(): lax.ppermute(value, axes, [(i, (i + step) % count) for i in range(count)])  12.3 us
    all_to_all x1, starting transfers between devices, all_to_all(): return lax.all_to_all(value, axes, split_axis=0, concat_axis=0, tiled=True)  6.78 us
    ppermute x4, waiting for transfers between devices, shift_by(): lax.ppermute(value, axes, [(i, (i + step) % count) for i in range(count)])  4.74 us
    all_to_all x1, waiting for transfers between devices, all_to_all(): return lax.all_to_all(value, axes, split_axis=0, concat_axis=0, tiled=True)  3.98 us
    pallas_call x1, Pallas kernels, unpack(): pl.pallas_call(unpack_kernel, grid=(3,), out_shape=(jax.ShapeDtypeStruct(...  3.26 us
    unnamed x12, local copies, waits for them, and re-layouts  2.14 us
  transfers between devices with their start and end apart: 5, of which 4 were waited for; matrix products, arithmetic and copies ran while one was open for 2% of the time, Pallas kernels for 0%

profile of v2, /device:TPU:1, one launch (start us, length us, event | category | flops | bytes accessed | tf_op | source)
XLA Modules:
  0.0 101.7 jit_solution(13063065110740815875)
XLA Ops:
  1.3 1.5 %pack.1 = f32[8,2,16,128]{3,2,1,0:T(8,128)} custom-call(f32[4,2,1024]{2,1,0:T(2,128)} %target.1, f32[4,2,1024]{2,1,0:T(2,128)} %noise.1, s32[2,1024]{1,0:T(2,128)} %land_mask.1, s32[1,1]{1,0:T(1,128)S(6)} %copy.21.level), custom_call_target="tpu_custom_call" | custom-call | tf_op jit(solution)/shard_map/pack/pallas_call | solution.py:517
  2.8 6.8 %all-to-all-start = ((f32[8,2,16,128]{3,2,1,0:T(8,128)}), f32[8,2,16,128]{3,2,1,0:T(8,128)S(1)}, u32[]{:S(2)}, u32[]{:S(2)}) async-start(f32[8,2,16,128]{3,2,1,0:T(8,128)} %pack.1), calls=%async_computation | async-start | bytes 262144 | tf_op jit(solution)/shard_map/all_to_all | solution.py:615
  9.6 1.5 %copy.20 = f32[12,16,128]{2,0,1:T(8,128)} copy(bf16[12,16,128]{2,1,0:T(8,128)(2,1)} %param.12) | data formatting | bytes 147456 | tf_op jit(solution)/shard_map/convert_element_type | solution.py:640
  11.0 4.0 %all-to-all-done = f32[8,2,16,128]{3,2,1,0:T(8,128)S(1)} async-done(((f32[8,2,16,128]{3,2,1,0:T(8,128)}), f32[8,2,16,128]{3,2,1,0:T(8,128)S(1)}, u32[]{:S(2)}, u32[]{:S(2)}) %all-to-all-start) | async-done | bytes 131104 | tf_op jit(solution)/shard_map/all_to_all | solution.py:615
  15.0 0.0 copy-start.2
  15.0 0.7 copy-done.2
  15.7 1.7 %edges.1 = (f32[16,24,128]{2,1,0:T(8,128)}, f32[2,24,128]{2,1,0:T(8,128)}, f32[2,24,128]{2,1,0:T(8,128)}) custom-call(f32[16,16,128]{2,1,0:T(8,128)} %bitcast.24, f32[16,12,128]{2,1,0:T(8,128)} %bitcast.25), custom_call_target="tpu_custom_call" | custom-call | tf_op jit(solution)/shard_map/edges/pallas_call | solution.py:528
  17.4 0.2 collective-permute-start
  17.6 3.6 %collective-permute-start.1 = (f32[2,24,128]{2,1,0:T(8,128)}, f32[2,24,128]{2,1,0:T(8,128)S(1)}, u32[]{:S(2)}, u32[]{:S(2)}) collective-permute-start(f32[2,24,128]{2,1,0:T(8,128)} %get-tuple-element.18), channel_id=1, source_target_pairs={{0,127},{1,0},{2,1},{3,2},{4,3},{5,4},{6,5},{7,6},{8,7},{9,8},{10,... | collective-permute-start | bytes 73736 | tf_op jit(solution)/shard_map/ppermute | solution.py:620
  21.3 1.7 %collective-permute-done.refs_2_ = f32[2,24,128]{2,1,0:T(8,128)S(1)} collective-permute-done((f32[2,24,128]{2,1,0:T(8,128)}, f32[2,24,128]{2,1,0:T(8,128)S(1)}, u32[]{:S(2)}, u32[]{:S(2)}) %collective-permute-start) | collective-permute-done | bytes 24608 | tf_op jit(solution)/shard_map/ppermute | solution.py:620
  23.0 0.0 collective-permute-done.1.refs_3_
  23.0 0.0 copy-start.4
  23.0 0.6 copy-done.3
  23.6 0.0 copy-done.4
  23.6 18.7 %step.1 = (bf16[2560,128]{1,0:T(8,128)(2,1)}, bf16[2560,128]{1,0:T(8,128)(2,1)}, bf16[8,8,128]{2,1,0:T(8,128)(2,1)}) custom-call(s32[1]{0:T(128)} %bitcast.refs_0_.place, f32[16,24,128]{2,1,0:T(8,128)} %get-tuple-element.16.refs_1_, f32[2,24,128]{2,1,0:T(8,128)} %copy-done.3, f32[2,24,128]{2,1,0:T(8,128)} %copy-done.4, bf16[3,3,12,128]{3,2,1,0:T(8,128)(2,1)} %bitcast.28, ...), custom_call_target="tpu_custom_call" | custom-call | tf_op jit(solution)/shard_map/step/pallas_call | solution.py:541
  42.3 0.0 copy-start.5
  42.3 5.5 %collective-permute-start.2 = (bf16[2560,128]{1,0:T(8,128)(2,1)}, bf16[2560,128]{1,0:T(8,128)(2,1)S(1)}, u32[]{:S(2)}, u32[]{:S(2)}) collective-permute-start(bf16[2560,128]{1,0:T(8,128)(2,1)} %get-tuple-element.20), channel_id=1, source_target_pairs={{0,8},{8,0},{1,9},{9,1},{2,10},{10,2},{3,11},{11,3},{4,12},{12,4},... | collective-permute-start | bytes 1966088 | tf_op jit(solution)/shard_map/ppermute | solution.py:620
  47.8 1.9 %collective-permute-done.2 = bf16[2560,128]{1,0:T(8,128)(2,1)S(1)} collective-permute-done((bf16[2560,128]{1,0:T(8,128)(2,1)}, bf16[2560,128]{1,0:T(8,128)(2,1)S(1)}, u32[]{:S(2)}, u32[]{:S(2)}) %collective-permute-start.2) | collective-permute-done | bytes 655392 | tf_op jit(solution)/shard_map/ppermute | solution.py:620
  49.7 1.3 %add_convert_fusion = bf16[2560,128]{1,0:T(8,128)(2,1)S(1)} fusion(bf16[2560,128]{1,0:T(8,128)(2,1)S(1)} %collective-permute-done.2, bf16[2560,128]{1,0:T(8,128)(2,1)} %get-tuple-element.19), kind=kLoop, calls=%fused_computation | loop fusion | flops 1310720 | bytes 1966080 | tf_op jit(solution)/shard_map/convert_element_type | solution.py:660
  51.0 0.0 copy-done.5
  51.0 0.1 pad_maximum_fusion
  51.1 24.4 %all_to_all.15 = bf16[64,48,128]{2,1,0:T(8,128)(2,1)S(1)} all-to-all(bf16[64,48,128]{2,1,0:T(8,128)(2,1)S(1)} %pad_maximum_fusion), channel_id=1, replica_groups=mesh['y'=4,'x_hi'=2,'core'=2,'x_lo'=2,'z'=4] {'y','x_hi','x_lo','z'}, dimensions={0} | all-to-all | bytes 1572864 | tf_op jit(solution)/shard_map/all_to_all | solution.py:615
  75.5 0.1 slice_reduce_fusion
  75.6 0.1 broadcast_in_dim.8
  75.7 17.1 %all_to_all.16 = bf16[64,40,128]{2,1,0:T(8,128)(2,1)S(1)} all-to-all(bf16[64,40,128]{2,1,0:T(8,128)(2,1)S(1)} %broadcast_in_dim.8), channel_id=1, replica_groups=mesh['y'=4,'x_hi'=2,'core'=2,'x_lo'=2,'z'=4] {'y','x_hi','x_lo','z'}, dimensions={0} | all-to-all | bytes 1310720 | tf_op jit(solution)/shard_map/spread/all_to_all | solution.py:615
  92.9 0.0 copy-start
  92.9 3.0 %collective-permute-start.3 = (bf16[2560,128]{1,0:T(8,128)(2,1)S(1)}, bf16[2560,128]{1,0:T(8,128)(2,1)S(1)}, u32[]{:S(2)}, u32[]{:S(2)}) collective-permute-start(bf16[2560,128]{1,0:T(8,128)(2,1)S(1)} %bitcast.18), channel_id=1, source_target_pairs={{0,8},{8,0},{1,9},{9,1},{2,10},{10,2},{3,11},{11,3},{4,12},{12,4},... | collective-permute-start | bytes 1966088 | tf_op jit(solution)/shard_map/ppermute | solution.py:620
  95.8 0.6 dynamic-slice_bitcast_fusion.tiles
  96.4 1.1 %collective-permute-done.3.other = bf16[2560,128]{1,0:T(8,128)(2,1)S(1)} collective-permute-done((bf16[2560,128]{1,0:T(8,128)(2,1)S(1)}, bf16[2560,128]{1,0:T(8,128)(2,1)S(1)}, u32[]{:S(2)}, u32[]{:S(2)}) %collective-permute-start.3) | collective-permute-done | bytes 655392 | tf_op jit(solution)/shard_map/ppermute | solution.py:620
  97.5 0.0 copy-done
  97.5 0.9 copy-done.1
  98.4 3.3 %unpack.1 = (f32[4,2,1024]{2,1,0:T(2,128)}, f32[3,3,20,128]{3,2,1,0:T(8,128)}, f32[3,3,256,128]{3,2,1,0:T(8,128)}, f32[3,3,128,256]{3,2,1,0:T(8,128)}, f32[3,3,4,128]{3,2,1,0:T(4,128)}) custom-call(s32[1]{0:T(128)} %bitcast.refs_0_.place, bf16[2560,128]{1,0:T(8,128)(2,1)} %bitcast.19, bf16[2560,128]{1,0:T(8,128)(2,1)} %copy-done.1, ...), custom_call_target="tpu_custom_call" | custom-call | tf_op jit(solution)/shard_map/unpack/pallas_call | solution.py:592
  (4 shorter events, 0.0 us)
Async XLA Ops:
  2.8 12.2 %all-to-all-start = ((f32[8,2,16,128]{3,2,1,0:T(8,128)}), f32[8,2,16,128]{3,2,1,0:T(8,128)S(1)}, u32[]{:S(2)}, u32[]{:S(2)}) async-start(f32[8,2,16,128]{3,2,1,0:T(8,128)} %pack.1), calls=%async_computation | async-start | bytes 262144 | tf_op jit(solution)/shard_map/all_to_all | solution.py:615
  15.0 0.7 copy-start.2
  17.4 5.6 %collective-permute-start = (f32[2,24,128]{2,1,0:T(8,128)}, f32[2,24,128]{2,1,0:T(8,128)S(1)}, u32[]{:S(2)}, u32[]{:S(2)}) collective-permute-start(f32[2,24,128]{2,1,0:T(8,128)} %get-tuple-element.17), channel_id=1, source_target_pairs={{0,1},{1,2},{2,3},{3,4},{4,5},{5,6},{6,7},{7,8},{8,9},{9,10},{10,1... | collective-permute-start | bytes 73736 | tf_op jit(solution)/shard_map/ppermute | solution.py:620
  17.6 5.4 %collective-permute-start.1 = (f32[2,24,128]{2,1,0:T(8,128)}, f32[2,24,128]{2,1,0:T(8,128)S(1)}, u32[]{:S(2)}, u32[]{:S(2)}) collective-permute-start(f32[2,24,128]{2,1,0:T(8,128)} %get-tuple-element.18), channel_id=1, source_target_pairs={{0,127},{1,0},{2,1},{3,2},{4,3},{5,4},{6,5},{7,6},{8,7},{9,8},{10,... | collective-permute-start | bytes 73736 | tf_op jit(solution)/shard_map/ppermute | solution.py:620
  23.0 0.6 copy-start.3
  23.0 0.6 copy-start.4
  42.3 8.7 %copy-start.5 = (bf16[8,8,128]{2,1,0:T(8,128)(2,1)S(1)}, bf16[8,8,128]{2,1,0:T(8,128)(2,1)}, u32[]{:S(2)}) copy-start(bf16[8,8,128]{2,1,0:T(8,128)(2,1)} %get-tuple-element.21) | copy-start | bytes 49156
  42.3 7.4 %collective-permute-start.2 = (bf16[2560,128]{1,0:T(8,128)(2,1)}, bf16[2560,128]{1,0:T(8,128)(2,1)S(1)}, u32[]{:S(2)}, u32[]{:S(2)}) collective-permute-start(bf16[2560,128]{1,0:T(8,128)(2,1)} %get-tuple-element.20), channel_id=1, source_target_pairs={{0,8},{8,0},{1,9},{9,1},{2,10},{10,2},{3,11},{11,3},{4,12},{12,4},... | collective-permute-start | bytes 1966088 | tf_op jit(solution)/shard_map/ppermute | solution.py:620
  92.9 4.7 %copy-start = (bf16[64,40,128]{2,1,0:T(8,128)(2,1)}, bf16[64,40,128]{2,1,0:T(8,128)(2,1)S(1)}, u32[]{:S(2)}) copy-start(bf16[64,40,128]{2,1,0:T(8,128)(2,1)S(1)} %all_to_all.16) | copy-start | bytes 1966084
  92.9 4.7 %collective-permute-start.3 = (bf16[2560,128]{1,0:T(8,128)(2,1)S(1)}, bf16[2560,128]{1,0:T(8,128)(2,1)S(1)}, u32[]{:S(2)}, u32[]{:S(2)}) collective-permute-start(bf16[2560,128]{1,0:T(8,128)(2,1)S(1)} %bitcast.18), channel_id=1, source_target_pairs={{0,8},{8,0},{1,9},{9,1},{2,10},{10,2},{3,11},{11,3},{4,12},{12,4},... | collective-permute-start | bytes 1966088 | tf_op jit(solution)/shard_map/ppermute | solution.py:620
  97.5 0.9 copy-start.1

commit v3 on v2

--- a/solution.py
+++ b/solution.py
@@ -45,8 +45,12 @@
     "back_one": (4, 1),
     "three": 2,
     "blocks": 4,
+    "gather": 4,
+    "taps": 4,
+    "enter": 4,
+    "last": 4,
+    "loss": 2,
 }
-EDGE_ROWS = OWN // HALO
 
 
 def mm(x, w):
@@ -145,25 +149,6 @@
             packed[p, r, 4:8] = target[:, r, lanes]
             packed[p, r, 8:12] = jnp.zeros((4, OWN), F32)
             packed[p, r, 12:16] = noise[:, r, lanes]
-
-
-def edges_kernel(packed, coarse, fields, first_columns, last_columns):
-    lane = lax.broadcasted_iota(jnp.int32, (FIELDS, OWN), 1)
-    for g in range(ROWS // EDGE_ROWS):
-        firsts = lasts = jnp.zeros((FIELDS, OWN), F32)
-        for j in range(EDGE_ROWS):
-            r = g * EDGE_ROWS + j
-            fields[r, 0:8] = packed[r, 0:8]
-            fields[r, 8:20] = coarse[r]
-            fields[r, 20:24] = packed[r, 12:16]
-            row = fields[r]
-            here = (lane >= j * HALO) & (lane < (j + 1) * HALO)
-            at = j * HALO
-            firsts = jnp.where(here, pltpu.roll(row, at, 1) if at else row, firsts)
-            at = (j + 1) * HALO % OWN
-            lasts = jnp.where(here, pltpu.roll(row, at, 1) if at else row, lasts)
-        first_columns[g] = firsts
-        last_columns[g] = lasts
 
 
 def stack_inputs(ref, weight, room):
@@ -237,18 +222,12 @@
         zero_edges(ref)
     first_w = stack_inputs(stack, w_first, 16)
 
-    def gather(g):
-        from_left, from_right = left[g], right[g]
-        for j in range(EDGE_ROWS):
-            r = g * EDGE_ROWS + j
-            at = OWN - HALO - j * HALO
-            before = pltpu.roll(from_left, at, 1) if at else from_left
-            after = pltpu.roll(from_right, OWN - j * HALO, 1) if j else from_right
-            wide = with_halo(own[r], before, after)
-            field[r] = wide
-            net[r + 1] = to_cells(lon_shifts(wide[8:24]))
-
-    each(ROWS // EDGE_ROWS, gather)
+    def gather(r):
+        wide = with_halo(own[r], left[r], right[r])
+        field[r] = wide
+        net[r + 1] = to_cells(lon_shifts(wide[8:24]))
+
+    each(ROWS, gather, CHUNK["gather"])
 
     n1, u1 = CHUNK["first"]
 
@@ -271,7 +250,7 @@
     def mean_taps(r):
         taps[r + 1] = mm_nt(last_w, to_lanes(act_c[r]))
 
-    each(ROWS, mean_taps, 4)
+    each(ROWS, mean_taps, CHUNK["taps"])
     in_w = stack_inputs(stack, w_in, FIELDS)
     lane = lax.broadcasted_iota(jnp.int32, (8, LANES), 1)
     held = (lane < OWN + HALO) | (lane >= LANES - HALO)
@@ -289,7 +268,7 @@
         both = jnp.where(low_half, pltpu.roll(mean_r, 4, 0), scaled)
         net[r + 1] = to_cells(lon_shifts(jnp.concatenate([both, field[r, 8:24]], axis=0)))
 
-    each(ROWS, enter, 4)
+    each(ROWS, enter, CHUNK["enter"])
 
     n3, u3 = CHUNK["one"]
 
@@ -351,7 +330,7 @@
     def field_taps(r):
         taps[r + 1] = mm_nt(out_w[0:72], to_lanes(act_c[r]))
 
-    each(ROWS, field_taps, 4)
+    each(ROWS, field_taps, CHUNK["taps"])
 
     def loss(i):
         for k in range(2):
@@ -368,7 +347,7 @@
             cot = (c_out * loss_grad).astype(BF).astype(F32)
             grad_f[r + 1] = jnp.where(low_half, 0.0, cot)
 
-    each(LOW, loss, 2)
+    each(LOW, loss, CHUNK["loss"])
     tiles[...] = den[...].astype(BF)
     last_sum[...] = jnp.zeros_like(last_sum)
 
@@ -381,7 +360,7 @@
         last_sum[...] += mm(cots[:, :OWN].astype(BF), act_c[r, 0:OWN])
         spread_f[r] = to_cells(cots)
 
-    each(ROWS, last_grads, 4)
+    each(ROWS, last_grads, CHUNK["last"])
     near, far = 0, 1
 
     def keep(half, at, value):
@@ -476,29 +455,41 @@
         pltpu.make_async_copy(halves.at[half], mine, sems.at[half]).wait()
 
 
-def unpack_kernel(place, mine, other, tiles, tile, first, down, up, last):
+def unpack_kernel(place, *refs):
+    mine, other = refs[0:4], refs[4:8]
+    parts, tile, first, down, up, last, seat, sem = refs[8:]
     a = pl.program_id(0)
     even = place[0] == 0
-
-    def half(k, at, count):
+    copy = pltpu.make_async_copy(parts.at[place[1], :, pl.ds(parts.shape[2] - CELL_ROWS, CELL_ROWS)], seat, sem)
+
+    @pl.when(a == 0)
+    def _():
+        copy.start()
+
+    def half(k, piece):
+        one, two = mine[piece][...].astype(F32), other[piece][...].astype(F32)
+        return jnp.where(even, one, two) if k == 0 else jnp.where(even, two, one)
+
+    low = half(0, 0).reshape(3, HID1, HID1)
+    high = half(0, 1).reshape(3, HID1, HID1)
+    up[0] = jnp.concatenate([low, high], axis=2)
+    down[0] = half(1, 2).reshape(3, HID2, HID1)
+
+    def small(k, at, count):
         rows = pl.ds(pl.multiple_of(at, 8), count)
-        if k == 0:
-            return jnp.where(even, mine[rows].astype(F32), other[rows].astype(F32))
-        return jnp.where(even, other[rows].astype(F32), mine[rows].astype(F32))
-
-    low = half(0, a * (3 * HID1), 3 * HID1).reshape(3, HID1, HID1)
-    high = half(0, a * (3 * HID1) + UP_ROWS, 3 * HID1).reshape(3, HID1, HID1)
-    up[0] = jnp.concatenate([low, high], axis=2)
-    down[0] = half(1, a * (3 * HID2), 3 * HID2).reshape(3, HID2, HID1)
-    firsts = half(1, BIG_ROWS + a * (3 * FIELDS), 3 * FIELDS)
-    lasts = half(0, BIG_ROWS + a * FIELDS, FIELDS)
+        one, two = mine[3][rows].astype(F32), other[3][rows].astype(F32)
+        return jnp.where(even, one, two) if k == 0 else jnp.where(even, two, one)
+
+    firsts = small(1, a * (3 * FIELDS), 3 * FIELDS)
+    lasts = small(0, a * FIELDS, FIELDS)
     for b in range(3):
         first[0, b] = firsts[b * FIELDS : b * FIELDS + 20]
         last[0, b] = lasts[b * 8 + 4 : b * 8 + 8]
 
-    @pl.when(a == 0)
+    @pl.when(a == 2)
     def _():
-        blocks = tiles[...].astype(F32)
+        copy.wait()
+        blocks = seat[...].astype(F32)
         for k in range(8):
             for r in range(2):
                 tile[:, r, k * OWN : (k + 1) * OWN] = blocks[k, 4 * r : 4 * r + 4]
@@ -523,17 +514,6 @@
     )(target, noise, land_mask, level_index)
 
 
-def edges(packed, coarse):
-    columns = jax.ShapeDtypeStruct((ROWS // EDGE_ROWS, FIELDS, OWN), F32)
-    return pl.pallas_call(
-        edges_kernel,
-        out_shape=(jax.ShapeDtypeStruct((ROWS, FIELDS, OWN), F32), columns, columns),
-        in_specs=in_vmem(2),
-        out_specs=tuple(in_vmem(3)),
-        name="edges",
-    )(packed, coarse)
-
-
 def step(scale, *operands):
     def kernel(*refs):
         step_kernel(scale, *refs)
@@ -546,7 +526,7 @@
             jax.ShapeDtypeStruct((LOW, CELL_ROWS, OWN), BF),
         ),
         in_specs=[in_smem(), *in_vmem(10)],
-        out_specs=(*[pl.BlockSpec(memory_space=pl.ANY)] * 2, *in_vmem(1)),
+        out_specs=(*in_vmem(1), pl.BlockSpec(memory_space=pl.ANY), *in_vmem(1)),
         scratch_shapes=[
             pltpu.VMEM((3, OWN, OWN), F32),
             pltpu.VMEM((OWN, OWN), F32),
@@ -582,9 +562,14 @@
     )(*operands)
 
 
-def unpack(place, mine, other, tiles):
-    whole = pl.BlockSpec((HALF_ROWS, OWN), lambda a: (0, 0))
-    cells = pl.BlockSpec((8, CELL_ROWS, OWN), lambda a: (0, 0, 0))
+def unpack(place, mine, other, parts):
+    third = 3 * HID1
+    pieces = [
+        pl.BlockSpec((third, OWN), lambda a: (a, 0)),
+        pl.BlockSpec((third, OWN), lambda a: (a + UP_ROWS // third, 0)),
+        pl.BlockSpec((2 * third, OWN), lambda a: (a, 0)),
+        pl.BlockSpec((HALF_ROWS - BIG_ROWS, OWN), lambda a: (BIG_ROWS // (HALF_ROWS - BIG_ROWS), 0)),
+    ]
 
     def taps(rows, lanes):
         return pl.BlockSpec((1, 3, rows, lanes), lambda a: (a, 0, 0, 0))
@@ -599,7 +584,7 @@
             jax.ShapeDtypeStruct((3, 3, HID1, HID2), F32),
             jax.ShapeDtypeStruct((3, 3, 4, HID1), F32),
         ),
-        in_specs=[in_smem(), whole, whole, cells],
+        in_specs=[in_smem(), *pieces, *pieces, pl.BlockSpec(memory_space=pl.ANY)],
         out_specs=(
             pl.BlockSpec((4, 2, 8 * OWN), lambda a: (0, 0, 0)),
             taps(20, HID1),
@@ -607,8 +592,9 @@
             taps(HID1, HID2),
             taps(4, HID1),
         ),
+        scratch_shapes=[pltpu.VMEM((8, CELL_ROWS, OWN), BF), pltpu.SemaphoreType.DMA(())],
         name="unpack",
-    )(place, mine, other, tiles)
+    )(place, *[mine] * 4, *[other] * 4, parts)
 
 
 def all_to_all(value, axes):
@@ -635,15 +621,15 @@
     diffuse_out,
 ):
     scale = 1.0 / (target.shape[0] * math.sqrt(target.shape[1] * target.shape[2] * lax.axis_size(STRIPS)))
-    place = lax.axis_index("core").astype(jnp.int32)[None]
+    place = jnp.stack([lax.axis_index("core"), lax.axis_index(("y", "x_hi"))]).astype(jnp.int32)
     packed = all_to_all(pack(target, noise, land_mask, level_index), LAT).reshape(ROWS, 16, OWN)
-    fields, first_columns, last_columns = edges(packed, coarse.transpose(1, 0, 2).astype(F32))
+    fields = jnp.concatenate([packed[:, :8], coarse.transpose(1, 0, 2).astype(F32), packed[:, 12:]], axis=1)
     grads, partner, tiles = step(
         scale,
         place,
         fields,
-        shift_by(last_columns, STRIPS, 1),
-        shift_by(first_columns, STRIPS, -1),
+        shift_by(fields, STRIPS, 1),
+        shift_by(fields, STRIPS, -1),
         frozen_first.transpose(0, 1, 3, 2),
         frozen_middle.reshape(3, 3 * HID1, HID1),
         frozen_last,
@@ -660,11 +646,10 @@
     sent = jnp.concatenate([half.astype(BF).reshape(chips, rows, OWN), blocks], axis=1)
     parts = all_to_all(sent, CHIPS)
     total = parts[:, :rows].astype(F32).sum(0).astype(BF)
-    seats = parts.reshape(chips // lats, lats, rows + CELL_ROWS, OWN)[:, :, rows:]
-    tiles = lax.dynamic_index_in_dim(seats, lax.axis_index(("y", "x_hi")), 0, False)
+    parts = parts.reshape(chips // lats, lats, rows + CELL_ROWS, OWN)
     with jax.named_scope("spread"):
         mine = all_to_all(jnp.broadcast_to(total[None], (chips, rows, OWN)), CHIPS).reshape(HALF_ROWS, OWN)
-    tile, first, down, up, last = unpack(place, mine, shift_by(mine, "core", 1), tiles)
+    tile, first, down, up, last = unpack(place, mine, shift_by(mine, "core", 1), parts)
     return (tile, first.transpose(0, 1, 3, 2), down, up, last)
 
 

time: 102 us -> 101 us (level)
  waiting for transfers between devices: 8.72 us -> 14.9 us
  blocking collectives: 41.5 us -> 36.1 us
  local copies, waits for them, and re-layouts: 4.34 us -> 2.47 us
  Pallas kernels: 25.2 us -> 24.1 us
    ppermute x4, waiting for transfers between devices: 4.74 us -> 10.3 us  [shift_by(): lax.ppermute(value, axes, [(i, (i + step) % count) for i in range(count)])]
    all_to_all x2, blocking collectives: 41.5 us -> 36.1 us  [all_to_all(): return lax.all_to_all(value, axes, split_axis=0, concat_axis=0, tiled=True)]
    pallas_call x1 -> x0, Pallas kernels: 1.75 us -> none  [edges(): pl.pallas_call(edges_kernel, out_shape=(jax.ShapeDtypeStruct((ROWS, FIELD...]
    unnamed x12 -> x14, local copies, waits for them, and re-layouts: 2.14 us -> 1.54 us
  transfers between devices with their start and end apart: 5 -> 5, of which waited for: 4 -> 5; matrix products, arithmetic and copies ran while one was open for 2% -> 1% of each run, Pallas kernels for 0% -> 0%
where the time goes in v3:
time: 101 us; the launch traced here: 100 us
  blocking collectives  36.1 us (36%)
  Pallas kernels  24.1 us (24%)
  starting transfers between devices  19.4 us (19%)
  waiting for transfers between devices  14.9 us (15%)
  local copies, waits for them, and re-layouts  2.47 us (2%)
  other arithmetic  2.04 us (2%)
  between operations  1.37 us (1%)
    all_to_all x2, blocking collectives, all_to_all(): return lax.all_to_all(value, axes, split_axis=0, concat_axis=0, tiled=True)  36.1 us
    pallas_call x1, Pallas kernels, step(): pl.pallas_call(kernel, out_shape=(jax.ShapeDtypeStruct((HALF_ROWS, OWN),...  18.4 us
    ppermute x4, starting transfers between devices, shift_by(): lax.ppermute(value, axes, [(i, (i + step) % count) for i in range(count)])  12.6 us
    ppermute x4, waiting for transfers between devices, shift_by(): lax.ppermute(value, axes, [(i, (i + step) % count) for i in range(count)])  10.3 us
    all_to_all x1, starting transfers between devices, all_to_all(): return lax.all_to_all(value, axes, split_axis=0, concat_axis=0, tiled=True)  6.78 us
    all_to_all x1, waiting for transfers between devices, all_to_all(): return lax.all_to_all(value, axes, split_axis=0, concat_axis=0, tiled=True)  4.63 us
    pallas_call x1, Pallas kernels, unpack(): pl.pallas_call(unpack_kernel, grid=(3,), out_shape=(jax.ShapeDtypeStruct(...  4.13 us
  transfers between devices with their start and end apart: 5, of which 5 were waited for; matrix products, arithmetic and copies ran while one was open for 1% of the time, Pallas kernels for 0%

profile of v3, /device:TPU:1, one launch (start us, length us, event | category | flops | bytes accessed | tf_op | source)
XLA Modules:
  0.0 100.4 jit_solution(12806351867766421147)
XLA Ops:
  1.3 1.5 %pack.1 = f32[8,2,16,128]{3,2,1,0:T(8,128)} custom-call(f32[4,2,1024]{2,1,0:T(2,128)} %target.1, f32[4,2,1024]{2,1,0:T(2,128)} %noise.1, s32[2,1024]{1,0:T(2,128)} %land_mask.1, s32[1,1]{1,0:T(1,128)S(6)} %copy.21.level), custom_call_target="tpu_custom_call" | custom-call | tf_op jit(solution)/shard_map/pack/pallas_call | solution.py:508
  2.8 6.8 %all-to-all-start = ((f32[8,2,16,128]{3,2,1,0:T(8,128)}), f32[8,2,16,128]{3,2,1,0:T(8,128)S(1)}, u32[]{:S(2)}, u32[]{:S(2)}) async-start(f32[8,2,16,128]{3,2,1,0:T(8,128)} %pack.1), calls=%async_computation | async-start | bytes 262144 | tf_op jit(solution)/shard_map/all_to_all | solution.py:601
  9.6 0.8 copy.20
  10.4 4.6 %all-to-all-done = f32[8,2,16,128]{3,2,1,0:T(8,128)S(1)} async-done(((f32[8,2,16,128]{3,2,1,0:T(8,128)}), f32[8,2,16,128]{3,2,1,0:T(8,128)S(1)}, u32[]{:S(2)}, u32[]{:S(2)}) %all-to-all-start) | async-done | bytes 131104 | tf_op jit(solution)/shard_map/all_to_all | solution.py:601
  15.1 0.0 copy-start.3
  15.1 3.2 %collective-permute-start.1 = (f32[16,24,128]{2,1,0:T(8,128)S(1)}, f32[16,24,128]{2,1,0:T(8,128)S(1)}, u32[]{:S(2)}, u32[]{:S(2)}) collective-permute-start(f32[16,24,128]{2,1,0:T(8,128)S(1)} %pad_maximum_fusion.1.refs_1_), channel_id=1, source_target_pairs={{0,127},{1,0},{2,1},{3,2},{4,3},{5,4},{6,5},{7,6},{8,7},{9,8},{10,... | collective-permute-start | bytes 589832 | tf_op jit(solution)/shard_map/ppermute | solution.py:606
  18.3 0.0 collective-permute-start
  18.3 0.6 pad_add_fusion.refs_0_.place
  18.9 3.1 %collective-permute-done.1.refs_3_ = f32[16,24,128]{2,1,0:T(8,128)S(1)} collective-permute-done((f32[16,24,128]{2,1,0:T(8,128)S(1)}, f32[16,24,128]{2,1,0:T(8,128)S(1)}, u32[]{:S(2)}, u32[]{:S(2)}) %collective-permute-start.1) | collective-permute-done | bytes 196640 | tf_op jit(solution)/shard_map/ppermute | solution.py:606
  22.0 0.0 copy-start.4
  22.0 3.5 %collective-permute-done.refs_2_ = f32[16,24,128]{2,1,0:T(8,128)S(1)} collective-permute-done((f32[16,24,128]{2,1,0:T(8,128)S(1)}, f32[16,24,128]{2,1,0:T(8,128)S(1)}, u32[]{:S(2)}, u32[]{:S(2)}) %collective-permute-start) | collective-permute-done | bytes 196640 | tf_op jit(solution)/shard_map/ppermute | solution.py:606
  25.5 0.0 copy-start.5
  25.5 0.0 copy-done.3
  25.5 0.0 copy-done.4
  25.5 0.7 copy-done.5
  26.2 18.4 %step.1 = (bf16[2560,128]{1,0:T(8,128)(2,1)}, bf16[2560,128]{1,0:T(8,128)(2,1)}, bf16[8,8,128]{2,1,0:T(8,128)(2,1)}) custom-call(s32[2]{0:T(128)} %pad_add_fusion.refs_0_.place, f32[16,24,128]{2,1,0:T(8,128)} %copy-done.3, f32[16,24,128]{2,1,0:T(8,128)} %copy-done.5, f32[16,24,128]{2,1,0:T(8,128)} %copy-done.4, bf16[3,3,12,128]{3,2,1,0:T(8,128)(2,1)} %bitcast.31, ...), custom_call_target="tpu_custom_call" | custom-call | tf_op jit(solution)/shard_map/step/pallas_call | solution.py:521
  44.6 0.0 copy-start.6
  44.7 6.4 %collective-permute-start.2 = (bf16[2560,128]{1,0:T(8,128)(2,1)}, bf16[2560,128]{1,0:T(8,128)(2,1)S(1)}, u32[]{:S(2)}, u32[]{:S(2)}) collective-permute-start(bf16[2560,128]{1,0:T(8,128)(2,1)} %get-tuple-element.14), channel_id=1, source_target_pairs={{0,8},{8,0},{1,9},{9,1},{2,10},{10,2},{3,11},{11,3},{4,12},{12,4},... | collective-permute-start | bytes 1966088 | tf_op jit(solution)/shard_map/ppermute | solution.py:606
  51.1 1.9 %collective-permute-done.2 = bf16[2560,128]{1,0:T(8,128)(2,1)S(1)} collective-permute-done((bf16[2560,128]{1,0:T(8,128)(2,1)}, bf16[2560,128]{1,0:T(8,128)(2,1)S(1)}, u32[]{:S(2)}, u32[]{:S(2)}) %collective-permute-start.2) | collective-permute-done | bytes 655392 | tf_op jit(solution)/shard_map/ppermute | solution.py:606
  53.0 1.3 %add_convert_fusion = bf16[2560,128]{1,0:T(8,128)(2,1)S(1)} fusion(bf16[2560,128]{1,0:T(8,128)(2,1)S(1)} %collective-permute-done.2, bf16[2560,128]{1,0:T(8,128)(2,1)} %get-tuple-element.13), kind=kLoop, calls=%fused_computation | loop fusion | flops 1310720 | bytes 1966080 | tf_op jit(solution)/shard_map/convert_element_type | solution.py:646
  54.3 0.0 copy-done.6
  54.3 0.1 pad_maximum_fusion
  54.4 19.0 %all_to_all.15 = bf16[64,48,128]{2,1,0:T(8,128)(2,1)S(1)} all-to-all(bf16[64,48,128]{2,1,0:T(8,128)(2,1)S(1)} %pad_maximum_fusion), channel_id=1, replica_groups=mesh['y'=4,'x_hi'=2,'core'=2,'x_lo'=2,'z'=4] {'y','x_hi','x_lo','z'}, dimensions={0} | all-to-all | bytes 1572864 | tf_op jit(solution)/shard_map/all_to_all | solution.py:601
  73.4 0.1 slice_reduce_fusion
  73.5 0.1 broadcast_in_dim.5
  73.6 17.1 %all_to_all.16 = bf16[64,40,128]{2,1,0:T(8,128)(2,1)S(1)} all-to-all(bf16[64,40,128]{2,1,0:T(8,128)(2,1)S(1)} %broadcast_in_dim.5), channel_id=1, replica_groups=mesh['y'=4,'x_hi'=2,'core'=2,'x_lo'=2,'z'=4] {'y','x_hi','x_lo','z'}, dimensions={0} | all-to-all | bytes 1310720 | tf_op jit(solution)/shard_map/spread/all_to_all | solution.py:601
  90.7 0.0 copy-done.2
  90.7 3.0 %collective-permute-start.3 = (bf16[2560,128]{1,0:T(8,128)(2,1)S(1)}, bf16[2560,128]{1,0:T(8,128)(2,1)S(1)}, u32[]{:S(2)}, u32[]{:S(2)}) collective-permute-start(bf16[2560,128]{1,0:T(8,128)(2,1)S(1)} %bitcast.16), channel_id=1, source_target_pairs={{0,8},{8,0},{1,9},{9,1},{2,10},{10,2},{3,11},{11,3},{4,12},{12,4},... | collective-permute-start | bytes 1966088 | tf_op jit(solution)/shard_map/ppermute | solution.py:606
  93.7 1.7 %collective-permute-done.3.refs_4_.refs_5_.refs_6_.refs_7_ = bf16[2560,128]{1,0:T(8,128)(2,1)S(1)} collective-permute-done((bf16[2560,128]{1,0:T(8,128)(2,1)S(1)}, bf16[2560,128]{1,0:T(8,128)(2,1)S(1)}, u32[]{:S(2)}, u32[]{:S(2)}) %collective-permute-start.3) | collective-permute-done | bytes 655392 | tf_op jit(solution)/shard_map/ppermute | solution.py:606
  95.4 0.0 copy-done
  95.4 0.8 copy-done.1
  96.2 4.1 %unpack.1 = (f32[4,2,1024]{2,1,0:T(2,128)}, f32[3,3,20,128]{3,2,1,0:T(8,128)}, f32[3,3,256,128]{3,2,1,0:T(8,128)}, f32[3,3,128,256]{3,2,1,0:T(8,128)}, f32[3,3,4,128]{3,2,1,0:T(4,128)}) custom-call(s32[2]{0:T(128)} %pad_add_fusion.refs_0_.place, bf16[2560,128]{1,0:T(8,128)(2,1)} %bitcast.17, bf16[2560,128]{1,0:T(8,128)(2,1)} %bitcast.18, ...), custom_call_target="tpu_custom_call" | custom-call | tf_op jit(solution)/shard_map/unpack/pallas_call | solution.py:577
  (7 shorter events, 0.1 us)
Async XLA Ops:
  2.8 12.2 %all-to-all-start = ((f32[8,2,16,128]{3,2,1,0:T(8,128)}), f32[8,2,16,128]{3,2,1,0:T(8,128)S(1)}, u32[]{:S(2)}, u32[]{:S(2)}) async-start(f32[8,2,16,128]{3,2,1,0:T(8,128)} %pack.1), calls=%async_computation | async-start | bytes 262144 | tf_op jit(solution)/shard_map/all_to_all | solution.py:601
  15.1 10.4 %copy-start.3 = (f32[16,24,128]{2,1,0:T(8,128)}, f32[16,24,128]{2,1,0:T(8,128)S(1)}, u32[]{:S(2)}) copy-start(f32[16,24,128]{2,1,0:T(8,128)S(1)} %pad_maximum_fusion.1.refs_1_) | copy-start | bytes 589828
  15.1 6.9 %collective-permute-start.1 = (f32[16,24,128]{2,1,0:T(8,128)S(1)}, f32[16,24,128]{2,1,0:T(8,128)S(1)}, u32[]{:S(2)}, u32[]{:S(2)}) collective-permute-start(f32[16,24,128]{2,1,0:T(8,128)S(1)} %pad_maximum_fusion.1.refs_1_), channel_id=1, source_target_pairs={{0,127},{1,0},{2,1},{3,2},{4,3},{5,4},{6,5},{7,6},{8,7},{9,8},{10,... | collective-permute-start | bytes 589832 | tf_op jit(solution)/shard_map/ppermute | solution.py:606
  18.3 7.2 %collective-permute-start = (f32[16,24,128]{2,1,0:T(8,128)S(1)}, f32[16,24,128]{2,1,0:T(8,128)S(1)}, u32[]{:S(2)}, u32[]{:S(2)}) collective-permute-start(f32[16,24,128]{2,1,0:T(8,128)S(1)} %pad_maximum_fusion.1.refs_1_), channel_id=1, source_target_pairs={{0,1},{1,2},{2,3},{3,4},{4,5},{5,6},{6,7},{7,8},{8,9},{9,10},{10,1... | collective-permute-start | bytes 589832 | tf_op jit(solution)/shard_map/ppermute | solution.py:606
  22.0 3.5 %copy-start.4 = (f32[16,24,128]{2,1,0:T(8,128)}, f32[16,24,128]{2,1,0:T(8,128)S(1)}, u32[]{:S(2)}) copy-start(f32[16,24,128]{2,1,0:T(8,128)S(1)} %collective-permute-done.1.refs_3_) | copy-start | bytes 589828
  25.5 0.7 copy-start.5
  44.6 9.6 %copy-start.6 = (bf16[8,8,128]{2,1,0:T(8,128)(2,1)S(1)}, bf16[8,8,128]{2,1,0:T(8,128)(2,1)}, u32[]{:S(2)}) copy-start(bf16[8,8,128]{2,1,0:T(8,128)(2,1)} %get-tuple-element.15) | copy-start | bytes 49156
  44.7 8.4 %collective-permute-start.2 = (bf16[2560,128]{1,0:T(8,128)(2,1)}, bf16[2560,128]{1,0:T(8,128)(2,1)S(1)}, u32[]{:S(2)}, u32[]{:S(2)}) collective-permute-start(bf16[2560,128]{1,0:T(8,128)(2,1)} %get-tuple-element.14), channel_id=1, source_target_pairs={{0,8},{8,0},{1,9},{9,1},{2,10},{10,2},{3,11},{11,3},{4,12},{12,4},... | collective-permute-start | bytes 1966088 | tf_op jit(solution)/shard_map/ppermute | solution.py:606
  73.4 17.3 %copy-start.2 = (bf16[64,48,128]{2,1,0:T(8,128)(2,1)}, bf16[64,48,128]{2,1,0:T(8,128)(2,1)S(1)}, u32[]{:S(2)}) copy-start(bf16[64,48,128]{2,1,0:T(8,128)(2,1)S(1)} %all_to_all.15) | copy-start | bytes 2359300
  90.7 4.7 %copy-start = (bf16[64,40,128]{2,1,0:T(8,128)(2,1)}, bf16[64,40,128]{2,1,0:T(8,128)(2,1)S(1)}, u32[]{:S(2)}) copy-start(bf16[64,40,128]{2,1,0:T(8,128)(2,1)S(1)} %all_to_all.16) | copy-start | bytes 1966084
  90.7 4.7 %collective-permute-start.3 = (bf16[2560,128]{1,0:T(8,128)(2,1)S(1)}, bf16[2560,128]{1,0:T(8,128)(2,1)S(1)}, u32[]{:S(2)}, u32[]{:S(2)}) collective-permute-start(bf16[2560,128]{1,0:T(8,128)(2,1)S(1)} %bitcast.16), channel_id=1, source_target_pairs={{0,8},{8,0},{1,9},{9,1},{2,10},{10,2},{3,11},{11,3},{4,12},{12,4},... | collective-permute-start | bytes 1966088 | tf_op jit(solution)/shard_map/ppermute | solution.py:606
  95.4 0.8 copy-start.1

commit v4 on v3

--- a/solution.py
+++ b/solution.py
@@ -35,21 +35,21 @@
 HALF_ROWS = 2560
 CELL_ROWS = 8
 CHUNK = {
+    "gather": 8,
     "first": (8, 1),
-    "second": (4, 2),
+    "second": (4, 4),
+    "taps": 8,
+    "enter": 8,
     "one": (8, 1),
     "two": (4, 2),
     "up": (8, 1),
+    "three": 2,
+    "loss": 4,
+    "last": 8,
     "back_three": (8, 1),
-    "back_two": (2, 2),
-    "back_one": (4, 1),
-    "three": 2,
     "blocks": 4,
-    "gather": 4,
-    "taps": 4,
-    "enter": 4,
-    "last": 4,
-    "loss": 2,
+    "back_two": (2, 4),
+    "back_one": (4, 2),
 }
 
 
@@ -173,8 +173,8 @@
     scale,
     place,
     own,
-    left,
-    right,
+    pair,
+    across,
     w_first,
     w_middle,
     w_last,
@@ -220,10 +220,12 @@
     ) = scratch
     for ref in (net, hid, pooled, up_taps, taps, grad_f, grad_c, grad_b):
         zero_edges(ref)
+    even = place[1] == 0
     first_w = stack_inputs(stack, w_first, 16)
 
     def gather(r):
-        wide = with_halo(own[r], left[r], right[r])
+        near, far = pair[r], across[r]
+        wide = with_halo(own[r], jnp.where(even, far, near), jnp.where(even, near, far))
         field[r] = wide
         net[r + 1] = to_cells(lon_shifts(wide[8:24]))
 
@@ -455,44 +457,51 @@
         pltpu.make_async_copy(halves.at[half], mine, sems.at[half]).wait()
 
 
-def unpack_kernel(place, *refs):
-    mine, other = refs[0:4], refs[4:8]
-    parts, tile, first, down, up, last, seat, sem = refs[8:]
-    a = pl.program_id(0)
-    even = place[0] == 0
-    copy = pltpu.make_async_copy(parts.at[place[1], :, pl.ds(parts.shape[2] - CELL_ROWS, CELL_ROWS)], seat, sem)
-
-    @pl.when(a == 0)
-    def _():
+def unpack_kernel(place, mine, other, parts, tile, first, down, up, last, halves, seat, downs, ups, sems):
+    seats = parts.at[place[2], :, pl.ds(parts.shape[2] - CELL_ROWS, CELL_ROWS)]
+    arrive = [
+        pltpu.make_async_copy(mine, halves.at[0], sems.at[0]),
+        pltpu.make_async_copy(other, halves.at[1], sems.at[1]),
+        pltpu.make_async_copy(seats, seat, sems.at[2]),
+    ]
+    for copy in arrive:
         copy.start()
-
-    def half(k, piece):
-        one, two = mine[piece][...].astype(F32), other[piece][...].astype(F32)
-        return jnp.where(even, one, two) if k == 0 else jnp.where(even, two, one)
-
-    low = half(0, 0).reshape(3, HID1, HID1)
-    high = half(0, 1).reshape(3, HID1, HID1)
-    up[0] = jnp.concatenate([low, high], axis=2)
-    down[0] = half(1, 2).reshape(3, HID2, HID1)
-
-    def small(k, at, count):
-        rows = pl.ds(pl.multiple_of(at, 8), count)
-        one, two = mine[3][rows].astype(F32), other[3][rows].astype(F32)
-        return jnp.where(even, one, two) if k == 0 else jnp.where(even, two, one)
-
-    firsts = small(1, a * (3 * FIELDS), 3 * FIELDS)
-    lasts = small(0, a * FIELDS, FIELDS)
-    for b in range(3):
-        first[0, b] = firsts[b * FIELDS : b * FIELDS + 20]
-        last[0, b] = lasts[b * 8 + 4 : b * 8 + 8]
-
-    @pl.when(a == 2)
-    def _():
+    for copy in arrive:
         copy.wait()
-        blocks = seat[...].astype(F32)
-        for k in range(8):
-            for r in range(2):
-                tile[:, r, k * OWN : (k + 1) * OWN] = blocks[k, 4 * r : 4 * r + 4]
+    low, high = place[0], 1 - place[0]
+
+    def leave(a, ups_a, downs_a):
+        return (
+            pltpu.make_async_copy(ups_a, up.at[a], sems.at[0]),
+            pltpu.make_async_copy(downs_a, down.at[a], sems.at[1]),
+        )
+
+    def thirds(a):
+        at = pl.multiple_of(a * (3 * HID1), 3 * HID1)
+        for k in range(2):
+            piece = halves[low, pl.ds(at + k * UP_ROWS, 3 * HID1)]
+            ups[a, :, :, k * HID1 : (k + 1) * HID1] = piece.astype(F32).reshape(3, HID1, HID1)
+        piece = halves[high, pl.ds(2 * at, 3 * HID2)]
+        downs[a] = piece.astype(F32).reshape(3, HID2, HID1)
+        for copy in leave(a, ups.at[a], downs.at[a]):
+            copy.start()
+
+    each(3, thirds)
+    firsts = halves[high, BIG_ROWS : BIG_ROWS + IN_ROWS].astype(F32)
+    lasts = halves[low, BIG_ROWS : BIG_ROWS + 80].astype(F32)
+    for a in range(3):
+        for b in range(3):
+            at = (a * 3 + b) * FIELDS
+            first[a, b] = firsts[at : at + 20]
+            at = (a * 3 + b) * 8 + 4
+            last[a, b] = lasts[at : at + 4]
+    blocks = seat[...].astype(F32)
+    for k in range(8):
+        for r in range(2):
+            tile[:, r, k * OWN : (k + 1) * OWN] = blocks[k, 4 * r : 4 * r + 4]
+    for a in range(3):
+        for copy in leave(a, ups.at[a], downs.at[a]):
+            copy.wait()
 
 
 def in_vmem(count):
@@ -526,7 +535,7 @@
             jax.ShapeDtypeStruct((LOW, CELL_ROWS, OWN), BF),
         ),
         in_specs=[in_smem(), *in_vmem(10)],
-        out_specs=(*in_vmem(1), pl.BlockSpec(memory_space=pl.ANY), *in_vmem(1)),
+        out_specs=tuple(in_vmem(3)),
         scratch_shapes=[
             pltpu.VMEM((3, OWN, OWN), F32),
             pltpu.VMEM((OWN, OWN), F32),
@@ -563,20 +572,10 @@
 
 
 def unpack(place, mine, other, parts):
-    third = 3 * HID1
-    pieces = [
-        pl.BlockSpec((third, OWN), lambda a: (a, 0)),
-        pl.BlockSpec((third, OWN), lambda a: (a + UP_ROWS // third, 0)),
-        pl.BlockSpec((2 * third, OWN), lambda a: (a, 0)),
-        pl.BlockSpec((HALF_ROWS - BIG_ROWS, OWN), lambda a: (BIG_ROWS // (HALF_ROWS - BIG_ROWS), 0)),
-    ]
-
-    def taps(rows, lanes):
-        return pl.BlockSpec((1, 3, rows, lanes), lambda a: (a, 0, 0, 0))
-
+    anywhere = pl.BlockSpec(memory_space=pl.ANY)
+    vmem = in_vmem(1)[0]
     return pl.pallas_call(
         unpack_kernel,
-        grid=(3,),
         out_shape=(
             jax.ShapeDtypeStruct((4, 2, 8 * OWN), F32),
             jax.ShapeDtypeStruct((3, 3, 20, HID1), F32),
@@ -584,26 +583,30 @@
             jax.ShapeDtypeStruct((3, 3, HID1, HID2), F32),
             jax.ShapeDtypeStruct((3, 3, 4, HID1), F32),
         ),
-        in_specs=[in_smem(), *pieces, *pieces, pl.BlockSpec(memory_space=pl.ANY)],
-        out_specs=(
-            pl.BlockSpec((4, 2, 8 * OWN), lambda a: (0, 0, 0)),
-            taps(20, HID1),
-            taps(HID2, HID1),
-            taps(HID1, HID2),
-            taps(4, HID1),
-        ),
-        scratch_shapes=[pltpu.VMEM((8, CELL_ROWS, OWN), BF), pltpu.SemaphoreType.DMA(())],
+        in_specs=[in_smem(), *[pl.BlockSpec(memory_space=pltpu.MemorySpace.HBM)] * 3],
+        out_specs=(vmem, vmem, anywhere, anywhere, vmem),
+        scratch_shapes=[
+            pltpu.VMEM((2, HALF_ROWS, OWN), BF),
+            pltpu.VMEM((8, CELL_ROWS, OWN), BF),
+            pltpu.VMEM((3, 3, HID2, HID1), F32),
+            pltpu.VMEM((3, 3, HID1, HID2), F32),
+            pltpu.SemaphoreType.DMA((3,)),
+        ],
         name="unpack",
-    )(place, *[mine] * 4, *[other] * 4, parts)
+    )(place, mine, other, parts)
 
 
 def all_to_all(value, axes):
     return lax.all_to_all(value, axes, split_axis=0, concat_axis=0, tiled=True)
 
 
-def shift_by(value, axes, step):
+def swap(value, axes, offset):
     count = lax.axis_size(axes)
-    return lax.ppermute(value, axes, [(i, (i + step) % count) for i in range(count)])
+    pairs = []
+    for i in range(offset, count + offset, 2):
+        here, there = i % count, (i + 1) % count
+        pairs += [(here, there), (there, here)]
+    return lax.ppermute(value, axes, sorted(set(pairs)))
 
 
 def local(
@@ -621,15 +624,18 @@
     diffuse_out,
 ):
     scale = 1.0 / (target.shape[0] * math.sqrt(target.shape[1] * target.shape[2] * lax.axis_size(STRIPS)))
-    place = jnp.stack([lax.axis_index("core"), lax.axis_index(("y", "x_hi"))]).astype(jnp.int32)
+    place = jnp.stack([lax.axis_index("core"), lax.axis_index("z") % 2, lax.axis_index(("y", "x_hi"))])
+    place = place.astype(jnp.int32)
     packed = all_to_all(pack(target, noise, land_mask, level_index), LAT).reshape(ROWS, 16, OWN)
     fields = jnp.concatenate([packed[:, :8], coarse.transpose(1, 0, 2).astype(F32), packed[:, 12:]], axis=1)
+    across = swap(fields, STRIPS, 1)
+    pair = swap(fields, STRIPS, 0)
     grads, partner, tiles = step(
         scale,
         place,
         fields,
-        shift_by(fields, STRIPS, 1),
-        shift_by(fields, STRIPS, -1),
+        pair,
+        across,
         frozen_first.transpose(0, 1, 3, 2),
         frozen_middle.reshape(3, 3 * HID1, HID1),
         frozen_last,
@@ -641,7 +647,7 @@
     chips = lax.axis_size(CHIPS)
     rows = HALF_ROWS // chips
     lats = tiles.shape[0]
-    half = grads.astype(F32) + shift_by(partner, "core", 1).astype(F32)
+    half = grads.astype(F32) + swap(partner, "core", 0).astype(F32)
     blocks = jnp.broadcast_to(tiles[None], (chips // lats, *tiles.shape)).reshape(chips, CELL_ROWS, OWN)
     sent = jnp.concatenate([half.astype(BF).reshape(chips, rows, OWN), blocks], axis=1)
     parts = all_to_all(sent, CHIPS)
@@ -649,7 +655,7 @@
     parts = parts.reshape(chips // lats, lats, rows + CELL_ROWS, OWN)
     with jax.named_scope("spread"):
         mine = all_to_all(jnp.broadcast_to(total[None], (chips, rows, OWN)), CHIPS).reshape(HALF_ROWS, OWN)
-    tile, first, down, up, last = unpack(place, mine, shift_by(mine, "core", 1), parts)
+    tile, first, down, up, last = unpack(place, mine, swap(mine, "core", 0), parts)
     return (tile, first.transpose(0, 1, 3, 2), down, up, last)
 
 

time: 101 us -> 96.6 us (0.956)
  waiting for transfers between devices: 14.9 us -> 12.3 us
  Pallas kernels: 24.1 us -> 22 us
  blocking collectives: 36.1 us -> 37.9 us
  starting transfers between devices: 19.4 us -> 18.1 us
    ppermute x4, waiting for transfers between devices: 10.3 us -> 7.62 us  [swap(): return lax.ppermute(value, axes, sorted(set(pairs)))]
    pallas_call x1, Pallas kernels: 18.4 us -> 16.4 us  [step(): pl.pallas_call(kernel, out_shape=(jax.ShapeDtypeStruct((HALF_ROWS, OWN),...]
    all_to_all x2, blocking collectives: 36.1 us -> 37.9 us  [all_to_all(): return lax.all_to_all(value, axes, split_axis=0, concat_axis=0, tiled=True)]
    ppermute x4, starting transfers between devices: 12.6 us -> 11.3 us  [swap(): return lax.ppermute(value, axes, sorted(set(pairs)))]
where the time goes in v4:
time: 96.6 us; the launch traced here: 96.1 us
  blocking collectives  37.9 us (39%)
  Pallas kernels  22 us (23%)
  starting transfers between devices  18.1 us (19%)
  waiting for transfers between devices  12.3 us (13%)
  local copies, waits for them, and re-layouts  2.47 us (3%)
  other arithmetic  2.04 us (2%)
  between operations  1.37 us (1%)
    all_to_all x2, blocking collectives, all_to_all(): return lax.all_to_all(value, axes, split_axis=0, concat_axis=0, tiled=True)  37.9 us
    pallas_call x1, Pallas kernels, step(): pl.pallas_call(kernel, out_shape=(jax.ShapeDtypeStruct((HALF_ROWS, OWN),...  16.4 us
    ppermute x4, starting transfers between devices, swap(): return lax.ppermute(value, axes, sorted(set(pairs)))  11.3 us
    ppermute x4, waiting for transfers between devices, swap(): return lax.ppermute(value, axes, sorted(set(pairs)))  7.62 us
    all_to_all x1, starting transfers between devices, all_to_all(): return lax.all_to_all(value, axes, split_axis=0, concat_axis=0, tiled=True)  6.78 us
    all_to_all x1, waiting for transfers between devices, all_to_all(): return lax.all_to_all(value, axes, split_axis=0, concat_axis=0, tiled=True)  4.63 us
    pallas_call x1, Pallas kernels, unpack(): pl.pallas_call(unpack_kernel, out_shape=(jax.ShapeDtypeStruct((4, 2, 8 *...  4.04 us
  transfers between devices with their start and end apart: 5, of which 5 were waited for; matrix products, arithmetic and copies ran while one was open for 1% of the time, Pallas kernels for 0%

profile of v4, /device:TPU:1, one launch (start us, length us, event | category | flops | bytes accessed | tf_op | source)
XLA Modules:
  0.0 96.1 jit_solution(1020623172161688220)
XLA Ops:
  1.3 1.5 %pack.1 = f32[8,2,16,128]{3,2,1,0:T(8,128)} custom-call(f32[4,2,1024]{2,1,0:T(2,128)} %target.1, f32[4,2,1024]{2,1,0:T(2,128)} %noise.1, s32[2,1024]{1,0:T(2,128)} %land_mask.1, s32[1,1]{1,0:T(1,128)S(6)} %copy.21.level), custom_call_target="tpu_custom_call" | custom-call | tf_op jit(solution)/shard_map/pack/pallas_call | solution.py:517
  2.8 6.8 %all-to-all-start = ((f32[8,2,16,128]{3,2,1,0:T(8,128)}), f32[8,2,16,128]{3,2,1,0:T(8,128)S(1)}, u32[]{:S(2)}, u32[]{:S(2)}) async-start(f32[8,2,16,128]{3,2,1,0:T(8,128)} %pack.1), calls=%async_computation | async-start | bytes 262144 | tf_op jit(solution)/shard_map/all_to_all | solution.py:600
  9.6 0.8 copy.20
  10.4 4.6 %all-to-all-done = f32[8,2,16,128]{3,2,1,0:T(8,128)S(1)} async-done(((f32[8,2,16,128]{3,2,1,0:T(8,128)}), f32[8,2,16,128]{3,2,1,0:T(8,128)S(1)}, u32[]{:S(2)}, u32[]{:S(2)}) %all-to-all-start) | async-done | bytes 131104 | tf_op jit(solution)/shard_map/all_to_all | solution.py:600
  15.1 0.0 copy-start.2
  15.1 3.2 %collective-permute-start.1 = (f32[16,24,128]{2,1,0:T(8,128)S(1)}, f32[16,24,128]{2,1,0:T(8,128)S(1)}, u32[]{:S(2)}, u32[]{:S(2)}) collective-permute-start(f32[16,24,128]{2,1,0:T(8,128)S(1)} %pad_maximum_fusion.1.refs_1_), channel_id=1, source_target_pairs={{0,127},{1,2},{2,1},{3,4},{4,3},{5,6},{6,5},{7,8},{8,7},{9,10},{10... | collective-permute-start | bytes 589832 | tf_op jit(solution)/shard_map/ppermute | solution.py:609
  18.3 0.0 collective-permute-start
  18.3 0.6 pad_add_fusion.refs_0_.place
  18.9 3.5 %collective-permute-done.1.refs_3_ = f32[16,24,128]{2,1,0:T(8,128)S(1)} collective-permute-done((f32[16,24,128]{2,1,0:T(8,128)S(1)}, f32[16,24,128]{2,1,0:T(8,128)S(1)}, u32[]{:S(2)}, u32[]{:S(2)}) %collective-permute-start.1) | collective-permute-done | bytes 196640 | tf_op jit(solution)/shard_map/ppermute | solution.py:609
  22.4 0.0 copy-start.4
  22.4 0.5 collective-permute-done.refs_2_
  22.8 0.0 copy-start.5
  22.8 0.0 copy-done.2
  22.9 0.2 copy-done.4
  23.1 0.5 copy-done.5
  23.5 16.4 %step.1 = (bf16[2560,128]{1,0:T(8,128)(2,1)}, bf16[2560,128]{1,0:T(8,128)(2,1)}, bf16[8,8,128]{2,1,0:T(8,128)(2,1)}) custom-call(s32[3]{0:T(128)} %pad_add_fusion.refs_0_.place, f32[16,24,128]{2,1,0:T(8,128)} %copy-done.2, f32[16,24,128]{2,1,0:T(8,128)} %copy-done.5, f32[16,24,128]{2,1,0:T(8,128)} %copy-done.4, bf16[3,3,12,128]{3,2,1,0:T(8,128)(2,1)} %bitcast.29, ...), custom_call_target="tpu_custom_call" | custom-call | tf_op jit(solution)/shard_map/step/pallas_call | solution.py:530
  40.0 0.0 copy-start.6
  40.0 5.1 %collective-permute-start.2 = (bf16[2560,128]{1,0:T(8,128)(2,1)}, bf16[2560,128]{1,0:T(8,128)(2,1)S(1)}, u32[]{:S(2)}, u32[]{:S(2)}) collective-permute-start(bf16[2560,128]{1,0:T(8,128)(2,1)} %get-tuple-element.14), channel_id=1, source_target_pairs={{0,8},{8,0},{1,9},{9,1},{2,10},{10,2},{3,11},{11,3},{4,12},{12,4},... | collective-permute-start | bytes 1966088 | tf_op jit(solution)/shard_map/ppermute | solution.py:609
  45.1 1.9 %collective-permute-done.2 = bf16[2560,128]{1,0:T(8,128)(2,1)S(1)} collective-permute-done((bf16[2560,128]{1,0:T(8,128)(2,1)}, bf16[2560,128]{1,0:T(8,128)(2,1)S(1)}, u32[]{:S(2)}, u32[]{:S(2)}) %collective-permute-start.2) | collective-permute-done | bytes 655392 | tf_op jit(solution)/shard_map/ppermute | solution.py:609
  47.0 1.3 %add_convert_fusion = bf16[2560,128]{1,0:T(8,128)(2,1)S(1)} fusion(bf16[2560,128]{1,0:T(8,128)(2,1)S(1)} %collective-permute-done.2, bf16[2560,128]{1,0:T(8,128)(2,1)} %get-tuple-element.13), kind=kLoop, calls=%fused_computation | loop fusion | flops 1310720 | bytes 1966080 | tf_op jit(solution)/shard_map/convert_element_type | solution.py:652
  48.3 0.0 copy-done.6
  48.3 0.1 pad_maximum_fusion
  48.4 20.8 %all_to_all.15 = bf16[64,48,128]{2,1,0:T(8,128)(2,1)S(1)} all-to-all(bf16[64,48,128]{2,1,0:T(8,128)(2,1)S(1)} %pad_maximum_fusion), channel_id=1, replica_groups=mesh['y'=4,'x_hi'=2,'core'=2,'x_lo'=2,'z'=4] {'y','x_hi','x_lo','z'}, dimensions={0} | all-to-all | bytes 1572864 | tf_op jit(solution)/shard_map/all_to_all | solution.py:600
  69.1 0.1 slice_reduce_fusion
  69.2 0.1 broadcast_in_dim.5
  69.3 17.1 %all_to_all.16 = bf16[64,40,128]{2,1,0:T(8,128)(2,1)S(1)} all-to-all(bf16[64,40,128]{2,1,0:T(8,128)(2,1)S(1)} %broadcast_in_dim.5), channel_id=1, replica_groups=mesh['y'=4,'x_hi'=2,'core'=2,'x_lo'=2,'z'=4] {'y','x_hi','x_lo','z'}, dimensions={0} | all-to-all | bytes 1310720 | tf_op jit(solution)/shard_map/spread/all_to_all | solution.py:600
  86.5 0.0 copy-done
  86.5 3.0 %collective-permute-start.3 = (bf16[2560,128]{1,0:T(8,128)(2,1)S(1)}, bf16[2560,128]{1,0:T(8,128)(2,1)S(1)}, u32[]{:S(2)}, u32[]{:S(2)}) collective-permute-start(bf16[2560,128]{1,0:T(8,128)(2,1)S(1)} %bitcast.18), channel_id=1, source_target_pairs={{0,8},{8,0},{1,9},{9,1},{2,10},{10,2},{3,11},{11,3},{4,12},{12,4},... | collective-permute-start | bytes 1966088 | tf_op jit(solution)/shard_map/ppermute | solution.py:609
  89.4 1.7 %collective-permute-done.3.other = bf16[2560,128]{1,0:T(8,128)(2,1)S(1)} collective-permute-done((bf16[2560,128]{1,0:T(8,128)(2,1)S(1)}, bf16[2560,128]{1,0:T(8,128)(2,1)S(1)}, u32[]{:S(2)}, u32[]{:S(2)}) %collective-permute-start.3) | collective-permute-done | bytes 655392 | tf_op jit(solution)/shard_map/ppermute | solution.py:609
  91.2 0.0 copy-done.1
  91.2 0.8 copy-done.3
  92.0 4.0 %unpack.1 = (f32[4,2,1024]{2,1,0:T(2,128)}, f32[3,3,20,128]{3,2,1,0:T(8,128)}, f32[3,3,256,128]{3,2,1,0:T(8,128)}, f32[3,3,128,256]{3,2,1,0:T(8,128)}, f32[3,3,4,128]{3,2,1,0:T(4,128)}) custom-call(s32[3]{0:T(128)} %pad_add_fusion.refs_0_.place, bf16[2560,128]{1,0:T(8,128)(2,1)} %bitcast.19, bf16[2560,128]{1,0:T(8,128)(2,1)} %copy-done.3, ...), custom_call_target="tpu_custom_call" | custom-call | tf_op jit(solution)/shard_map/unpack/pallas_call | solution.py:577
  (7 shorter events, 0.1 us)
Async XLA Ops:
  2.8 12.2 %all-to-all-start = ((f32[8,2,16,128]{3,2,1,0:T(8,128)}), f32[8,2,16,128]{3,2,1,0:T(8,128)S(1)}, u32[]{:S(2)}, u32[]{:S(2)}) async-start(f32[8,2,16,128]{3,2,1,0:T(8,128)} %pack.1), calls=%async_computation | async-start | bytes 262144 | tf_op jit(solution)/shard_map/all_to_all | solution.py:600
  15.1 7.8 %copy-start.2 = (f32[16,24,128]{2,1,0:T(8,128)}, f32[16,24,128]{2,1,0:T(8,128)S(1)}, u32[]{:S(2)}) copy-start(f32[16,24,128]{2,1,0:T(8,128)S(1)} %pad_maximum_fusion.1.refs_1_) | copy-start | bytes 589828
  15.1 7.3 %collective-permute-start.1 = (f32[16,24,128]{2,1,0:T(8,128)S(1)}, f32[16,24,128]{2,1,0:T(8,128)S(1)}, u32[]{:S(2)}, u32[]{:S(2)}) collective-permute-start(f32[16,24,128]{2,1,0:T(8,128)S(1)} %pad_maximum_fusion.1.refs_1_), channel_id=1, source_target_pairs={{0,127},{1,2},{2,1},{3,4},{4,3},{5,6},{6,5},{7,8},{8,7},{9,10},{10... | collective-permute-start | bytes 589832 | tf_op jit(solution)/shard_map/ppermute | solution.py:609
  18.3 4.5 %collective-permute-start = (f32[16,24,128]{2,1,0:T(8,128)S(1)}, f32[16,24,128]{2,1,0:T(8,128)S(1)}, u32[]{:S(2)}, u32[]{:S(2)}) collective-permute-start(f32[16,24,128]{2,1,0:T(8,128)S(1)} %pad_maximum_fusion.1.refs_1_), channel_id=1, source_target_pairs={{0,1},{1,0},{2,3},{3,2},{4,5},{5,4},{6,7},{7,6},{8,9},{9,8},{10,11... | collective-permute-start | bytes 589832 | tf_op jit(solution)/shard_map/ppermute | solution.py:609
  22.4 0.7 copy-start.4
  22.8 0.7 copy-start.5
  40.0 8.3 %copy-start.6 = (bf16[8,8,128]{2,1,0:T(8,128)(2,1)S(1)}, bf16[8,8,128]{2,1,0:T(8,128)(2,1)}, u32[]{:S(2)}) copy-start(bf16[8,8,128]{2,1,0:T(8,128)(2,1)} %get-tuple-element.15) | copy-start | bytes 49156
  40.0 7.0 %collective-permute-start.2 = (bf16[2560,128]{1,0:T(8,128)(2,1)}, bf16[2560,128]{1,0:T(8,128)(2,1)S(1)}, u32[]{:S(2)}, u32[]{:S(2)}) collective-permute-start(bf16[2560,128]{1,0:T(8,128)(2,1)} %get-tuple-element.14), channel_id=1, source_target_pairs={{0,8},{8,0},{1,9},{9,1},{2,10},{10,2},{3,11},{11,3},{4,12},{12,4},... | collective-permute-start | bytes 1966088 | tf_op jit(solution)/shard_map/ppermute | solution.py:609
  69.1 17.4 %copy-start = (bf16[64,48,128]{2,1,0:T(8,128)(2,1)}, bf16[64,48,128]{2,1,0:T(8,128)(2,1)S(1)}, u32[]{:S(2)}) copy-start(bf16[64,48,128]{2,1,0:T(8,128)(2,1)S(1)} %all_to_all.15) | copy-start | bytes 2359300
  86.5 4.7 %copy-start.1 = (bf16[64,40,128]{2,1,0:T(8,128)(2,1)}, bf16[64,40,128]{2,1,0:T(8,128)(2,1)S(1)}, u32[]{:S(2)}) copy-start(bf16[64,40,128]{2,1,0:T(8,128)(2,1)S(1)} %all_to_all.16) | copy-start | bytes 1966084
  86.5 4.7 %collective-permute-start.3 = (bf16[2560,128]{1,0:T(8,128)(2,1)S(1)}, bf16[2560,128]{1,0:T(8,128)(2,1)S(1)}, u32[]{:S(2)}, u32[]{:S(2)}) collective-permute-start(bf16[2560,128]{1,0:T(8,128)(2,1)S(1)} %bitcast.18), channel_id=1, source_target_pairs={{0,8},{8,0},{1,9},{9,1},{2,10},{10,2},{3,11},{11,3},{4,12},{12,4},... | collective-permute-start | bytes 1966088 | tf_op jit(solution)/shard_map/ppermute | solution.py:609
  91.2 0.8 copy-start.3

commit v5 on v4

--- a/solution.py
+++ b/solution.py
@@ -136,9 +136,18 @@
     lax.fori_loop(0, count, step, 0, unroll=unroll)
 
 
-def pack_kernel(target, noise, land_mask, level, packed):
-    power = level[...].astype(F32) / (LEVELS - 1)
-    sigma = jnp.broadcast_to(0.02 * jnp.exp(power * math.log(4000.0)), (1, OWN))
+def pack_kernel(level, target_far, noise_far, mask_far, packed, target, noise, land_mask, sems):
+    arrive = [
+        pltpu.make_async_copy(target_far, target, sems.at[0]),
+        pltpu.make_async_copy(noise_far, noise, sems.at[1]),
+        pltpu.make_async_copy(mask_far, land_mask, sems.at[2]),
+    ]
+    for copy in arrive:
+        copy.start()
+    power = jnp.full((1, OWN), level[0, 0], jnp.int32).astype(F32) / (LEVELS - 1)
+    sigma = 0.02 * jnp.exp(power * math.log(4000.0))
+    for copy in arrive:
+        copy.wait()
     weight = 1.0 + land_mask[...].astype(F32)
     for p in range(packed.shape[0]):
         lanes = slice(p * OWN, (p + 1) * OWN)
@@ -216,11 +225,14 @@
         last_sum,
         den,
         halves,
+        w_near,
         sems,
     ) = scratch
     for ref in (net, hid, pooled, up_taps, taps, grad_f, grad_c, grad_b):
         zero_edges(ref)
     even = place[1] == 0
+    fetch = pltpu.make_async_copy(w_middle, w_near, sems.at[2])
+    fetch.start()
     first_w = stack_inputs(stack, w_first, 16)
 
     def gather(r):
@@ -238,7 +250,8 @@
         hid[pl.ds(n1 * i + 1, n1)] = jax.nn.silu(pre).astype(BF).reshape(n1, WIDE, HID1)
 
     each(ROWS // n1, first, u1)
-    middle_w = jnp.concatenate([w_middle[a] for a in range(3)], axis=1)
+    fetch.wait()
+    middle_w = jnp.concatenate([w_near[a] for a in range(3)], axis=1)
 
     n2, u2 = CHUNK["second"]
 
@@ -457,55 +470,59 @@
         pltpu.make_async_copy(halves.at[half], mine, sems.at[half]).wait()
 
 
-def unpack_kernel(place, mine, other, parts, tile, first, down, up, last, halves, seat, downs, ups, sems):
-    seats = parts.at[place[2], :, pl.ds(parts.shape[2] - CELL_ROWS, CELL_ROWS)]
-    arrive = [
-        pltpu.make_async_copy(mine, halves.at[0], sems.at[0]),
-        pltpu.make_async_copy(other, halves.at[1], sems.at[1]),
-        pltpu.make_async_copy(seats, seat, sems.at[2]),
-    ]
-    for copy in arrive:
-        copy.start()
-    for copy in arrive:
-        copy.wait()
-    low, high = place[0], 1 - place[0]
-
-    def leave(a, ups_a, downs_a):
+def unpack_kernel(place, mine, other, seats, tile, first, down, up, last, downs, ups, firsts, lasts, tiles, sems):
+    even = place[0] == 0
+
+    def half(k, at, count):
+        one, two = mine[pl.ds(at, count)], other[pl.ds(at, count)]
+        return (jnp.where(even, one, two) if k == 0 else jnp.where(even, two, one)).astype(F32)
+
+    def leave(a):
         return (
-            pltpu.make_async_copy(ups_a, up.at[a], sems.at[0]),
-            pltpu.make_async_copy(downs_a, down.at[a], sems.at[1]),
+            pltpu.make_async_copy(ups.at[a], up.at[a], sems.at[0]),
+            pltpu.make_async_copy(downs.at[a], down.at[a], sems.at[1]),
         )
 
     def thirds(a):
         at = pl.multiple_of(a * (3 * HID1), 3 * HID1)
         for k in range(2):
-            piece = halves[low, pl.ds(at + k * UP_ROWS, 3 * HID1)]
-            ups[a, :, :, k * HID1 : (k + 1) * HID1] = piece.astype(F32).reshape(3, HID1, HID1)
-        piece = halves[high, pl.ds(2 * at, 3 * HID2)]
-        downs[a] = piece.astype(F32).reshape(3, HID2, HID1)
-        for copy in leave(a, ups.at[a], downs.at[a]):
+            piece = half(0, at + k * UP_ROWS, 3 * HID1)
+            ups[a, :, :, k * HID1 : (k + 1) * HID1] = piece.reshape(3, HID1, HID1)
+        downs[a] = half(1, 2 * at, 3 * HID2).reshape(3, HID2, HID1)
+        for copy in leave(a):
             copy.start()
 
     each(3, thirds)
-    firsts = halves[high, BIG_ROWS : BIG_ROWS + IN_ROWS].astype(F32)
-    lasts = halves[low, BIG_ROWS : BIG_ROWS + 80].astype(F32)
+    inputs = half(1, BIG_ROWS, IN_ROWS)
+    outputs = half(0, BIG_ROWS, 80)
     for a in range(3):
         for b in range(3):
             at = (a * 3 + b) * FIELDS
-            first[a, b] = firsts[at : at + 20]
+            firsts[a, b] = inputs[at : at + 20]
             at = (a * 3 + b) * 8 + 4
-            last[a, b] = lasts[at : at + 4]
-    blocks = seat[...].astype(F32)
+            lasts[a, b] = outputs[at : at + 4]
+    small = [pltpu.make_async_copy(firsts, first, sems.at[2]), pltpu.make_async_copy(lasts, last, sems.at[3])]
+    for copy in small:
+        copy.start()
+    blocks = seats[...].astype(F32)
     for k in range(8):
         for r in range(2):
-            tile[:, r, k * OWN : (k + 1) * OWN] = blocks[k, 4 * r : 4 * r + 4]
+            tiles[:, r, k * OWN : (k + 1) * OWN] = blocks[k, 4 * r : 4 * r + 4]
+    small.append(pltpu.make_async_copy(tiles, tile, sems.at[4]))
+    small[2].start()
+    for copy in small:
+        copy.wait()
     for a in range(3):
-        for copy in leave(a, ups.at[a], downs.at[a]):
+        for copy in leave(a):
             copy.wait()
 
 
 def in_vmem(count):
     return [pl.BlockSpec(memory_space=pltpu.MemorySpace.VMEM) for _ in range(count)]
+
+
+def in_hbm(count):
+    return [pl.BlockSpec(memory_space=pltpu.MemorySpace.HBM) for _ in range(count)]
 
 
 def in_smem():
@@ -517,10 +534,17 @@
     return pl.pallas_call(
         pack_kernel,
         out_shape=jax.ShapeDtypeStruct((lats, 2, 16, OWN), F32),
-        in_specs=in_vmem(4),
+        in_specs=[in_smem(), *in_hbm(3)],
         out_specs=in_vmem(1)[0],
+        scratch_shapes=[
+            pltpu.VMEM(target.shape, F32),
+            pltpu.VMEM(noise.shape, F32),
+            pltpu.VMEM(land_mask.shape, jnp.int32),
+            pltpu.SemaphoreType.DMA((3,)),
+        ],
+        compiler_params=pltpu.CompilerParams(vmem_limit_bytes=8 * 2**20),
         name="pack",
-    )(target, noise, land_mask, level_index)
+    )(level_index, target, noise, land_mask)
 
 
 def step(scale, *operands):
@@ -534,7 +558,7 @@
             jax.ShapeDtypeStruct((HALF_ROWS, OWN), BF),
             jax.ShapeDtypeStruct((LOW, CELL_ROWS, OWN), BF),
         ),
-        in_specs=[in_smem(), *in_vmem(10)],
+        in_specs=[in_smem(), *in_vmem(4), *in_hbm(1), *in_vmem(5)],
         out_specs=tuple(in_vmem(3)),
         scratch_shapes=[
             pltpu.VMEM((3, OWN, OWN), F32),
@@ -565,35 +589,34 @@
             pltpu.VMEM((80, HID1), F32),
             pltpu.VMEM((LOW, CELL_ROWS, OWN), F32),
             pltpu.VMEM((2, HALF_ROWS, OWN), BF),
-            pltpu.SemaphoreType.DMA((2,)),
+            pltpu.VMEM((3, 3 * HID1, HID1), BF),
+            pltpu.SemaphoreType.DMA((3,)),
         ],
+        compiler_params=pltpu.CompilerParams(vmem_limit_bytes=44 * 2**20),
         name="step",
     )(*operands)
 
 
-def unpack(place, mine, other, parts):
-    anywhere = pl.BlockSpec(memory_space=pl.ANY)
-    vmem = in_vmem(1)[0]
+def unpack(place, mine, other, seats):
+    outs = (
+        (4, 2, 8 * OWN),
+        (3, 3, 20, HID1),
+        (3, 3, HID2, HID1),
+        (3, 3, HID1, HID2),
+        (3, 3, 4, HID1),
+    )
     return pl.pallas_call(
         unpack_kernel,
-        out_shape=(
-            jax.ShapeDtypeStruct((4, 2, 8 * OWN), F32),
-            jax.ShapeDtypeStruct((3, 3, 20, HID1), F32),
-            jax.ShapeDtypeStruct((3, 3, HID2, HID1), F32),
-            jax.ShapeDtypeStruct((3, 3, HID1, HID2), F32),
-            jax.ShapeDtypeStruct((3, 3, 4, HID1), F32),
-        ),
-        in_specs=[in_smem(), *[pl.BlockSpec(memory_space=pltpu.MemorySpace.HBM)] * 3],
-        out_specs=(vmem, vmem, anywhere, anywhere, vmem),
+        out_shape=tuple(jax.ShapeDtypeStruct(shape, F32) for shape in outs),
+        in_specs=[in_smem(), *in_vmem(3)],
+        out_specs=tuple([pl.BlockSpec(memory_space=pl.ANY)] * 5),
         scratch_shapes=[
-            pltpu.VMEM((2, HALF_ROWS, OWN), BF),
-            pltpu.VMEM((8, CELL_ROWS, OWN), BF),
-            pltpu.VMEM((3, 3, HID2, HID1), F32),
-            pltpu.VMEM((3, 3, HID1, HID2), F32),
-            pltpu.SemaphoreType.DMA((3,)),
+            *(pltpu.VMEM(outs[k], F32) for k in (2, 3, 1, 4, 0)),
+            pltpu.SemaphoreType.DMA((5,)),
         ],
+        compiler_params=pltpu.CompilerParams(vmem_limit_bytes=16 * 2**20),
         name="unpack",
-    )(place, mine, other, parts)
+    )(place, mine, other, seats)
 
 
 def all_to_all(value, axes):
@@ -624,7 +647,7 @@
     diffuse_out,
 ):
     scale = 1.0 / (target.shape[0] * math.sqrt(target.shape[1] * target.shape[2] * lax.axis_size(STRIPS)))
-    place = jnp.stack([lax.axis_index("core"), lax.axis_index("z") % 2, lax.axis_index(("y", "x_hi"))])
+    place = jnp.stack([lax.axis_index("core"), lax.axis_index("z") % 2])
     place = place.astype(jnp.int32)
     packed = all_to_all(pack(target, noise, land_mask, level_index), LAT).reshape(ROWS, 16, OWN)
     fields = jnp.concatenate([packed[:, :8], coarse.transpose(1, 0, 2).astype(F32), packed[:, 12:]], axis=1)
@@ -652,10 +675,11 @@
     sent = jnp.concatenate([half.astype(BF).reshape(chips, rows, OWN), blocks], axis=1)
     parts = all_to_all(sent, CHIPS)
     total = parts[:, :rows].astype(F32).sum(0).astype(BF)
-    parts = parts.reshape(chips // lats, lats, rows + CELL_ROWS, OWN)
+    seats = parts.reshape(chips // lats, lats, rows + CELL_ROWS, OWN)[:, :, rows:]
+    seats = lax.dynamic_index_in_dim(seats, lax.axis_index(("y", "x_hi")), 0, False)
     with jax.named_scope("spread"):
         mine = all_to_all(jnp.broadcast_to(total[None], (chips, rows, OWN)), CHIPS).reshape(HALF_ROWS, OWN)
-    tile, first, down, up, last = unpack(place, mine, swap(mine, "core", 0), parts)
+    tile, first, down, up, last = unpack(place, mine, swap(mine, "core", 0), seats)
     return (tile, first.transpose(0, 1, 3, 2), down, up, last)
 
 

time: 96.6 us -> 92.4 us (0.957)
  Pallas kernels: 22 us -> 17.3 us
  local copies, waits for them, and re-layouts: 2.47 us -> 4.15 us
  other arithmetic: 2.04 us -> 0.47 us
    pallas_call x1, Pallas kernels: 16.4 us -> 14.4 us  [step(): pl.pallas_call(kernel, out_shape=(jax.ShapeDtypeStruct((HALF_ROWS, OWN),...]
    pallas_call x1, Pallas kernels: 4.04 us -> 2.11 us  [unpack(): pl.pallas_call(unpack_kernel, out_shape=tuple((jax.ShapeDtypeStruct(shape...]
    unnamed x14 -> x20, local copies, waits for them, and re-layouts: 1.54 us -> 3.19 us
    convert_element_type x1, other arithmetic: 1.26 us -> 0.17 us  [local(): half.astype(BF).reshape(chips, rows, OWN)]
where the time goes in v5:
time: 92.4 us; the launch traced here: 91.8 us
  blocking collectives  37.9 us (41%)
  starting transfers between devices  18 us (19%)
  Pallas kernels  17.3 us (19%)
  waiting for transfers between devices  12.5 us (14%)
  local copies, waits for them, and re-layouts  4.15 us (4%)
  between operations  1.53 us (2%)
    all_to_all x2, blocking collectives, all_to_all(): return lax.all_to_all(value, axes, split_axis=0, concat_axis=0, tiled=True)  37.9 us
    pallas_call x1, Pallas kernels, step(): pl.pallas_call(kernel, out_shape=(jax.ShapeDtypeStruct((HALF_ROWS, OWN),...  14.4 us
    ppermute x4, starting transfers between devices, swap(): return lax.ppermute(value, axes, sorted(set(pairs)))  11.2 us
    ppermute x4, waiting for transfers between devices, swap(): return lax.ppermute(value, axes, sorted(set(pairs)))  7.84 us
    all_to_all x1, starting transfers between devices, all_to_all(): return lax.all_to_all(value, axes, split_axis=0, concat_axis=0, tiled=True)  6.79 us
    all_to_all x1, waiting for transfers between devices, all_to_all(): return lax.all_to_all(value, axes, split_axis=0, concat_axis=0, tiled=True)  4.63 us
    unnamed x20, local copies, waits for them, and re-layouts  3.19 us
    pallas_call x1, Pallas kernels, unpack(): pl.pallas_call(unpack_kernel, out_shape=tuple((jax.ShapeDtypeStruct(shape...  2.11 us
  transfers between devices with their start and end apart: 5, of which 5 were waited for; matrix products, arithmetic and copies ran while one was open for 1% of the time, Pallas kernels for 0%

profile of v5, /device:TPU:1, one launch (start us, length us, event | category | flops | bytes accessed | tf_op | source)
XLA Modules:
  0.0 91.8 jit_solution(1614096398062940419)
XLA Ops:
  0.6 0.0 copy-start.1
  0.6 0.0 copy-start
  0.7 0.0 copy-start.3
  0.7 0.0 copy-start.4
  1.4 0.0 copy-start.5
  1.4 0.7 copy-done.5
  2.2 0.8 copy-done.6
  2.9 0.7 copy-done.9
  3.6 0.8 pack.1
  4.5 6.8 %all-to-all-start = ((f32[8,2,16,128]{3,2,1,0:T(8,128)}), f32[8,2,16,128]{3,2,1,0:T(8,128)S(1)}, u32[]{:S(2)}, u32[]{:S(2)}) async-start(f32[8,2,16,128]{3,2,1,0:T(8,128)} %pack.1), calls=%async_computation | async-start | bytes 262144 | tf_op jit(solution)/shard_map/all_to_all | solution.py:623
  11.3 0.8 copy.20
  12.1 4.6 %all-to-all-done = f32[8,2,16,128]{3,2,1,0:T(8,128)S(1)} async-done(((f32[8,2,16,128]{3,2,1,0:T(8,128)}), f32[8,2,16,128]{3,2,1,0:T(8,128)S(1)}, u32[]{:S(2)}, u32[]{:S(2)}) %all-to-all-start) | async-done | bytes 131104 | tf_op jit(solution)/shard_map/all_to_all | solution.py:623
  16.8 3.2 %collective-permute-start.1 = (f32[16,24,128]{2,1,0:T(8,128)S(1)}, f32[16,24,128]{2,1,0:T(8,128)S(1)}, u32[]{:S(2)}, u32[]{:S(2)}) collective-permute-start(f32[16,24,128]{2,1,0:T(8,128)S(1)} %pad_maximum_fusion.1.refs_1_), channel_id=1, source_target_pairs={{0,127},{1,2},{2,1},{3,4},{4,3},{5,6},{6,5},{7,8},{8,7},{9,10},{10... | collective-permute-start | bytes 589832 | tf_op jit(solution)/shard_map/ppermute | solution.py:632
  20.0 0.0 collective-permute-start
  20.0 0.1 pad_add_fusion.refs_0_.place
  20.1 4.0 %collective-permute-done.1.refs_3_ = f32[16,24,128]{2,1,0:T(8,128)S(1)} collective-permute-done((f32[16,24,128]{2,1,0:T(8,128)S(1)}, f32[16,24,128]{2,1,0:T(8,128)S(1)}, u32[]{:S(2)}, u32[]{:S(2)}) %collective-permute-start.1) | collective-permute-done | bytes 196640 | tf_op jit(solution)/shard_map/ppermute | solution.py:632
  24.1 0.5 collective-permute-done.refs_2_
  24.5 0.0 copy-done.1
  24.6 0.0 copy-start.2
  24.6 1.0 %copy-done.2 = bf16[3,3,128,128]{3,2,1,0:T(8,128)(2,1)S(1)} copy-done((bf16[3,3,128,128]{3,2,1,0:T(8,128)(2,1)S(1)}, bf16[3,3,128,128]{3,2,1,0:T(8,128)(2,1)}, u32[]{:S(2)}) %copy-start.2) | copy-done | bytes 294936
  25.5 14.4 %step.1 = (bf16[2560,128]{1,0:T(8,128)(2,1)S(1)}, bf16[2560,128]{1,0:T(8,128)(2,1)S(1)}, bf16[8,8,128]{2,1,0:T(8,128)(2,1)S(1)}) custom-call(s32[2]{0:T(128)S(1)} %pad_add_fusion.refs_0_.place, f32[16,24,128]{2,1,0:T(8,128)S(1)} %pad_maximum_fusion.1.refs_1_, f32[16,24,128]{2,1,0:T(8,128)S(1)} %collective-permute-done.refs_2_, ...), custom_call_target="tpu_custom_call" | custom-call | tf_op jit(solution)/shard_map/step/pallas_call | solution.py:554
  39.9 5.0 %collective-permute-start.2 = (bf16[2560,128]{1,0:T(8,128)(2,1)S(1)}, bf16[2560,128]{1,0:T(8,128)(2,1)S(1)}, u32[]{:S(2)}, u32[]{:S(2)}) collective-permute-start(bf16[2560,128]{1,0:T(8,128)(2,1)S(1)} %get-tuple-element.14), channel_id=1, source_target_pairs={{0,8},{8,0},{1,9},{9,1},{2,10},{10,2},{3,11},{11,3},{4,12},{12,4},... | collective-permute-start | bytes 1966088 | tf_op jit(solution)/shard_map/ppermute | solution.py:632
  44.9 1.7 %collective-permute-done.2 = bf16[2560,128]{1,0:T(8,128)(2,1)S(1)} collective-permute-done((bf16[2560,128]{1,0:T(8,128)(2,1)S(1)}, bf16[2560,128]{1,0:T(8,128)(2,1)S(1)}, u32[]{:S(2)}, u32[]{:S(2)}) %collective-permute-start.2) | collective-permute-done | bytes 655392 | tf_op jit(solution)/shard_map/ppermute | solution.py:632
  46.7 0.2 add_convert_fusion
  46.9 0.1 pad_maximum_fusion
  46.9 20.7 %all_to_all.15 = bf16[64,48,128]{2,1,0:T(8,128)(2,1)S(1)} all-to-all(bf16[64,48,128]{2,1,0:T(8,128)(2,1)S(1)} %pad_maximum_fusion), channel_id=1, replica_groups=mesh['y'=4,'x_hi'=2,'core'=2,'x_lo'=2,'z'=4] {'y','x_hi','x_lo','z'}, dimensions={0} | all-to-all | bytes 1572864 | tf_op jit(solution)/shard_map/all_to_all | solution.py:623
  67.7 0.1 slice_reduce_fusion
  67.8 0.1 broadcast_in_dim.5
  67.9 17.1 %all_to_all.16 = bf16[64,40,128]{2,1,0:T(8,128)(2,1)S(1)} all-to-all(bf16[64,40,128]{2,1,0:T(8,128)(2,1)S(1)} %broadcast_in_dim.5), channel_id=1, replica_groups=mesh['y'=4,'x_hi'=2,'core'=2,'x_lo'=2,'z'=4] {'y','x_hi','x_lo','z'}, dimensions={0} | all-to-all | bytes 1310720 | tf_op jit(solution)/shard_map/spread/all_to_all | solution.py:623
  85.0 3.0 %collective-permute-start.3 = (bf16[2560,128]{1,0:T(8,128)(2,1)S(1)}, bf16[2560,128]{1,0:T(8,128)(2,1)S(1)}, u32[]{:S(2)}, u32[]{:S(2)}) collective-permute-start(bf16[2560,128]{1,0:T(8,128)(2,1)S(1)} %bitcast.18), channel_id=1, source_target_pairs={{0,8},{8,0},{1,9},{9,1},{2,10},{10,2},{3,11},{11,3},{4,12},{12,4},... | collective-permute-start | bytes 1966088 | tf_op jit(solution)/shard_map/ppermute | solution.py:632
  88.0 1.7 %collective-permute-done.3.other = bf16[2560,128]{1,0:T(8,128)(2,1)S(1)} collective-permute-done((bf16[2560,128]{1,0:T(8,128)(2,1)S(1)}, bf16[2560,128]{1,0:T(8,128)(2,1)S(1)}, u32[]{:S(2)}, u32[]{:S(2)}) %collective-permute-start.3) | collective-permute-done | bytes 655392 | tf_op jit(solution)/shard_map/ppermute | solution.py:632
  89.7 2.1 %unpack.1 = (f32[4,2,1024]{2,1,0:T(2,128)}, f32[3,3,20,128]{3,2,1,0:T(8,128)}, f32[3,3,256,128]{3,2,1,0:T(8,128)}, f32[3,3,128,256]{3,2,1,0:T(8,128)}, f32[3,3,4,128]{3,2,1,0:T(4,128)}) custom-call(s32[2]{0:T(128)S(1)} %pad_add_fusion.refs_0_.place, bf16[2560,128]{1,0:T(8,128)(2,1)S(1)} %bitcast.19, bf16[2560,128]{1,0:T(8,128)(2,1)S(1)} %collective-permute-done.3.other, ...), custom_call_target="tpu_custom_call" | custom-call | tf_op jit(solution)/shard_map/unpack/pallas_call | solution.py:608
  (15 shorter events, 0.1 us)
Async XLA Ops:
  0.6 23.9 %copy-start.1 = (bf16[3,3,128,256]{3,2,1,0:T(8,128)(2,1)S(1)}, bf16[3,3,128,256]{3,2,1,0:T(8,128)(2,1)}, u32[]{:S(2)}) copy-start(bf16[3,3,128,256]{3,2,1,0:T(8,128)(2,1)} %param.22) | copy-start | bytes 1769476
  0.6 23.9 %copy-start = (bf16[3,3,256,128]{3,2,1,0:T(8,128)(2,1)S(1)}, bf16[3,3,256,128]{3,2,1,0:T(8,128)(2,1)}, u32[]{:S(2)}) copy-start(bf16[3,3,256,128]{3,2,1,0:T(8,128)(2,1)} %param.21) | copy-start | bytes 1769476
  0.7 23.9 %copy-start.3 = (bf16[3,3,128,20]{2,3,1,0:T(8,128)(2,1)S(1)}, bf16[3,3,128,20]{2,3,1,0:T(8,128)(2,1)}, u32[]{:S(2)}) copy-start(bf16[3,3,128,20]{2,3,1,0:T(8,128)(2,1)} %param.20) | copy-start | bytes 138244
  0.7 23.9 %copy-start.4 = (bf16[3,3,128,12]{2,3,1,0:T(8,128)(2,1)S(1)}, bf16[3,3,128,12]{2,3,1,0:T(8,128)(2,1)}, u32[]{:S(2)}) copy-start(bf16[3,3,128,12]{2,3,1,0:T(8,128)(2,1)} %param.17) | copy-start | bytes 82948
  1.4 0.8 copy-start.5
  2.2 0.8 copy-start.6
  2.9 0.7 copy-start.9
  3.6 20.9 %copy-start.7 = (bf16[3,3,4,128]{3,2,1,0:T(4,128)(2,1)S(1)}, bf16[3,3,4,128]{3,2,1,0:T(4,128)(2,1)}, u32[]{:S(2)}) copy-start(bf16[3,3,4,128]{3,2,1,0:T(4,128)(2,1)} %refs_6_.1) | copy-start | bytes 27652
  3.6 20.9 %copy-start.8 = (bf16[3,3,4,128]{3,2,1,0:T(4,128)(2,1)S(1)}, bf16[3,3,4,128]{3,2,1,0:T(4,128)(2,1)}, u32[]{:S(2)}) copy-start(bf16[3,3,4,128]{3,2,1,0:T(4,128)(2,1)} %refs_10_.1) | copy-start | bytes 27652
  4.5 12.2 %all-to-all-start = ((f32[8,2,16,128]{3,2,1,0:T(8,128)}), f32[8,2,16,128]{3,2,1,0:T(8,128)S(1)}, u32[]{:S(2)}, u32[]{:S(2)}) async-start(f32[8,2,16,128]{3,2,1,0:T(8,128)} %pack.1), calls=%async_computation | async-start | bytes 262144 | tf_op jit(solution)/shard_map/all_to_all | solution.py:623
  16.8 7.3 %collective-permute-start.1 = (f32[16,24,128]{2,1,0:T(8,128)S(1)}, f32[16,24,128]{2,1,0:T(8,128)S(1)}, u32[]{:S(2)}, u32[]{:S(2)}) collective-permute-start(f32[16,24,128]{2,1,0:T(8,128)S(1)} %pad_maximum_fusion.1.refs_1_), channel_id=1, source_target_pairs={{0,127},{1,2},{2,1},{3,4},{4,3},{5,6},{6,5},{7,8},{8,7},{9,10},{10... | collective-permute-start | bytes 589832 | tf_op jit(solution)/shard_map/ppermute | solution.py:632
  20.0 4.5 %collective-permute-start = (f32[16,24,128]{2,1,0:T(8,128)S(1)}, f32[16,24,128]{2,1,0:T(8,128)S(1)}, u32[]{:S(2)}, u32[]{:S(2)}) collective-permute-start(f32[16,24,128]{2,1,0:T(8,128)S(1)} %pad_maximum_fusion.1.refs_1_), channel_id=1, source_target_pairs={{0,1},{1,0},{2,3},{3,2},{4,5},{5,4},{6,7},{7,6},{8,9},{9,8},{10,11... | collective-permute-start | bytes 589832 | tf_op jit(solution)/shard_map/ppermute | solution.py:632
  24.6 1.0 %copy-start.2 = (bf16[3,3,128,128]{3,2,1,0:T(8,128)(2,1)S(1)}, bf16[3,3,128,128]{3,2,1,0:T(8,128)(2,1)}, u32[]{:S(2)}) copy-start(bf16[3,3,128,128]{3,2,1,0:T(8,128)(2,1)} %param.18) | copy-start | bytes 884740
  39.9 6.8 %collective-permute-start.2 = (bf16[2560,128]{1,0:T(8,128)(2,1)S(1)}, bf16[2560,128]{1,0:T(8,128)(2,1)S(1)}, u32[]{:S(2)}, u32[]{:S(2)}) collective-permute-start(bf16[2560,128]{1,0:T(8,128)(2,1)S(1)} %get-tuple-element.14), channel_id=1, source_target_pairs={{0,8},{8,0},{1,9},{9,1},{2,10},{10,2},{3,11},{11,3},{4,12},{12,4},... | collective-permute-start | bytes 1966088 | tf_op jit(solution)/shard_map/ppermute | solution.py:632
  85.0 4.7 %collective-permute-start.3 = (bf16[2560,128]{1,0:T(8,128)(2,1)S(1)}, bf16[2560,128]{1,0:T(8,128)(2,1)S(1)}, u32[]{:S(2)}, u32[]{:S(2)}) collective-permute-start(bf16[2560,128]{1,0:T(8,128)(2,1)S(1)} %bitcast.18), channel_id=1, source_target_pairs={{0,8},{8,0},{1,9},{9,1},{2,10},{10,2},{3,11},{11,3},{4,12},{12,4},... | collective-permute-start | bytes 1966088 | tf_op jit(solution)/shard_map/ppermute | solution.py:632

commit v6 on v5

--- a/solution.py
+++ b/solution.py
@@ -37,7 +37,7 @@
 CHUNK = {
     "gather": 8,
     "first": (8, 1),
-    "second": (4, 4),
+    "second": (2, 2),
     "taps": 8,
     "enter": 8,
     "one": (8, 1),
@@ -49,7 +49,7 @@
     "back_three": (8, 1),
     "blocks": 4,
     "back_two": (2, 4),
-    "back_one": (4, 2),
+    "back_one": 4,
 }
 
 
@@ -226,10 +226,14 @@
         den,
         halves,
         w_near,
+        pair_w,
+        low_taps,
         sems,
     ) = scratch
-    for ref in (net, hid, pooled, up_taps, taps, grad_f, grad_c, grad_b):
+    for ref in (net, pooled, up_taps, taps, grad_f, grad_c, grad_b, low_taps):
         zero_edges(ref)
+    hid[0, 0] = jnp.zeros((WIDE, HID1), BF)
+    hid[LOW, 1] = jnp.zeros((WIDE, HID1), BF)
     even = place[1] == 0
     fetch = pltpu.make_async_copy(w_middle, w_near, sems.at[2])
     fetch.start()
@@ -247,19 +251,30 @@
 
     def first(i):
         pre = mm(three_rows(net, n1 * i, n1), first_w)
-        hid[pl.ds(n1 * i + 1, n1)] = jax.nn.silu(pre).astype(BF).reshape(n1, WIDE, HID1)
+        act = jax.nn.silu(pre).astype(BF).reshape(n1 // 2, 2, WIDE, HID1)
+        hid[pl.ds((n1 // 2) * i, n1 // 2), 1] = act[:, 0]
+        hid[pl.ds((n1 // 2) * i + 1, n1 // 2), 0] = act[:, 1]
 
     each(ROWS // n1, first, u1)
     fetch.wait()
-    middle_w = jnp.concatenate([w_near[a] for a in range(3)], axis=1)
-
+    gap = jnp.zeros((HID1, HID1), BF)
+    for b in range(3):
+        taps_b = [w_near[a, b * HID1 : (b + 1) * HID1] for a in range(3)]
+        pair_w[b, 0:HID1] = jnp.concatenate([*taps_b, gap], axis=1)
+        pair_w[b, HID1:] = jnp.concatenate([gap, *taps_b], axis=1)
     n2, u2 = CHUNK["second"]
 
     def second(i):
-        pre = lon_sum(mm_nt(three_rows(hid, n2 * i, n2), middle_w), n2, WIDE, HID1)
-        act_c[pl.ds(n2 * i, n2)] = jax.nn.silu(pre).astype(BF)
-
-    each(ROWS // n2, second, u2)
+        rows = [hid[pl.ds(n2 * i + j // 2, n2), j % 2].reshape(n2 * WIDE, HID1) for j in range(4)]
+        quads = jnp.concatenate(rows, axis=1)
+        parts = [mm_nt(quads, pair_w[b]).reshape(n2, WIDE, 2 * HID1) for b in range(3)]
+        act = jax.nn.silu(ahead(parts[0], 1) + parts[1] + back(parts[2], 1)).astype(BF)
+        for k in range(n2):
+            row = 2 * (n2 * i + k)
+            act_c[row] = act[k, :, :HID1]
+            act_c[row + 1] = act[k, :, HID1:]
+
+    each(LOW // n2, second, u2)
     last_w = stack_outputs(stack_o, w_last)[0:72]
 
     def mean_taps(r):
@@ -438,25 +453,25 @@
         down = mm_tn(grad_b[1 : LOW + 1, :held_low, at : at + HID2].reshape(cells, HID2), low_a)
         for a in range(3):
             keep(far, (a * 3 + b) * HID2, down[:, HID1 * a : HID1 * (a + 1)])
-    n8, u8 = CHUNK["back_one"]
+    spread_w = jnp.concatenate([w_down[a] for a in range(3)], axis=1)
+    wide = mm(grad_b[1 : LOW + 1, :held_low].reshape(cells, 3 * HID2), spread_w)
+    low_taps[1 : LOW + 1] = wide.reshape(LOW, held_low, 3 * HID1)
 
     def back_one(i):
-        total = None
-        for a in range(3):
-            cot = grad_b[pl.ds(n8 * i + 2 - a, n8)].reshape(n8 * WLOW, 3 * HID2)
-            part = mm(cot, w_down[a])
-            total = part if total is None else total + part
-        low = (0.25 * total).reshape(n8, WLOW, HID1)
-        for k in range(n8):
-            row = n8 * i + k
-            phases[row, pl.ds(0, WLOW, stride=2)] = low[k]
-            phases[row, pl.ds(1, WLOW, stride=2)] = low[k]
-            spread = phases[row, 0:OWN]
-            for pi in range(2):
-                r = 2 * row + pi
-                grad_a[r] = ((back_c[r, 0:OWN] + spread) * slope_a[r, 0:OWN]).astype(BF)
-
-    each(LOW // n8, back_one, u8)
+        low = (
+            low_taps[i + 2, :, 0:HID1]
+            + low_taps[i + 1, :, HID1 : 2 * HID1]
+            + low_taps[i, :, 2 * HID1 :]
+        )
+        low = 0.25 * low
+        phases[i, pl.ds(0, held_low, stride=2)] = low
+        phases[i, pl.ds(1, held_low, stride=2)] = low
+        spread = phases[i, 0:OWN]
+        for pi in range(2):
+            r = 2 * i + pi
+            grad_a[r] = ((back_c[r, 0:OWN] + spread) * slope_a[r, 0:OWN]).astype(BF)
+
+    each(LOW, back_one, CHUNK["back_one"])
     near_cells = jnp.concatenate(
         [net[a : a + ROWS, :OWN].reshape(ROWS * OWN, OWN) for a in range(3)], axis=1
     )
@@ -542,7 +557,6 @@
             pltpu.VMEM(land_mask.shape, jnp.int32),
             pltpu.SemaphoreType.DMA((3,)),
         ],
-        compiler_params=pltpu.CompilerParams(vmem_limit_bytes=8 * 2**20),
         name="pack",
     )(level_index, target, noise, land_mask)
 
@@ -565,7 +579,7 @@
             pltpu.VMEM((OWN, OWN), F32),
             pltpu.VMEM((ROWS, FIELDS, LANES), F32),
             pltpu.VMEM((ROWS + 2, WIDE, OWN), BF),
-            pltpu.VMEM((ROWS + 2, WIDE, HID1), BF),
+            pltpu.VMEM((LOW + 1, 2, WIDE, HID1), BF),
             pltpu.VMEM((ROWS, WIDE, HID1), BF),
             pltpu.VMEM((ROWS + 2, 72, LANES), F32),
             pltpu.VMEM((ROWS, 8, LANES), F32),
@@ -590,6 +604,8 @@
             pltpu.VMEM((LOW, CELL_ROWS, OWN), F32),
             pltpu.VMEM((2, HALF_ROWS, OWN), BF),
             pltpu.VMEM((3, 3 * HID1, HID1), BF),
+            pltpu.VMEM((3, 2 * HID1, 4 * HID1), BF),
+            pltpu.VMEM((LOW + 2, OWN // 2, 3 * HID1), F32),
             pltpu.SemaphoreType.DMA((3,)),
         ],
         compiler_params=pltpu.CompilerParams(vmem_limit_bytes=44 * 2**20),
@@ -660,7 +676,7 @@
         pair,
         across,
         frozen_first.transpose(0, 1, 3, 2),
-        frozen_middle.reshape(3, 3 * HID1, HID1),
+        pltpu.with_memory_space_constraint(frozen_middle.reshape(3, 3 * HID1, HID1), pltpu.HBM),
         frozen_last,
         diffuse_in.transpose(0, 1, 3, 2),
         diffuse_down.reshape(3, 3 * HID2, HID1),

time: 92.4 us -> 89.7 us (0.971)
  local copies, waits for them, and re-layouts: 4.15 us -> 0.99 us
    unnamed x20 -> x12, local copies, waits for them, and re-layouts: 3.19 us -> 0.03 us
where the time goes in v6:
time: 89.7 us; the launch traced here: 89.4 us
  blocking collectives  37.9 us (42%)
  Pallas kernels  18 us (20%)
  starting transfers between devices  18 us (20%)
  waiting for transfers between devices  12.5 us (14%)
  between operations  1.52 us (2%)
  local copies, waits for them, and re-layouts  0.99 us (1%)
    all_to_all x2, blocking collectives, all_to_all(): return lax.all_to_all(value, axes, split_axis=0, concat_axis=0, tiled=True)  37.9 us
    pallas_call x1, Pallas kernels, step(): pl.pallas_call(kernel, out_shape=(jax.ShapeDtypeStruct((HALF_ROWS, OWN),...  14.4 us
    ppermute x4, starting transfers between devices, swap(): return lax.ppermute(value, axes, sorted(set(pairs)))  11.2 us
    ppermute x4, waiting for transfers between devices, swap(): return lax.ppermute(value, axes, sorted(set(pairs)))  7.84 us
    all_to_all x1, starting transfers between devices, all_to_all(): return lax.all_to_all(value, axes, split_axis=0, concat_axis=0, tiled=True)  6.79 us
    all_to_all x1, waiting for transfers between devices, all_to_all(): return lax.all_to_all(value, axes, split_axis=0, concat_axis=0, tiled=True)  4.63 us
    pallas_call x1, Pallas kernels, unpack(): pl.pallas_call(unpack_kernel, out_shape=tuple((jax.ShapeDtypeStruct(shape...  2.11 us
  transfers between devices with their start and end apart: 5, of which 5 were waited for; matrix products, arithmetic and copies ran while one was open for 1% of the time, Pallas kernels for 0%

profile of v6, /device:TPU:1, one launch (start us, length us, event | category | flops | bytes accessed | tf_op | source)
XLA Modules:
  0.0 89.4 jit_solution(576584890935714238)
XLA Ops:
  0.6 0.0 copy-start.5
  0.6 0.0 copy-start.1
  0.7 0.0 copy-start
  0.7 0.0 copy-start.2
  0.7 0.0 copy-start.4
  0.7 0.0 copy-start.3
  1.4 1.5 %pack.1 = f32[8,2,16,128]{3,2,1,0:T(8,128)} custom-call(s32[1,1]{1,0:T(1,128)S(6)} %copy.21.level, f32[4,2,1024]{2,1,0:T(2,128)} %target_far.1, f32[4,2,1024]{2,1,0:T(2,128)} %noise_far.1, s32[2,1024]{1,0:T(2,128)} %mask_far.1), custom_call_target="tpu_custom_call" | custom-call | tf_op jit(solution)/shard_map/pack/pallas_call | solution.py:549
  3.0 6.8 %all-to-all-start = ((f32[8,2,16,128]{3,2,1,0:T(8,128)}), f32[8,2,16,128]{3,2,1,0:T(8,128)S(1)}, u32[]{:S(2)}, u32[]{:S(2)}) async-start(f32[8,2,16,128]{3,2,1,0:T(8,128)} %pack.1), calls=%async_computation | async-start | bytes 262144 | tf_op jit(solution)/shard_map/all_to_all | solution.py:639
  9.7 0.8 copy.20
  10.6 4.6 %all-to-all-done = f32[8,2,16,128]{3,2,1,0:T(8,128)S(1)} async-done(((f32[8,2,16,128]{3,2,1,0:T(8,128)}), f32[8,2,16,128]{3,2,1,0:T(8,128)S(1)}, u32[]{:S(2)}, u32[]{:S(2)}) %all-to-all-start) | async-done | bytes 131104 | tf_op jit(solution)/shard_map/all_to_all | solution.py:639
  15.3 3.2 %collective-permute-start.1 = (f32[16,24,128]{2,1,0:T(8,128)S(1)}, f32[16,24,128]{2,1,0:T(8,128)S(1)}, u32[]{:S(2)}, u32[]{:S(2)}) collective-permute-start(f32[16,24,128]{2,1,0:T(8,128)S(1)} %pad_maximum_fusion.1.refs_1_), channel_id=1, source_target_pairs={{0,127},{1,2},{2,1},{3,4},{4,3},{5,6},{6,5},{7,8},{8,7},{9,10},{10... | collective-permute-start | bytes 589832 | tf_op jit(solution)/shard_map/ppermute | solution.py:648
  18.5 0.0 collective-permute-start
  18.5 0.1 pad_add_fusion.refs_0_.place
  18.6 4.0 %collective-permute-done.1.refs_3_ = f32[16,24,128]{2,1,0:T(8,128)S(1)} collective-permute-done((f32[16,24,128]{2,1,0:T(8,128)S(1)}, f32[16,24,128]{2,1,0:T(8,128)S(1)}, u32[]{:S(2)}, u32[]{:S(2)}) %collective-permute-start.1) | collective-permute-done | bytes 196640 | tf_op jit(solution)/shard_map/ppermute | solution.py:648
  22.5 0.5 collective-permute-done.refs_2_
  23.0 0.0 copy-done.5
  23.0 0.0 copy-done.1
  23.0 0.0 copy-done
  23.0 0.0 copy-done.2
  23.0 0.0 copy-done.4
  23.0 14.4 %step.1 = (bf16[2560,128]{1,0:T(8,128)(2,1)S(1)}, bf16[2560,128]{1,0:T(8,128)(2,1)S(1)}, bf16[8,8,128]{2,1,0:T(8,128)(2,1)S(1)}) custom-call(s32[2]{0:T(128)S(1)} %pad_add_fusion.refs_0_.place, f32[16,24,128]{2,1,0:T(8,128)S(1)} %pad_maximum_fusion.1.refs_1_, f32[16,24,128]{2,1,0:T(8,128)S(1)} %collective-permute-done.refs_2_, ...), custom_call_target="tpu_custom_call" | custom-call | tf_op jit(solution)/shard_map/step/pallas_call | solution.py:568
  37.4 5.0 %collective-permute-start.2 = (bf16[2560,128]{1,0:T(8,128)(2,1)S(1)}, bf16[2560,128]{1,0:T(8,128)(2,1)S(1)}, u32[]{:S(2)}, u32[]{:S(2)}) collective-permute-start(bf16[2560,128]{1,0:T(8,128)(2,1)S(1)} %get-tuple-element.14), channel_id=1, source_target_pairs={{0,8},{8,0},{1,9},{9,1},{2,10},{10,2},{3,11},{11,3},{4,12},{12,4},... | collective-permute-start | bytes 1966088 | tf_op jit(solution)/shard_map/ppermute | solution.py:648
  42.4 1.7 %collective-permute-done.2 = bf16[2560,128]{1,0:T(8,128)(2,1)S(1)} collective-permute-done((bf16[2560,128]{1,0:T(8,128)(2,1)S(1)}, bf16[2560,128]{1,0:T(8,128)(2,1)S(1)}, u32[]{:S(2)}, u32[]{:S(2)}) %collective-permute-start.2) | collective-permute-done | bytes 655392 | tf_op jit(solution)/shard_map/ppermute | solution.py:648
  44.2 0.2 add_convert_fusion
  44.4 0.1 pad_maximum_fusion
  44.5 20.8 %all_to_all.15 = bf16[64,48,128]{2,1,0:T(8,128)(2,1)S(1)} all-to-all(bf16[64,48,128]{2,1,0:T(8,128)(2,1)S(1)} %pad_maximum_fusion), channel_id=1, replica_groups=mesh['y'=4,'x_hi'=2,'core'=2,'x_lo'=2,'z'=4] {'y','x_hi','x_lo','z'}, dimensions={0} | all-to-all | bytes 1572864 | tf_op jit(solution)/shard_map/all_to_all | solution.py:639
  65.2 0.1 slice_reduce_fusion
  65.3 0.1 broadcast_in_dim.5
  65.4 17.1 %all_to_all.16 = bf16[64,40,128]{2,1,0:T(8,128)(2,1)S(1)} all-to-all(bf16[64,40,128]{2,1,0:T(8,128)(2,1)S(1)} %broadcast_in_dim.5), channel_id=1, replica_groups=mesh['y'=4,'x_hi'=2,'core'=2,'x_lo'=2,'z'=4] {'y','x_hi','x_lo','z'}, dimensions={0} | all-to-all | bytes 1310720 | tf_op jit(solution)/shard_map/spread/all_to_all | solution.py:639
  82.6 3.0 %collective-permute-start.3 = (bf16[2560,128]{1,0:T(8,128)(2,1)S(1)}, bf16[2560,128]{1,0:T(8,128)(2,1)S(1)}, u32[]{:S(2)}, u32[]{:S(2)}) collective-permute-start(bf16[2560,128]{1,0:T(8,128)(2,1)S(1)} %bitcast.18), channel_id=1, source_target_pairs={{0,8},{8,0},{1,9},{9,1},{2,10},{10,2},{3,11},{11,3},{4,12},{12,4},... | collective-permute-start | bytes 1966088 | tf_op jit(solution)/shard_map/ppermute | solution.py:648
  85.6 1.7 %collective-permute-done.3.other = bf16[2560,128]{1,0:T(8,128)(2,1)S(1)} collective-permute-done((bf16[2560,128]{1,0:T(8,128)(2,1)S(1)}, bf16[2560,128]{1,0:T(8,128)(2,1)S(1)}, u32[]{:S(2)}, u32[]{:S(2)}) %collective-permute-start.3) | collective-permute-done | bytes 655392 | tf_op jit(solution)/shard_map/ppermute | solution.py:648
  87.2 2.1 %unpack.1 = (f32[4,2,1024]{2,1,0:T(2,128)}, f32[3,3,20,128]{3,2,1,0:T(8,128)}, f32[3,3,256,128]{3,2,1,0:T(8,128)}, f32[3,3,128,256]{3,2,1,0:T(8,128)}, f32[3,3,4,128]{3,2,1,0:T(4,128)}) custom-call(s32[2]{0:T(128)S(1)} %pad_add_fusion.refs_0_.place, bf16[2560,128]{1,0:T(8,128)(2,1)S(1)} %bitcast.19, bf16[2560,128]{1,0:T(8,128)(2,1)S(1)} %collective-permute-done.3.other, ...), custom_call_target="tpu_custom_call" | custom-call | tf_op jit(solution)/shard_map/unpack/pallas_call | solution.py:624
  (7 shorter events, 0.1 us)
Async XLA Ops:
  0.6 22.4 %copy-start.5 = (bf16[3,3,4,128]{3,2,1,0:T(4,128)(2,1)S(1)}, bf16[3,3,4,128]{3,2,1,0:T(4,128)(2,1)}, u32[]{:S(2)}) copy-start(bf16[3,3,4,128]{3,2,1,0:T(4,128)(2,1)} %refs_10_.1) | copy-start | bytes 27652
  0.6 22.4 %copy-start.1 = (bf16[3,3,128,256]{3,2,1,0:T(8,128)(2,1)S(1)}, bf16[3,3,128,256]{3,2,1,0:T(8,128)(2,1)}, u32[]{:S(2)}) copy-start(bf16[3,3,128,256]{3,2,1,0:T(8,128)(2,1)} %param.22) | copy-start | bytes 1769476
  0.7 22.4 %copy-start = (bf16[3,3,256,128]{3,2,1,0:T(8,128)(2,1)S(1)}, bf16[3,3,256,128]{3,2,1,0:T(8,128)(2,1)}, u32[]{:S(2)}) copy-start(bf16[3,3,256,128]{3,2,1,0:T(8,128)(2,1)} %param.21) | copy-start | bytes 1769476
  0.7 22.4 %copy-start.2 = (bf16[3,3,128,20]{2,3,1,0:T(8,128)(2,1)S(1)}, bf16[3,3,128,20]{2,3,1,0:T(8,128)(2,1)}, u32[]{:S(2)}) copy-start(bf16[3,3,128,20]{2,3,1,0:T(8,128)(2,1)} %param.20) | copy-start | bytes 138244
  0.7 22.4 %copy-start.4 = (bf16[3,3,4,128]{3,2,1,0:T(4,128)(2,1)S(1)}, bf16[3,3,4,128]{3,2,1,0:T(4,128)(2,1)}, u32[]{:S(2)}) copy-start(bf16[3,3,4,128]{3,2,1,0:T(4,128)(2,1)} %refs_6_.1) | copy-start | bytes 27652
  0.7 22.4 %copy-start.3 = (bf16[3,3,128,12]{2,3,1,0:T(8,128)(2,1)S(1)}, bf16[3,3,128,12]{2,3,1,0:T(8,128)(2,1)}, u32[]{:S(2)}) copy-start(bf16[3,3,128,12]{2,3,1,0:T(8,128)(2,1)} %param.17) | copy-start | bytes 82948
  3.0 12.2 %all-to-all-start = ((f32[8,2,16,128]{3,2,1,0:T(8,128)}), f32[8,2,16,128]{3,2,1,0:T(8,128)S(1)}, u32[]{:S(2)}, u32[]{:S(2)}) async-start(f32[8,2,16,128]{3,2,1,0:T(8,128)} %pack.1), calls=%async_computation | async-start | bytes 262144 | tf_op jit(solution)/shard_map/all_to_all | solution.py:639
  15.3 7.3 %collective-permute-start.1 = (f32[16,24,128]{2,1,0:T(8,128)S(1)}, f32[16,24,128]{2,1,0:T(8,128)S(1)}, u32[]{:S(2)}, u32[]{:S(2)}) collective-permute-start(f32[16,24,128]{2,1,0:T(8,128)S(1)} %pad_maximum_fusion.1.refs_1_), channel_id=1, source_target_pairs={{0,127},{1,2},{2,1},{3,4},{4,3},{5,6},{6,5},{7,8},{8,7},{9,10},{10... | collective-permute-start | bytes 589832 | tf_op jit(solution)/shard_map/ppermute | solution.py:648
  18.5 4.5 %collective-permute-start = (f32[16,24,128]{2,1,0:T(8,128)S(1)}, f32[16,24,128]{2,1,0:T(8,128)S(1)}, u32[]{:S(2)}, u32[]{:S(2)}) collective-permute-start(f32[16,24,128]{2,1,0:T(8,128)S(1)} %pad_maximum_fusion.1.refs_1_), channel_id=1, source_target_pairs={{0,1},{1,0},{2,3},{3,2},{4,5},{5,4},{6,7},{7,6},{8,9},{9,8},{10,11... | collective-permute-start | bytes 589832 | tf_op jit(solution)/shard_map/ppermute | solution.py:648
  37.4 6.8 %collective-permute-start.2 = (bf16[2560,128]{1,0:T(8,128)(2,1)S(1)}, bf16[2560,128]{1,0:T(8,128)(2,1)S(1)}, u32[]{:S(2)}, u32[]{:S(2)}) collective-permute-start(bf16[2560,128]{1,0:T(8,128)(2,1)S(1)} %get-tuple-element.14), channel_id=1, source_target_pairs={{0,8},{8,0},{1,9},{9,1},{2,10},{10,2},{3,11},{11,3},{4,12},{12,4},... | collective-permute-start | bytes 1966088 | tf_op jit(solution)/shard_map/ppermute | solution.py:648
  82.6 4.7 %collective-permute-start.3 = (bf16[2560,128]{1,0:T(8,128)(2,1)S(1)}, bf16[2560,128]{1,0:T(8,128)(2,1)S(1)}, u32[]{:S(2)}, u32[]{:S(2)}) collective-permute-start(bf16[2560,128]{1,0:T(8,128)(2,1)S(1)} %bitcast.18), channel_id=1, source_target_pairs={{0,8},{8,0},{1,9},{9,1},{2,10},{10,2},{3,11},{11,3},{4,12},{12,4},... | collective-permute-start | bytes 1966088 | tf_op jit(solution)/shard_map/ppermute | solution.py:648

commit v7 on v6

--- a/solution.py
+++ b/solution.py
@@ -178,8 +178,7 @@
     return ref[...].astype(BF)
 
 
-def step_kernel(
-    scale,
+def regression_kernel(
     place,
     own,
     pair,
@@ -187,6 +186,83 @@
     w_first,
     w_middle,
     w_last,
+    mean,
+    coarse,
+    stack,
+    stack_o,
+    net,
+    hid,
+    sec,
+    taps,
+    w_near,
+    pair_w,
+    sem,
+):
+    zero_edges(net)
+    zero_edges(taps)
+    hid[0, 0] = jnp.zeros((WIDE, HID1), BF)
+    hid[LOW, 1] = jnp.zeros((WIDE, HID1), BF)
+    even = place[1] == 0
+    fetch = pltpu.make_async_copy(w_middle, w_near, sem)
+    fetch.start()
+    first_w = stack_inputs(stack, w_first, 16)
+
+    def gather(r):
+        near, far = pair[r], across[r]
+        wide = with_halo(own[r], jnp.where(even, far, near), jnp.where(even, near, far))
+        coarse[r] = wide
+        net[r + 1] = to_cells(lon_shifts(wide))
+
+    each(ROWS, gather, CHUNK["gather"])
+
+    n1, u1 = CHUNK["first"]
+
+    def first(i):
+        pre = mm(three_rows(net, n1 * i, n1), first_w)
+        act = jax.nn.silu(pre).astype(BF).reshape(n1 // 2, 2, WIDE, HID1)
+        hid[pl.ds((n1 // 2) * i, n1 // 2), 1] = act[:, 0]
+        hid[pl.ds((n1 // 2) * i + 1, n1 // 2), 0] = act[:, 1]
+
+    each(ROWS // n1, first, u1)
+    fetch.wait()
+    gap = jnp.zeros((HID1, HID1), BF)
+    for b in range(3):
+        taps_b = [w_near[a, b * HID1 : (b + 1) * HID1] for a in range(3)]
+        pair_w[b, 0:HID1] = jnp.concatenate([*taps_b, gap], axis=1)
+        pair_w[b, HID1:] = jnp.concatenate([gap, *taps_b], axis=1)
+    n2, u2 = CHUNK["second"]
+
+    def second(i):
+        rows = [hid[pl.ds(n2 * i + j // 2, n2), j % 2].reshape(n2 * WIDE, HID1) for j in range(4)]
+        quads = jnp.concatenate(rows, axis=1)
+        parts = [mm_nt(quads, pair_w[b]).reshape(n2, WIDE, 2 * HID1) for b in range(3)]
+        act = jax.nn.silu(ahead(parts[0], 1) + parts[1] + back(parts[2], 1)).astype(BF)
+        for k in range(n2):
+            row = 2 * (n2 * i + k)
+            sec[row] = act[k, :, :HID1]
+            sec[row + 1] = act[k, :, HID1:]
+
+    each(LOW // n2, second, u2)
+    last_w = stack_outputs(stack_o, w_last)[0:72]
+
+    def mean_taps(r):
+        taps[r + 1] = mm_nt(last_w, to_lanes(sec[r]))
+
+    each(ROWS, mean_taps, CHUNK["taps"])
+    def collect(r):
+        mean[r] = four_channels(taps, r).astype(BF).astype(F32)
+
+    each(ROWS, collect, CHUNK["taps"])
+
+
+def step_kernel(
+    scale,
+    place,
+    own,
+    pair,
+    across,
+    mean,
+    coarse,
     w_in,
     w_down,
     w_up,
@@ -201,7 +277,6 @@
         stack_o,
         field,
         net,
-        hid,
         act_c,
         taps,
         residuals,
@@ -225,78 +300,31 @@
         last_sum,
         den,
         halves,
-        w_near,
-        pair_w,
         low_taps,
         sems,
     ) = scratch
     for ref in (net, pooled, up_taps, taps, grad_f, grad_c, grad_b, low_taps):
         zero_edges(ref)
-    hid[0, 0] = jnp.zeros((WIDE, HID1), BF)
-    hid[LOW, 1] = jnp.zeros((WIDE, HID1), BF)
     even = place[1] == 0
-    fetch = pltpu.make_async_copy(w_middle, w_near, sems.at[2])
-    fetch.start()
-    first_w = stack_inputs(stack, w_first, 16)
-
-    def gather(r):
-        near, far = pair[r], across[r]
-        wide = with_halo(own[r], jnp.where(even, far, near), jnp.where(even, near, far))
-        field[r] = wide
-        net[r + 1] = to_cells(lon_shifts(wide[8:24]))
-
-    each(ROWS, gather, CHUNK["gather"])
-
-    n1, u1 = CHUNK["first"]
-
-    def first(i):
-        pre = mm(three_rows(net, n1 * i, n1), first_w)
-        act = jax.nn.silu(pre).astype(BF).reshape(n1 // 2, 2, WIDE, HID1)
-        hid[pl.ds((n1 // 2) * i, n1 // 2), 1] = act[:, 0]
-        hid[pl.ds((n1 // 2) * i + 1, n1 // 2), 0] = act[:, 1]
-
-    each(ROWS // n1, first, u1)
-    fetch.wait()
-    gap = jnp.zeros((HID1, HID1), BF)
-    for b in range(3):
-        taps_b = [w_near[a, b * HID1 : (b + 1) * HID1] for a in range(3)]
-        pair_w[b, 0:HID1] = jnp.concatenate([*taps_b, gap], axis=1)
-        pair_w[b, HID1:] = jnp.concatenate([gap, *taps_b], axis=1)
-    n2, u2 = CHUNK["second"]
-
-    def second(i):
-        rows = [hid[pl.ds(n2 * i + j // 2, n2), j % 2].reshape(n2 * WIDE, HID1) for j in range(4)]
-        quads = jnp.concatenate(rows, axis=1)
-        parts = [mm_nt(quads, pair_w[b]).reshape(n2, WIDE, 2 * HID1) for b in range(3)]
-        act = jax.nn.silu(ahead(parts[0], 1) + parts[1] + back(parts[2], 1)).astype(BF)
-        for k in range(n2):
-            row = 2 * (n2 * i + k)
-            act_c[row] = act[k, :, :HID1]
-            act_c[row + 1] = act[k, :, HID1:]
-
-    each(LOW // n2, second, u2)
-    last_w = stack_outputs(stack_o, w_last)[0:72]
-
-    def mean_taps(r):
-        taps[r + 1] = mm_nt(last_w, to_lanes(act_c[r]))
-
-    each(ROWS, mean_taps, CHUNK["taps"])
     in_w = stack_inputs(stack, w_in, FIELDS)
     lane = lax.broadcasted_iota(jnp.int32, (8, LANES), 1)
     held = (lane < OWN + HALO) | (lane >= LANES - HALO)
     low_half = lax.broadcasted_iota(jnp.int32, (8, LANES), 0) < 4
 
     def enter(r):
-        mean_r = four_channels(taps, r).astype(BF).astype(F32)
-        sigma = jnp.where(held, jnp.broadcast_to(field[r, 1:2], (8, LANES)), 1.0)
-        residual = field[r, 0:8] - mean_r
-        noisy = residual + sigma * field[r, 16:24]
+        near, far = pair[r], across[r]
+        wide = with_halo(own[r], jnp.where(even, far, near), jnp.where(even, near, far))
+        field[r] = wide[0:8]
+        mean_r = mean[r]
+        sigma = jnp.where(held, jnp.broadcast_to(wide[1:2], (8, LANES)), 1.0)
+        residual = wide[0:8] - mean_r
+        noisy = residual + sigma * wide[8:16]
         variance = sigma * sigma + 0.25
         residuals[r] = residual
         noisies[r] = noisy
         scaled = (lax.rsqrt(variance) * noisy).astype(BF).astype(F32)
         both = jnp.where(low_half, pltpu.roll(mean_r, 4, 0), scaled)
-        net[r + 1] = to_cells(lon_shifts(jnp.concatenate([both, field[r, 8:24]], axis=0)))
+        net[r + 1] = to_cells(lon_shifts(jnp.concatenate([both, coarse[r]], axis=0)))
 
     each(ROWS, enter, CHUNK["enter"])
 
@@ -561,6 +589,32 @@
     )(level_index, target, noise, land_mask)
 
 
+def regress(*operands):
+    return pl.pallas_call(
+        regression_kernel,
+        out_shape=(
+            jax.ShapeDtypeStruct((ROWS, 8, LANES), F32),
+            jax.ShapeDtypeStruct((ROWS, 16, LANES), F32),
+        ),
+        in_specs=[in_smem(), *in_vmem(4), *in_hbm(1), *in_vmem(1)],
+        out_specs=tuple(in_vmem(2)),
+        scratch_shapes=[
+            pltpu.VMEM((3, OWN, OWN), F32),
+            pltpu.VMEM((OWN, OWN), F32),
+            pltpu.VMEM((ROWS + 2, WIDE, OWN), BF),
+            pltpu.VMEM((LOW + 1, 2, WIDE, HID1), BF),
+            pltpu.VMEM((ROWS, WIDE, HID1), BF),
+            pltpu.VMEM((ROWS + 2, 72, LANES), F32),
+            pltpu.VMEM((3, 3 * HID1, HID1), BF),
+            pltpu.VMEM((3, 2 * HID1, 4 * HID1), BF),
+            pltpu.SemaphoreType.DMA(()),
+        ],
+        compiler_params=pltpu.CompilerParams(vmem_limit_bytes=20 * 2**20),
+        cost_estimate=pl.CostEstimate(flops=2 * 10**9, transcendentals=10**6, bytes_accessed=2 * 10**6),
+        name="regress",
+    )(*operands)
+
+
 def step(scale, *operands):
     def kernel(*refs):
         step_kernel(scale, *refs)
@@ -572,14 +626,13 @@
             jax.ShapeDtypeStruct((HALF_ROWS, OWN), BF),
             jax.ShapeDtypeStruct((LOW, CELL_ROWS, OWN), BF),
         ),
-        in_specs=[in_smem(), *in_vmem(4), *in_hbm(1), *in_vmem(5)],
+        in_specs=[in_smem(), *in_vmem(9)],
         out_specs=tuple(in_vmem(3)),
         scratch_shapes=[
             pltpu.VMEM((3, OWN, OWN), F32),
             pltpu.VMEM((OWN, OWN), F32),
-            pltpu.VMEM((ROWS, FIELDS, LANES), F32),
+            pltpu.VMEM((ROWS, 8, LANES), F32),
             pltpu.VMEM((ROWS + 2, WIDE, OWN), BF),
-            pltpu.VMEM((LOW + 1, 2, WIDE, HID1), BF),
             pltpu.VMEM((ROWS, WIDE, HID1), BF),
             pltpu.VMEM((ROWS + 2, 72, LANES), F32),
             pltpu.VMEM((ROWS, 8, LANES), F32),
@@ -603,10 +656,8 @@
             pltpu.VMEM((80, HID1), F32),
             pltpu.VMEM((LOW, CELL_ROWS, OWN), F32),
             pltpu.VMEM((2, HALF_ROWS, OWN), BF),
-            pltpu.VMEM((3, 3 * HID1, HID1), BF),
-            pltpu.VMEM((3, 2 * HID1, 4 * HID1), BF),
             pltpu.VMEM((LOW + 2, OWN // 2, 3 * HID1), F32),
-            pltpu.SemaphoreType.DMA((3,)),
+            pltpu.SemaphoreType.DMA((2,)),
         ],
         compiler_params=pltpu.CompilerParams(vmem_limit_bytes=44 * 2**20),
         name="step",
@@ -639,6 +690,10 @@
     return lax.all_to_all(value, axes, split_axis=0, concat_axis=0, tiled=True)
 
 
+def in_place(value):
+    return pltpu.with_memory_space_constraint(value, pltpu.HBM)
+
+
 def swap(value, axes, offset):
     count = lax.axis_size(axes)
     pairs = []
@@ -666,18 +721,28 @@
     place = jnp.stack([lax.axis_index("core"), lax.axis_index("z") % 2])
     place = place.astype(jnp.int32)
     packed = all_to_all(pack(target, noise, land_mask, level_index), LAT).reshape(ROWS, 16, OWN)
-    fields = jnp.concatenate([packed[:, :8], coarse.transpose(1, 0, 2).astype(F32), packed[:, 12:]], axis=1)
-    across = swap(fields, STRIPS, 1)
-    pair = swap(fields, STRIPS, 0)
+    strip = jnp.pad(coarse.transpose(1, 0, 2).astype(F32), ((0, 0), (0, 4), (0, 0)))
+    strip_across = swap(strip, STRIPS, 1)
+    strip_pair = swap(strip, STRIPS, 0)
+    across = swap(packed, STRIPS, 1)
+    pair = swap(packed, STRIPS, 0)
+    mean, coarse_wide = regress(
+        place,
+        strip,
+        strip_pair,
+        strip_across,
+        in_place(frozen_first.transpose(0, 1, 3, 2)),
+        in_place(frozen_middle.reshape(3, 3 * HID1, HID1)),
+        in_place(frozen_last),
+    )
     grads, partner, tiles = step(
         scale,
         place,
-        fields,
+        packed,
         pair,
         across,
-        frozen_first.transpose(0, 1, 3, 2),
-        pltpu.with_memory_space_constraint(frozen_middle.reshape(3, 3 * HID1, HID1), pltpu.HBM),
-        frozen_last,
+        mean,
+        coarse_wide,
         diffuse_in.transpose(0, 1, 3, 2),
         diffuse_down.reshape(3, 3 * HID2, HID1),
         diffuse_up.reshape(9 * HID1, HID2),

time: 89.7 us -> 90.6 us (1.010)
  starting transfers between devices: 18 us -> 21.6 us
  waiting for transfers between devices: 12.5 us -> 9.34 us
    ppermute x4 -> x6, starting transfers between devices: 11.2 us -> 18.2 us  [swap(): return lax.ppermute(value, axes, sorted(set(pairs)))]
    pallas_call x0 -> x1, Pallas kernels: none -> 4.74 us  [regress(): pl.pallas_call(regression_kernel, out_shape=(jax.ShapeDtypeStruct((ROWS,...]
    pallas_call x1, Pallas kernels: 14.4 us -> 10.3 us  [step(): pl.pallas_call(kernel, out_shape=(jax.ShapeDtypeStruct((HALF_ROWS, OWN),...]
    ppermute x4 -> x6, waiting for transfers between devices: 7.84 us -> 4.06 us  [swap(): return lax.ppermute(value, axes, sorted(set(pairs)))]
    all_to_all x1, starting transfers between devices: 6.79 us -> 3.38 us  [all_to_all(): return lax.all_to_all(value, axes, split_axis=0, concat_axis=0, tiled=True)]
  transfers between devices with their start and end apart: 5 -> 7, of which waited for: 5 -> 4; matrix products, arithmetic and copies ran while one was open for 1% -> 0% of each run, Pallas kernels for 0% -> 7%
where the time goes in v7:
time: 90.6 us; the launch traced here: 90.2 us
  blocking collectives  37.7 us (42%)
  starting transfers between devices  21.6 us (24%)
  Pallas kernels  18.6 us (21%)
  waiting for transfers between devices  9.34 us (10%)
  between operations  1.43 us (2%)
  local copies, waits for them, and re-layouts  0.98 us (1%)
    all_to_all x2, blocking collectives, all_to_all(): return lax.all_to_all(value, axes, split_axis=0, concat_axis=0, tiled=True)  37.7 us
    ppermute x6, starting transfers between devices, swap(): return lax.ppermute(value, axes, sorted(set(pairs)))  18.2 us
    pallas_call x1, Pallas kernels, step(): pl.pallas_call(kernel, out_shape=(jax.ShapeDtypeStruct((HALF_ROWS, OWN),...  10.3 us
    all_to_all x1, waiting for transfers between devices, all_to_all(): return lax.all_to_all(value, axes, split_axis=0, concat_axis=0, tiled=True)  5.28 us
    pallas_call x1, Pallas kernels, regress(): pl.pallas_call(regression_kernel, out_shape=(jax.ShapeDtypeStruct((ROWS,...  4.74 us
    ppermute x6, waiting for transfers between devices, swap(): return lax.ppermute(value, axes, sorted(set(pairs)))  4.06 us
    all_to_all x1, starting transfers between devices, all_to_all(): return lax.all_to_all(value, axes, split_axis=0, concat_axis=0, tiled=True)  3.38 us
    pallas_call x1, Pallas kernels, unpack(): pl.pallas_call(unpack_kernel, out_shape=tuple((jax.ShapeDtypeStruct(shape...  2.11 us
  transfers between devices with their start and end apart: 7, of which 4 were waited for; matrix products, arithmetic and copies ran while one was open for 0% of the time, Pallas kernels for 7%

profile of v7, /device:TPU:1, one launch (start us, length us, event | category | flops | bytes accessed | tf_op | source)
XLA Modules:
  0.0 90.2 jit_solution(7992567225154427786)
XLA Ops:
  0.6 0.8 copy.19
  1.5 6.1 %collective-permute-start.3 = (f32[16,16,128]{2,1,0:T(8,128)S(1)}, f32[16,16,128]{2,1,0:T(8,128)S(1)}, u32[]{:S(2)}, u32[]{:S(2)}) collective-permute-start(f32[16,16,128]{2,1,0:T(8,128)S(1)} %pad_convert_fusion.own), channel_id=1, source_target_pairs={{0,127},{1,2},{2,1},{3,4},{4,3},{5,6},{6,5},{7,8},{8,7},{9,10},{10... | collective-permute-start | bytes 393224 | tf_op jit(solution)/shard_map/ppermute | solution.py:703
  7.6 0.0 collective-permute-start.2
  8.3 1.5 %pack.1 = f32[8,2,16,128]{3,2,1,0:T(8,128)} custom-call(s32[1,1]{1,0:T(1,128)S(6)} %copy.20.level, f32[4,2,1024]{2,1,0:T(2,128)} %target_far.1, f32[4,2,1024]{2,1,0:T(2,128)} %noise_far.1, s32[2,1024]{1,0:T(2,128)} %mask_far.1), custom_call_target="tpu_custom_call" | custom-call | tf_op jit(solution)/shard_map/pack/pallas_call | solution.py:577
  9.8 3.4 %all-to-all-start = ((f32[8,2,16,128]{3,2,1,0:T(8,128)}), f32[8,2,16,128]{3,2,1,0:T(8,128)S(1)}, u32[]{:S(2)}, u32[]{:S(2)}) async-start(f32[8,2,16,128]{3,2,1,0:T(8,128)} %pack.1), calls=%async_computation | async-start | bytes 262144 | tf_op jit(solution)/shard_map/all_to_all | solution.py:690
  13.2 0.1 pad_add_fusion.place.refs_0_
  13.3 5.3 %all-to-all-done = f32[8,2,16,128]{3,2,1,0:T(8,128)S(1)} async-done(((f32[8,2,16,128]{3,2,1,0:T(8,128)}), f32[8,2,16,128]{3,2,1,0:T(8,128)S(1)}, u32[]{:S(2)}, u32[]{:S(2)}) %all-to-all-start) | async-done | bytes 131104 | tf_op jit(solution)/shard_map/all_to_all | solution.py:690
  18.6 5.7 %collective-permute-start.1 = (f32[16,16,128]{2,1,0:T(8,128)S(1)}, f32[16,16,128]{2,1,0:T(8,128)S(1)}, u32[]{:S(2)}, u32[]{:S(2)}) collective-permute-start(f32[16,16,128]{2,1,0:T(8,128)S(1)} %bitcast.22), channel_id=1, source_target_pairs={{0,127},{1,2},{2,1},{3,4},{4,3},{5,6},{6,5},{7,8},{8,7},{9,10},{10... | collective-permute-start | bytes 393224 | tf_op jit(solution)/shard_map/ppermute | solution.py:703
  24.3 0.0 collective-permute-start
  24.3 0.0 collective-permute-done.3.across
  24.3 0.0 collective-permute-done.2.pair
  24.3 0.0 copy-start
  24.3 0.0 copy-start.1
  24.3 0.0 copy-start.2
  24.4 0.0 copy-start.3
  24.4 4.7 %regress.1 = (f32[16,8,256]{2,1,0:T(8,128)S(1)}, f32[16,16,256]{2,1,0:T(8,128)S(1)}) custom-call(s32[2]{0:T(128)S(1)} %pad_add_fusion.place.refs_0_, f32[16,16,128]{2,1,0:T(8,128)S(1)} %pad_convert_fusion.own, f32[16,16,128]{2,1,0:T(8,128)S(1)} %collective-permute-done.2.pair, f32[16,16,128]{2,1,0:T(8,128)S(1)} %collective-permute-done.3.across, ...), custom_call_target="tpu_custom_call" | custom-call | flops 2000000000 | bytes 2000000 | tf_op jit(solution)/shard_map/regress/pallas_call | solution.py:593
  29.1 0.0 collective-permute-done.1.refs_3_
  29.1 0.6 collective-permute-done.refs_2_
  29.8 0.0 copy-done
  29.8 0.0 copy-done.1
  29.8 10.3 %step.1 = (bf16[2560,128]{1,0:T(8,128)(2,1)S(1)}, bf16[2560,128]{1,0:T(8,128)(2,1)S(1)}, bf16[8,8,128]{2,1,0:T(8,128)(2,1)S(1)}) custom-call(s32[2]{0:T(128)S(1)} %pad_add_fusion.place.refs_0_, f32[16,16,128]{2,1,0:T(8,128)S(1)} %bitcast.24, f32[16,16,128]{2,1,0:T(8,128)S(1)} %collective-permute-done.refs_2_, ...), custom_call_target="tpu_custom_call" | custom-call | tf_op jit(solution)/shard_map/step/pallas_call | solution.py:622
  40.1 3.4 %collective-permute-start.4 = (bf16[2560,128]{1,0:T(8,128)(2,1)S(1)}, bf16[2560,128]{1,0:T(8,128)(2,1)S(1)}, u32[]{:S(2)}, u32[]{:S(2)}) collective-permute-start(bf16[2560,128]{1,0:T(8,128)(2,1)S(1)} %get-tuple-element.18), channel_id=1, source_target_pairs={{0,8},{8,0},{1,9},{9,1},{2,10},{10,2},{3,11},{11,3},{4,12},{12,4},... | collective-permute-start | bytes 1966088 | tf_op jit(solution)/shard_map/ppermute | solution.py:703
  43.5 1.7 %collective-permute-done.4 = bf16[2560,128]{1,0:T(8,128)(2,1)S(1)} collective-permute-done((bf16[2560,128]{1,0:T(8,128)(2,1)S(1)}, bf16[2560,128]{1,0:T(8,128)(2,1)S(1)}, u32[]{:S(2)}, u32[]{:S(2)}) %collective-permute-start.4) | collective-permute-done | bytes 655392 | tf_op jit(solution)/shard_map/ppermute | solution.py:703
  45.2 0.2 add_convert_fusion
  45.4 0.1 pad_maximum_fusion
  45.5 20.6 %all_to_all.15 = bf16[64,48,128]{2,1,0:T(8,128)(2,1)S(1)} all-to-all(bf16[64,48,128]{2,1,0:T(8,128)(2,1)S(1)} %pad_maximum_fusion), channel_id=1, replica_groups=mesh['y'=4,'x_hi'=2,'core'=2,'x_lo'=2,'z'=4] {'y','x_hi','x_lo','z'}, dimensions={0} | all-to-all | bytes 1572864 | tf_op jit(solution)/shard_map/all_to_all | solution.py:690
  66.0 0.1 slice_reduce_fusion
  66.1 0.1 broadcast_in_dim.5
  66.2 17.1 %all_to_all.16 = bf16[64,40,128]{2,1,0:T(8,128)(2,1)S(1)} all-to-all(bf16[64,40,128]{2,1,0:T(8,128)(2,1)S(1)} %broadcast_in_dim.5), channel_id=1, replica_groups=mesh['y'=4,'x_hi'=2,'core'=2,'x_lo'=2,'z'=4] {'y','x_hi','x_lo','z'}, dimensions={0} | all-to-all | bytes 1310720 | tf_op jit(solution)/shard_map/spread/all_to_all | solution.py:690
  83.4 3.0 %collective-permute-start.5 = (bf16[2560,128]{1,0:T(8,128)(2,1)S(1)}, bf16[2560,128]{1,0:T(8,128)(2,1)S(1)}, u32[]{:S(2)}, u32[]{:S(2)}) collective-permute-start(bf16[2560,128]{1,0:T(8,128)(2,1)S(1)} %bitcast.18), channel_id=1, source_target_pairs={{0,8},{8,0},{1,9},{9,1},{2,10},{10,2},{3,11},{11,3},{4,12},{12,4},... | collective-permute-start | bytes 1966088 | tf_op jit(solution)/shard_map/ppermute | solution.py:703
  86.4 1.7 %collective-permute-done.5.other = bf16[2560,128]{1,0:T(8,128)(2,1)S(1)} collective-permute-done((bf16[2560,128]{1,0:T(8,128)(2,1)S(1)}, bf16[2560,128]{1,0:T(8,128)(2,1)S(1)}, u32[]{:S(2)}, u32[]{:S(2)}) %collective-permute-start.5) | collective-permute-done | bytes 655392 | tf_op jit(solution)/shard_map/ppermute | solution.py:703
  88.1 2.1 %unpack.1 = (f32[4,2,1024]{2,1,0:T(2,128)}, f32[3,3,20,128]{3,2,1,0:T(8,128)}, f32[3,3,256,128]{3,2,1,0:T(8,128)}, f32[3,3,128,256]{3,2,1,0:T(8,128)}, f32[3,3,4,128]{3,2,1,0:T(4,128)}) custom-call(s32[2]{0:T(128)S(1)} %pad_add_fusion.place.refs_0_, bf16[2560,128]{1,0:T(8,128)(2,1)S(1)} %bitcast.19, bf16[2560,128]{1,0:T(8,128)(2,1)S(1)} %collective-permute-done.5.other, ...), custom_call_target="tpu_custom_call" | custom-call | tf_op jit(solution)/shard_map/unpack/pallas_call | solution.py:675
  (6 shorter events, 0.1 us)
Async XLA Ops:
  1.5 22.8 %collective-permute-start.3 = (f32[16,16,128]{2,1,0:T(8,128)S(1)}, f32[16,16,128]{2,1,0:T(8,128)S(1)}, u32[]{:S(2)}, u32[]{:S(2)}) collective-permute-start(f32[16,16,128]{2,1,0:T(8,128)S(1)} %pad_convert_fusion.own), channel_id=1, source_target_pairs={{0,127},{1,2},{2,1},{3,4},{4,3},{5,6},{6,5},{7,8},{8,7},{9,10},{10... | collective-permute-start | bytes 393224 | tf_op jit(solution)/shard_map/ppermute | solution.py:703
  7.6 16.7 %collective-permute-start.2 = (f32[16,16,128]{2,1,0:T(8,128)S(1)}, f32[16,16,128]{2,1,0:T(8,128)S(1)}, u32[]{:S(2)}, u32[]{:S(2)}) collective-permute-start(f32[16,16,128]{2,1,0:T(8,128)S(1)} %pad_convert_fusion.own), channel_id=1, source_target_pairs={{0,1},{1,0},{2,3},{3,2},{4,5},{5,4},{6,7},{7,6},{8,9},{9,8},{10,11... | collective-permute-start | bytes 393224 | tf_op jit(solution)/shard_map/ppermute | solution.py:703
  9.8 8.8 %all-to-all-start = ((f32[8,2,16,128]{3,2,1,0:T(8,128)}), f32[8,2,16,128]{3,2,1,0:T(8,128)S(1)}, u32[]{:S(2)}, u32[]{:S(2)}) async-start(f32[8,2,16,128]{3,2,1,0:T(8,128)} %pack.1), calls=%async_computation | async-start | bytes 262144 | tf_op jit(solution)/shard_map/all_to_all | solution.py:690
  18.6 10.6 %collective-permute-start.1 = (f32[16,16,128]{2,1,0:T(8,128)S(1)}, f32[16,16,128]{2,1,0:T(8,128)S(1)}, u32[]{:S(2)}, u32[]{:S(2)}) collective-permute-start(f32[16,16,128]{2,1,0:T(8,128)S(1)} %bitcast.22), channel_id=1, source_target_pairs={{0,127},{1,2},{2,1},{3,4},{4,3},{5,6},{6,5},{7,8},{8,7},{9,10},{10... | collective-permute-start | bytes 393224 | tf_op jit(solution)/shard_map/ppermute | solution.py:703
  24.3 5.5 %collective-permute-start = (f32[16,16,128]{2,1,0:T(8,128)S(1)}, f32[16,16,128]{2,1,0:T(8,128)S(1)}, u32[]{:S(2)}, u32[]{:S(2)}) collective-permute-start(f32[16,16,128]{2,1,0:T(8,128)S(1)} %bitcast.23), channel_id=1, source_target_pairs={{0,1},{1,0},{2,3},{3,2},{4,5},{5,4},{6,7},{7,6},{8,9},{9,8},{10,11... | collective-permute-start | bytes 393224 | tf_op jit(solution)/shard_map/ppermute | solution.py:703
  24.3 5.5 %copy-start = (bf16[3,3,256,128]{3,2,1,0:T(8,128)(2,1)S(1)}, bf16[3,3,256,128]{3,2,1,0:T(8,128)(2,1)}, u32[]{:S(2)}) copy-start(bf16[3,3,256,128]{3,2,1,0:T(8,128)(2,1)} %param.21) | copy-start | bytes 1769476
  24.3 5.4 %copy-start.1 = (bf16[3,3,128,256]{3,2,1,0:T(8,128)(2,1)S(1)}, bf16[3,3,128,256]{3,2,1,0:T(8,128)(2,1)}, u32[]{:S(2)}) copy-start(bf16[3,3,128,256]{3,2,1,0:T(8,128)(2,1)} %param.22) | copy-start | bytes 1769476
  24.3 5.4 %copy-start.2 = (bf16[3,3,128,20]{2,3,1,0:T(8,128)(2,1)S(1)}, bf16[3,3,128,20]{2,3,1,0:T(8,128)(2,1)}, u32[]{:S(2)}) copy-start(bf16[3,3,128,20]{2,3,1,0:T(8,128)(2,1)} %param.20) | copy-start | bytes 138244
  24.4 5.4 %copy-start.3 = (bf16[3,3,4,128]{3,2,1,0:T(4,128)(2,1)S(1)}, bf16[3,3,4,128]{3,2,1,0:T(4,128)(2,1)}, u32[]{:S(2)}) copy-start(bf16[3,3,4,128]{3,2,1,0:T(4,128)(2,1)} %refs_9_.1) | copy-start | bytes 27652
  40.1 5.1 %collective-permute-start.4 = (bf16[2560,128]{1,0:T(8,128)(2,1)S(1)}, bf16[2560,128]{1,0:T(8,128)(2,1)S(1)}, u32[]{:S(2)}, u32[]{:S(2)}) collective-permute-start(bf16[2560,128]{1,0:T(8,128)(2,1)S(1)} %get-tuple-element.18), channel_id=1, source_target_pairs={{0,8},{8,0},{1,9},{9,1},{2,10},{10,2},{3,11},{11,3},{4,12},{12,4},... | collective-permute-start | bytes 1966088 | tf_op jit(solution)/shard_map/ppermute | solution.py:703
  83.4 4.7 %collective-permute-start.5 = (bf16[2560,128]{1,0:T(8,128)(2,1)S(1)}, bf16[2560,128]{1,0:T(8,128)(2,1)S(1)}, u32[]{:S(2)}, u32[]{:S(2)}) collective-permute-start(bf16[2560,128]{1,0:T(8,128)(2,1)S(1)} %bitcast.18), channel_id=1, source_target_pairs={{0,8},{8,0},{1,9},{9,1},{2,10},{10,2},{3,11},{11,3},{4,12},{12,4},... | collective-permute-start | bytes 1966088 | tf_op jit(solution)/shard_map/ppermute | solution.py:703

commit v8 on v7

--- a/solution.py
+++ b/solution.py
@@ -7,6 +7,7 @@
 from jax.experimental.pallas import tpu as pltpu
 from jax.sharding import Mesh
 from jax.sharding import PartitionSpec as P
+
 
 LEVELS = 32
 ROWS = 16
@@ -28,7 +29,6 @@
 
 FIELDS = 24
 UP_ROWS = 9 * HID1
-DOWN_ROWS = 9 * HID2
 BIG_ROWS = 2304
 LAST_ROWS = 72
 IN_ROWS = 9 * FIELDS
@@ -249,6 +249,7 @@
         taps[r + 1] = mm_nt(last_w, to_lanes(sec[r]))
 
     each(ROWS, mean_taps, CHUNK["taps"])
+
     def collect(r):
         mean[r] = four_channels(taps, r).astype(BF).astype(F32)
 
@@ -720,7 +721,8 @@
     scale = 1.0 / (target.shape[0] * math.sqrt(target.shape[1] * target.shape[2] * lax.axis_size(STRIPS)))
     place = jnp.stack([lax.axis_index("core"), lax.axis_index("z") % 2])
     place = place.astype(jnp.int32)
-    packed = all_to_all(pack(target, noise, land_mask, level_index), LAT).reshape(ROWS, 16, OWN)
+    packed = pack(target, noise, land_mask, level_index)
+    packed = all_to_all(packed, LAT).reshape(ROWS, 16, OWN)
     strip = jnp.pad(coarse.transpose(1, 0, 2).astype(F32), ((0, 0), (0, 4), (0, 0)))
     strip_across = swap(strip, STRIPS, 1)
     strip_pair = swap(strip, STRIPS, 0)
@@ -758,8 +760,7 @@
     total = parts[:, :rows].astype(F32).sum(0).astype(BF)
     seats = parts.reshape(chips // lats, lats, rows + CELL_ROWS, OWN)[:, :, rows:]
     seats = lax.dynamic_index_in_dim(seats, lax.axis_index(("y", "x_hi")), 0, False)
-    with jax.named_scope("spread"):
-        mine = all_to_all(jnp.broadcast_to(total[None], (chips, rows, OWN)), CHIPS).reshape(HALF_ROWS, OWN)
+    mine = all_to_all(jnp.broadcast_to(total[None], (chips, rows, OWN)), CHIPS).reshape(HALF_ROWS, OWN)
     tile, first, down, up, last = unpack(place, mine, swap(mine, "core", 0), seats)
     return (tile, first.transpose(0, 1, 3, 2), down, up, last)
 

time: 90.6 us -> 90.6 us (level)
  no operation moved by 1% of the time
where the time goes in v8:
time: 90.6 us; the launch traced here: 90.2 us
  blocking collectives  37.7 us (42%)
  starting transfers between devices  21.6 us (24%)
  Pallas kernels  18.6 us (21%)
  waiting for transfers between devices  9.34 us (10%)
  between operations  1.43 us (2%)
  local copies, waits for them, and re-layouts  0.98 us (1%)
    all_to_all x2, blocking collectives, all_to_all(): return lax.all_to_all(value, axes, split_axis=0, concat_axis=0, tiled=True)  37.7 us
    ppermute x6, starting transfers between devices, swap(): return lax.ppermute(value, axes, sorted(set(pairs)))  18.2 us
    pallas_call x1, Pallas kernels, step(): pl.pallas_call(kernel, out_shape=(jax.ShapeDtypeStruct((HALF_ROWS, OWN),...  10.3 us
    all_to_all x1, waiting for transfers between devices, all_to_all(): return lax.all_to_all(value, axes, split_axis=0, concat_axis=0, tiled=True)  5.28 us
    pallas_call x1, Pallas kernels, regress(): pl.pallas_call(regression_kernel, out_shape=(jax.ShapeDtypeStruct((ROWS,...  4.74 us
    ppermute x6, waiting for transfers between devices, swap(): return lax.ppermute(value, axes, sorted(set(pairs)))  4.06 us
    all_to_all x1, starting transfers between devices, all_to_all(): return lax.all_to_all(value, axes, split_axis=0, concat_axis=0, tiled=True)  3.38 us
    pallas_call x1, Pallas kernels, unpack(): pl.pallas_call(unpack_kernel, out_shape=tuple((jax.ShapeDtypeStruct(shape...  2.11 us
  transfers between devices with their start and end apart: 7, of which 4 were waited for; matrix products, arithmetic and copies ran while one was open for 0% of the time, Pallas kernels for 7%

profile of v8, /device:TPU:1, one launch (start us, length us, event | category | flops | bytes accessed | tf_op | source)
XLA Modules:
  0.0 90.2 jit_solution(7992567225154427786)
XLA Ops:
  0.6 0.8 copy.19
  1.5 6.1 %collective-permute-start.3 = (f32[16,16,128]{2,1,0:T(8,128)S(1)}, f32[16,16,128]{2,1,0:T(8,128)S(1)}, u32[]{:S(2)}, u32[]{:S(2)}) collective-permute-start(f32[16,16,128]{2,1,0:T(8,128)S(1)} %pad_convert_fusion.own), channel_id=1, source_target_pairs={{0,127},{1,2},{2,1},{3,4},{4,3},{5,6},{6,5},{7,8},{8,7},{9,10},{10... | collective-permute-start | bytes 393224 | tf_op jit(solution)/shard_map/ppermute | solution.py:704
  7.6 0.0 collective-permute-start.2
  8.3 1.5 %pack.1 = f32[8,2,16,128]{3,2,1,0:T(8,128)} custom-call(s32[1,1]{1,0:T(1,128)S(6)} %copy.20.level, f32[4,2,1024]{2,1,0:T(2,128)} %target_far.1, f32[4,2,1024]{2,1,0:T(2,128)} %noise_far.1, s32[2,1024]{1,0:T(2,128)} %mask_far.1), custom_call_target="tpu_custom_call" | custom-call | tf_op jit(solution)/shard_map/pack/pallas_call | solution.py:578
  9.8 3.4 %all-to-all-start = ((f32[8,2,16,128]{3,2,1,0:T(8,128)}), f32[8,2,16,128]{3,2,1,0:T(8,128)S(1)}, u32[]{:S(2)}, u32[]{:S(2)}) async-start(f32[8,2,16,128]{3,2,1,0:T(8,128)} %pack.1), calls=%async_computation | async-start | bytes 262144 | tf_op jit(solution)/shard_map/all_to_all | solution.py:691
  13.2 0.1 pad_add_fusion.place.refs_0_
  13.3 5.3 %all-to-all-done = f32[8,2,16,128]{3,2,1,0:T(8,128)S(1)} async-done(((f32[8,2,16,128]{3,2,1,0:T(8,128)}), f32[8,2,16,128]{3,2,1,0:T(8,128)S(1)}, u32[]{:S(2)}, u32[]{:S(2)}) %all-to-all-start) | async-done | bytes 131104 | tf_op jit(solution)/shard_map/all_to_all | solution.py:691
  18.6 5.7 %collective-permute-start.1 = (f32[16,16,128]{2,1,0:T(8,128)S(1)}, f32[16,16,128]{2,1,0:T(8,128)S(1)}, u32[]{:S(2)}, u32[]{:S(2)}) collective-permute-start(f32[16,16,128]{2,1,0:T(8,128)S(1)} %bitcast.22), channel_id=1, source_target_pairs={{0,127},{1,2},{2,1},{3,4},{4,3},{5,6},{6,5},{7,8},{8,7},{9,10},{10... | collective-permute-start | bytes 393224 | tf_op jit(solution)/shard_map/ppermute | solution.py:704
  24.3 0.0 collective-permute-start
  24.3 0.0 collective-permute-done.3.across
  24.3 0.0 collective-permute-done.2.pair
  24.3 0.0 copy-start
  24.3 0.0 copy-start.1
  24.3 0.0 copy-start.2
  24.4 0.0 copy-start.3
  24.4 4.7 %regress.1 = (f32[16,8,256]{2,1,0:T(8,128)S(1)}, f32[16,16,256]{2,1,0:T(8,128)S(1)}) custom-call(s32[2]{0:T(128)S(1)} %pad_add_fusion.place.refs_0_, f32[16,16,128]{2,1,0:T(8,128)S(1)} %pad_convert_fusion.own, f32[16,16,128]{2,1,0:T(8,128)S(1)} %collective-permute-done.2.pair, f32[16,16,128]{2,1,0:T(8,128)S(1)} %collective-permute-done.3.across, ...), custom_call_target="tpu_custom_call" | custom-call | flops 2000000000 | bytes 2000000 | tf_op jit(solution)/shard_map/regress/pallas_call | solution.py:594
  29.1 0.0 collective-permute-done.1.refs_3_
  29.1 0.6 collective-permute-done.refs_2_
  29.8 0.0 copy-done
  29.8 0.0 copy-done.1
  29.8 10.3 %step.1 = (bf16[2560,128]{1,0:T(8,128)(2,1)S(1)}, bf16[2560,128]{1,0:T(8,128)(2,1)S(1)}, bf16[8,8,128]{2,1,0:T(8,128)(2,1)S(1)}) custom-call(s32[2]{0:T(128)S(1)} %pad_add_fusion.place.refs_0_, f32[16,16,128]{2,1,0:T(8,128)S(1)} %bitcast.24, f32[16,16,128]{2,1,0:T(8,128)S(1)} %collective-permute-done.refs_2_, ...), custom_call_target="tpu_custom_call" | custom-call | tf_op jit(solution)/shard_map/step/pallas_call | solution.py:623
  40.1 3.4 %collective-permute-start.4 = (bf16[2560,128]{1,0:T(8,128)(2,1)S(1)}, bf16[2560,128]{1,0:T(8,128)(2,1)S(1)}, u32[]{:S(2)}, u32[]{:S(2)}) collective-permute-start(bf16[2560,128]{1,0:T(8,128)(2,1)S(1)} %get-tuple-element.18), channel_id=1, source_target_pairs={{0,8},{8,0},{1,9},{9,1},{2,10},{10,2},{3,11},{11,3},{4,12},{12,4},... | collective-permute-start | bytes 1966088 | tf_op jit(solution)/shard_map/ppermute | solution.py:704
  43.5 1.7 %collective-permute-done.4 = bf16[2560,128]{1,0:T(8,128)(2,1)S(1)} collective-permute-done((bf16[2560,128]{1,0:T(8,128)(2,1)S(1)}, bf16[2560,128]{1,0:T(8,128)(2,1)S(1)}, u32[]{:S(2)}, u32[]{:S(2)}) %collective-permute-start.4) | collective-permute-done | bytes 655392 | tf_op jit(solution)/shard_map/ppermute | solution.py:704
  45.2 0.2 add_convert_fusion
  45.4 0.1 pad_maximum_fusion
  45.5 20.6 %all_to_all.15 = bf16[64,48,128]{2,1,0:T(8,128)(2,1)S(1)} all-to-all(bf16[64,48,128]{2,1,0:T(8,128)(2,1)S(1)} %pad_maximum_fusion), channel_id=1, replica_groups=mesh['y'=4,'x_hi'=2,'core'=2,'x_lo'=2,'z'=4] {'y','x_hi','x_lo','z'}, dimensions={0} | all-to-all | bytes 1572864 | tf_op jit(solution)/shard_map/all_to_all | solution.py:691
  66.0 0.1 slice_reduce_fusion
  66.1 0.1 broadcast_in_dim.5
  66.2 17.1 %all_to_all.16 = bf16[64,40,128]{2,1,0:T(8,128)(2,1)S(1)} all-to-all(bf16[64,40,128]{2,1,0:T(8,128)(2,1)S(1)} %broadcast_in_dim.5), channel_id=1, replica_groups=mesh['y'=4,'x_hi'=2,'core'=2,'x_lo'=2,'z'=4] {'y','x_hi','x_lo','z'}, dimensions={0} | all-to-all | bytes 1310720 | tf_op jit(solution)/shard_map/all_to_all | solution.py:691
  83.4 3.0 %collective-permute-start.5 = (bf16[2560,128]{1,0:T(8,128)(2,1)S(1)}, bf16[2560,128]{1,0:T(8,128)(2,1)S(1)}, u32[]{:S(2)}, u32[]{:S(2)}) collective-permute-start(bf16[2560,128]{1,0:T(8,128)(2,1)S(1)} %bitcast.18), channel_id=1, source_target_pairs={{0,8},{8,0},{1,9},{9,1},{2,10},{10,2},{3,11},{11,3},{4,12},{12,4},... | collective-permute-start | bytes 1966088 | tf_op jit(solution)/shard_map/ppermute | solution.py:704
  86.4 1.7 %collective-permute-done.5.other = bf16[2560,128]{1,0:T(8,128)(2,1)S(1)} collective-permute-done((bf16[2560,128]{1,0:T(8,128)(2,1)S(1)}, bf16[2560,128]{1,0:T(8,128)(2,1)S(1)}, u32[]{:S(2)}, u32[]{:S(2)}) %collective-permute-start.5) | collective-permute-done | bytes 655392 | tf_op jit(solution)/shard_map/ppermute | solution.py:704
  88.1 2.1 %unpack.1 = (f32[4,2,1024]{2,1,0:T(2,128)}, f32[3,3,20,128]{3,2,1,0:T(8,128)}, f32[3,3,256,128]{3,2,1,0:T(8,128)}, f32[3,3,128,256]{3,2,1,0:T(8,128)}, f32[3,3,4,128]{3,2,1,0:T(4,128)}) custom-call(s32[2]{0:T(128)S(1)} %pad_add_fusion.place.refs_0_, bf16[2560,128]{1,0:T(8,128)(2,1)S(1)} %bitcast.19, bf16[2560,128]{1,0:T(8,128)(2,1)S(1)} %collective-permute-done.5.other, ...), custom_call_target="tpu_custom_call" | custom-call | tf_op jit(solution)/shard_map/unpack/pallas_call | solution.py:676
  (6 shorter events, 0.1 us)
Async XLA Ops:
  1.5 22.8 %collective-permute-start.3 = (f32[16,16,128]{2,1,0:T(8,128)S(1)}, f32[16,16,128]{2,1,0:T(8,128)S(1)}, u32[]{:S(2)}, u32[]{:S(2)}) collective-permute-start(f32[16,16,128]{2,1,0:T(8,128)S(1)} %pad_convert_fusion.own), channel_id=1, source_target_pairs={{0,127},{1,2},{2,1},{3,4},{4,3},{5,6},{6,5},{7,8},{8,7},{9,10},{10... | collective-permute-start | bytes 393224 | tf_op jit(solution)/shard_map/ppermute | solution.py:704
  7.6 16.7 %collective-permute-start.2 = (f32[16,16,128]{2,1,0:T(8,128)S(1)}, f32[16,16,128]{2,1,0:T(8,128)S(1)}, u32[]{:S(2)}, u32[]{:S(2)}) collective-permute-start(f32[16,16,128]{2,1,0:T(8,128)S(1)} %pad_convert_fusion.own), channel_id=1, source_target_pairs={{0,1},{1,0},{2,3},{3,2},{4,5},{5,4},{6,7},{7,6},{8,9},{9,8},{10,11... | collective-permute-start | bytes 393224 | tf_op jit(solution)/shard_map/ppermute | solution.py:704
  9.8 8.8 %all-to-all-start = ((f32[8,2,16,128]{3,2,1,0:T(8,128)}), f32[8,2,16,128]{3,2,1,0:T(8,128)S(1)}, u32[]{:S(2)}, u32[]{:S(2)}) async-start(f32[8,2,16,128]{3,2,1,0:T(8,128)} %pack.1), calls=%async_computation | async-start | bytes 262144 | tf_op jit(solution)/shard_map/all_to_all | solution.py:691
  18.6 10.6 %collective-permute-start.1 = (f32[16,16,128]{2,1,0:T(8,128)S(1)}, f32[16,16,128]{2,1,0:T(8,128)S(1)}, u32[]{:S(2)}, u32[]{:S(2)}) collective-permute-start(f32[16,16,128]{2,1,0:T(8,128)S(1)} %bitcast.22), channel_id=1, source_target_pairs={{0,127},{1,2},{2,1},{3,4},{4,3},{5,6},{6,5},{7,8},{8,7},{9,10},{10... | collective-permute-start | bytes 393224 | tf_op jit(solution)/shard_map/ppermute | solution.py:704
  24.3 5.5 %collective-permute-start = (f32[16,16,128]{2,1,0:T(8,128)S(1)}, f32[16,16,128]{2,1,0:T(8,128)S(1)}, u32[]{:S(2)}, u32[]{:S(2)}) collective-permute-start(f32[16,16,128]{2,1,0:T(8,128)S(1)} %bitcast.23), channel_id=1, source_target_pairs={{0,1},{1,0},{2,3},{3,2},{4,5},{5,4},{6,7},{7,6},{8,9},{9,8},{10,11... | collective-permute-start | bytes 393224 | tf_op jit(solution)/shard_map/ppermute | solution.py:704
  24.3 5.5 %copy-start = (bf16[3,3,256,128]{3,2,1,0:T(8,128)(2,1)S(1)}, bf16[3,3,256,128]{3,2,1,0:T(8,128)(2,1)}, u32[]{:S(2)}) copy-start(bf16[3,3,256,128]{3,2,1,0:T(8,128)(2,1)} %param.21) | copy-start | bytes 1769476
  24.3 5.4 %copy-start.1 = (bf16[3,3,128,256]{3,2,1,0:T(8,128)(2,1)S(1)}, bf16[3,3,128,256]{3,2,1,0:T(8,128)(2,1)}, u32[]{:S(2)}) copy-start(bf16[3,3,128,256]{3,2,1,0:T(8,128)(2,1)} %param.22) | copy-start | bytes 1769476
  24.3 5.4 %copy-start.2 = (bf16[3,3,128,20]{2,3,1,0:T(8,128)(2,1)S(1)}, bf16[3,3,128,20]{2,3,1,0:T(8,128)(2,1)}, u32[]{:S(2)}) copy-start(bf16[3,3,128,20]{2,3,1,0:T(8,128)(2,1)} %param.20) | copy-start | bytes 138244
  24.4 5.4 %copy-start.3 = (bf16[3,3,4,128]{3,2,1,0:T(4,128)(2,1)S(1)}, bf16[3,3,4,128]{3,2,1,0:T(4,128)(2,1)}, u32[]{:S(2)}) copy-start(bf16[3,3,4,128]{3,2,1,0:T(4,128)(2,1)} %refs_9_.1) | copy-start | bytes 27652
  40.1 5.1 %collective-permute-start.4 = (bf16[2560,128]{1,0:T(8,128)(2,1)S(1)}, bf16[2560,128]{1,0:T(8,128)(2,1)S(1)}, u32[]{:S(2)}, u32[]{:S(2)}) collective-permute-start(bf16[2560,128]{1,0:T(8,128)(2,1)S(1)} %get-tuple-element.18), channel_id=1, source_target_pairs={{0,8},{8,0},{1,9},{9,1},{2,10},{10,2},{3,11},{11,3},{4,12},{12,4},... | collective-permute-start | bytes 1966088 | tf_op jit(solution)/shard_map/ppermute | solution.py:704
  83.4 4.7 %collective-permute-start.5 = (bf16[2560,128]{1,0:T(8,128)(2,1)S(1)}, bf16[2560,128]{1,0:T(8,128)(2,1)S(1)}, u32[]{:S(2)}, u32[]{:S(2)}) collective-permute-start(bf16[2560,128]{1,0:T(8,128)(2,1)S(1)} %bitcast.18), channel_id=1, source_target_pairs={{0,8},{8,0},{1,9},{9,1},{2,10},{10,2},{3,11},{11,3},{4,12},{12,4},... | collective-permute-start | bytes 1966088 | tf_op jit(solution)/shard_map/ppermute | solution.py:704

commit v9 on v8

--- a/solution.py
+++ b/solution.py
@@ -36,19 +36,19 @@
 CELL_ROWS = 8
 CHUNK = {
     "gather": 8,
-    "first": (8, 1),
-    "second": (2, 2),
+    "first": (8, 2),
+    "second": (4, 2),
     "taps": 8,
-    "enter": 8,
-    "one": (8, 1),
-    "two": (4, 2),
-    "up": (8, 1),
+    "enter": 16,
+    "one": (8, 2),
+    "two": (2, 4),
+    "up": (4, 2),
     "three": 2,
-    "loss": 4,
-    "last": 8,
+    "loss": 8,
+    "last": 16,
     "back_three": (8, 1),
     "blocks": 4,
-    "back_two": (2, 4),
+    "back_two": (4, 2),
     "back_one": 4,
 }
 
@@ -208,8 +208,8 @@
     first_w = stack_inputs(stack, w_first, 16)
 
     def gather(r):
-        near, far = pair[r], across[r]
-        wide = with_halo(own[r], jnp.where(even, far, near), jnp.where(even, near, far))
+        near, far = pair[r].astype(F32), across[r].astype(F32)
+        wide = with_halo(own[r].astype(F32), jnp.where(even, far, near), jnp.where(even, near, far))
         coarse[r] = wide
         net[r + 1] = to_cells(lon_shifts(wide))
 
@@ -723,7 +723,7 @@
     place = place.astype(jnp.int32)
     packed = pack(target, noise, land_mask, level_index)
     packed = all_to_all(packed, LAT).reshape(ROWS, 16, OWN)
-    strip = jnp.pad(coarse.transpose(1, 0, 2).astype(F32), ((0, 0), (0, 4), (0, 0)))
+    strip = jnp.pad(coarse.transpose(1, 0, 2), ((0, 0), (0, 4), (0, 0)))
     strip_across = swap(strip, STRIPS, 1)
     strip_pair = swap(strip, STRIPS, 0)
     across = swap(packed, STRIPS, 1)

time: 90.6 us -> 85.4 us (0.943)
  waiting for transfers between devices: 9.34 us -> 3.83 us
  Pallas kernels: 18.6 us -> 17.3 us
  starting transfers between devices: 21.6 us -> 22.7 us
    all_to_all x1, waiting for transfers between devices: 5.28 us -> 0.01 us  [all_to_all(): return lax.all_to_all(value, axes, split_axis=0, concat_axis=0, tiled=True)]
    all_to_all x1, starting transfers between devices: 3.38 us -> 6.79 us  [all_to_all(): return lax.all_to_all(value, axes, split_axis=0, concat_axis=0, tiled=True)]
    ppermute x6, starting transfers between devices: 18.2 us -> 15.9 us  [swap(): return lax.ppermute(value, axes, sorted(set(pairs)))]
  transfers between devices with their start and end apart: 7 -> 7, of which waited for: 4 -> 3; matrix products, arithmetic and copies ran while one was open for 0% -> 1% of each run, Pallas kernels for 7% -> 5%
where the time goes in v9:
time: 85.4 us; the launch traced here: 85 us
  blocking collectives  38.4 us (45%)
  starting transfers between devices  22.7 us (27%)
  Pallas kernels  17.3 us (20%)
  waiting for transfers between devices  3.83 us (4%)
  between operations  1.41 us (2%)
  local copies, waits for them, and re-layouts  0.99 us (1%)
    all_to_all x2, blocking collectives, all_to_all(): return lax.all_to_all(value, axes, split_axis=0, concat_axis=0, tiled=True)  38.4 us
    ppermute x6, starting transfers between devices, swap(): return lax.ppermute(value, axes, sorted(set(pairs)))  15.9 us
    pallas_call x1, Pallas kernels, step(): pl.pallas_call(kernel, out_shape=(jax.ShapeDtypeStruct((HALF_ROWS, OWN),...  9.37 us
    all_to_all x1, starting transfers between devices, all_to_all(): return lax.all_to_all(value, axes, split_axis=0, concat_axis=0, tiled=True)  6.79 us
    pallas_call x1, Pallas kernels, regress(): pl.pallas_call(regression_kernel, out_shape=(jax.ShapeDtypeStruct((ROWS,...  4.29 us
    ppermute x6, waiting for transfers between devices, swap(): return lax.ppermute(value, axes, sorted(set(pairs)))  3.83 us
    pallas_call x1, Pallas kernels, unpack(): pl.pallas_call(unpack_kernel, out_shape=tuple((jax.ShapeDtypeStruct(shape...  2.11 us
  transfers between devices with their start and end apart: 7, of which 3 were waited for; matrix products, arithmetic and copies ran while one was open for 1% of the time, Pallas kernels for 5%

profile of v9, /device:TPU:1, one launch (start us, length us, event | category | flops | bytes accessed | tf_op | source)
XLA Modules:
  0.0 85.0 jit_solution(7537972904618586679)
XLA Ops:
  1.3 1.5 %pack.1 = f32[8,2,16,128]{3,2,1,0:T(8,128)} custom-call(s32[1,1]{1,0:T(1,128)S(6)} %copy.20.level, f32[4,2,1024]{2,1,0:T(2,128)} %target_far.1, f32[4,2,1024]{2,1,0:T(2,128)} %noise_far.1, s32[2,1024]{1,0:T(2,128)} %mask_far.1), custom_call_target="tpu_custom_call" | custom-call | tf_op jit(solution)/shard_map/pack/pallas_call | solution.py:578
  2.8 6.8 %all-to-all-start = ((f32[8,2,16,128]{3,2,1,0:T(8,128)}), f32[8,2,16,128]{3,2,1,0:T(8,128)S(1)}, u32[]{:S(2)}, u32[]{:S(2)}) async-start(f32[8,2,16,128]{3,2,1,0:T(8,128)} %pack.1), calls=%async_computation | async-start | bytes 262144 | tf_op jit(solution)/shard_map/all_to_all | solution.py:691
  9.6 0.8 copy.19
  10.4 4.8 %collective-permute-start.3 = (bf16[16,16,128]{2,1,0:T(8,128)(2,1)S(1)}, bf16[16,16,128]{2,1,0:T(8,128)(2,1)S(1)}, u32[]{:S(2)}, u32[]{:S(2)}) collective-permute-start(bf16[16,16,128]{2,1,0:T(8,128)(2,1)S(1)} %pad.4.own), channel_id=1, source_target_pairs={{0,127},{1,2},{2,1},{3,4},{4,3},{5,6},{6,5},{7,8},{8,7},{9,10},{10... | collective-permute-start | bytes 196616 | tf_op jit(solution)/shard_map/ppermute | solution.py:704
  15.2 0.0 collective-permute-start.2
  15.2 0.1 pad_add_fusion.place.refs_0_
  15.3 0.0 all-to-all-done
  15.3 2.9 %collective-permute-start.1 = (f32[16,16,128]{2,1,0:T(8,128)S(1)}, f32[16,16,128]{2,1,0:T(8,128)S(1)}, u32[]{:S(2)}, u32[]{:S(2)}) collective-permute-start(f32[16,16,128]{2,1,0:T(8,128)S(1)} %bitcast.22), channel_id=1, source_target_pairs={{0,127},{1,2},{2,1},{3,4},{4,3},{5,6},{6,5},{7,8},{8,7},{9,10},{10... | collective-permute-start | bytes 393224 | tf_op jit(solution)/shard_map/ppermute | solution.py:704
  18.2 0.0 collective-permute-start
  18.2 0.0 collective-permute-done.3.across
  18.2 0.4 collective-permute-done.2.pair
  18.6 0.0 copy-start
  18.6 0.0 copy-start.1
  18.6 4.3 %regress.1 = (f32[16,8,256]{2,1,0:T(8,128)S(1)}, f32[16,16,256]{2,1,0:T(8,128)S(1)}) custom-call(s32[2]{0:T(128)S(1)} %pad_add_fusion.place.refs_0_, bf16[16,16,128]{2,1,0:T(8,128)(2,1)S(1)} %pad.4.own, bf16[16,16,128]{2,1,0:T(8,128)(2,1)S(1)} %collective-permute-done.2.pair, bf16[16,16,128]{2,1,0:T(8,128)(2,1)S(1)} %collective-permute-done.3.across, ...), custom_call_target="tpu_custom_call" | custom-call | flops 2000000000 | bytes 2000000 | tf_op jit(solution)/shard_map/regress/pallas_call | solution.py:594
  22.9 0.0 collective-permute-done.1.refs_3_
  22.9 0.0 collective-permute-done.refs_2_
  22.9 0.0 copy-done
  23.0 0.0 copy-done.1
  23.0 0.0 copy-done.2
  23.0 0.0 copy-done.3
  23.0 9.4 %step.1 = (bf16[2560,128]{1,0:T(8,128)(2,1)S(1)}, bf16[2560,128]{1,0:T(8,128)(2,1)S(1)}, bf16[8,8,128]{2,1,0:T(8,128)(2,1)S(1)}) custom-call(s32[2]{0:T(128)S(1)} %pad_add_fusion.place.refs_0_, f32[16,16,128]{2,1,0:T(8,128)S(1)} %bitcast.24, f32[16,16,128]{2,1,0:T(8,128)S(1)} %collective-permute-done.refs_2_, ...), custom_call_target="tpu_custom_call" | custom-call | tf_op jit(solution)/shard_map/step/pallas_call | solution.py:623
  32.4 5.2 %collective-permute-start.4 = (bf16[2560,128]{1,0:T(8,128)(2,1)S(1)}, bf16[2560,128]{1,0:T(8,128)(2,1)S(1)}, u32[]{:S(2)}, u32[]{:S(2)}) collective-permute-start(bf16[2560,128]{1,0:T(8,128)(2,1)S(1)} %get-tuple-element.18), channel_id=1, source_target_pairs={{0,8},{8,0},{1,9},{9,1},{2,10},{10,2},{3,11},{11,3},{4,12},{12,4},... | collective-permute-start | bytes 1966088 | tf_op jit(solution)/shard_map/ppermute | solution.py:704
  37.6 1.7 %collective-permute-done.4 = bf16[2560,128]{1,0:T(8,128)(2,1)S(1)} collective-permute-done((bf16[2560,128]{1,0:T(8,128)(2,1)S(1)}, bf16[2560,128]{1,0:T(8,128)(2,1)S(1)}, u32[]{:S(2)}, u32[]{:S(2)}) %collective-permute-start.4) | collective-permute-done | bytes 655392 | tf_op jit(solution)/shard_map/ppermute | solution.py:704
  39.3 0.2 add_convert_fusion
  39.5 0.1 pad_maximum_fusion
  39.6 21.2 %all_to_all.15 = bf16[64,48,128]{2,1,0:T(8,128)(2,1)S(1)} all-to-all(bf16[64,48,128]{2,1,0:T(8,128)(2,1)S(1)} %pad_maximum_fusion), channel_id=1, replica_groups=mesh['y'=4,'x_hi'=2,'core'=2,'x_lo'=2,'z'=4] {'y','x_hi','x_lo','z'}, dimensions={0} | all-to-all | bytes 1572864 | tf_op jit(solution)/shard_map/all_to_all | solution.py:691
  60.8 0.1 slice_reduce_fusion
  61.0 0.1 broadcast_in_dim.5
  61.1 17.1 %all_to_all.16 = bf16[64,40,128]{2,1,0:T(8,128)(2,1)S(1)} all-to-all(bf16[64,40,128]{2,1,0:T(8,128)(2,1)S(1)} %broadcast_in_dim.5), channel_id=1, replica_groups=mesh['y'=4,'x_hi'=2,'core'=2,'x_lo'=2,'z'=4] {'y','x_hi','x_lo','z'}, dimensions={0} | all-to-all | bytes 1310720 | tf_op jit(solution)/shard_map/all_to_all | solution.py:691
  78.2 3.0 %collective-permute-start.5 = (bf16[2560,128]{1,0:T(8,128)(2,1)S(1)}, bf16[2560,128]{1,0:T(8,128)(2,1)S(1)}, u32[]{:S(2)}, u32[]{:S(2)}) collective-permute-start(bf16[2560,128]{1,0:T(8,128)(2,1)S(1)} %bitcast.18), channel_id=1, source_target_pairs={{0,8},{8,0},{1,9},{9,1},{2,10},{10,2},{3,11},{11,3},{4,12},{12,4},... | collective-permute-start | bytes 1966088 | tf_op jit(solution)/shard_map/ppermute | solution.py:704
  81.2 1.7 %collective-permute-done.5.other = bf16[2560,128]{1,0:T(8,128)(2,1)S(1)} collective-permute-done((bf16[2560,128]{1,0:T(8,128)(2,1)S(1)}, bf16[2560,128]{1,0:T(8,128)(2,1)S(1)}, u32[]{:S(2)}, u32[]{:S(2)}) %collective-permute-start.5) | collective-permute-done | bytes 655392 | tf_op jit(solution)/shard_map/ppermute | solution.py:704
  82.9 2.1 %unpack.1 = (f32[4,2,1024]{2,1,0:T(2,128)}, f32[3,3,20,128]{3,2,1,0:T(8,128)}, f32[3,3,256,128]{3,2,1,0:T(8,128)}, f32[3,3,128,256]{3,2,1,0:T(8,128)}, f32[3,3,4,128]{3,2,1,0:T(4,128)}) custom-call(s32[2]{0:T(128)S(1)} %pad_add_fusion.place.refs_0_, bf16[2560,128]{1,0:T(8,128)(2,1)S(1)} %bitcast.19, bf16[2560,128]{1,0:T(8,128)(2,1)S(1)} %collective-permute-done.5.other, ...), custom_call_target="tpu_custom_call" | custom-call | tf_op jit(solution)/shard_map/unpack/pallas_call | solution.py:676
  (6 shorter events, 0.1 us)
Async XLA Ops:
  2.8 12.5 %all-to-all-start = ((f32[8,2,16,128]{3,2,1,0:T(8,128)}), f32[8,2,16,128]{3,2,1,0:T(8,128)S(1)}, u32[]{:S(2)}, u32[]{:S(2)}) async-start(f32[8,2,16,128]{3,2,1,0:T(8,128)} %pack.1), calls=%async_computation | async-start | bytes 262144 | tf_op jit(solution)/shard_map/all_to_all | solution.py:691
  10.4 7.8 %collective-permute-start.3 = (bf16[16,16,128]{2,1,0:T(8,128)(2,1)S(1)}, bf16[16,16,128]{2,1,0:T(8,128)(2,1)S(1)}, u32[]{:S(2)}, u32[]{:S(2)}) collective-permute-start(bf16[16,16,128]{2,1,0:T(8,128)(2,1)S(1)} %pad.4.own), channel_id=1, source_target_pairs={{0,127},{1,2},{2,1},{3,4},{4,3},{5,6},{6,5},{7,8},{8,7},{9,10},{10... | collective-permute-start | bytes 196616 | tf_op jit(solution)/shard_map/ppermute | solution.py:704
  15.2 3.4 %collective-permute-start.2 = (bf16[16,16,128]{2,1,0:T(8,128)(2,1)S(1)}, bf16[16,16,128]{2,1,0:T(8,128)(2,1)S(1)}, u32[]{:S(2)}, u32[]{:S(2)}) collective-permute-start(bf16[16,16,128]{2,1,0:T(8,128)(2,1)S(1)} %pad.4.own), channel_id=1, source_target_pairs={{0,1},{1,0},{2,3},{3,2},{4,5},{5,4},{6,7},{7,6},{8,9},{9,8},{10,11... | collective-permute-start | bytes 196616 | tf_op jit(solution)/shard_map/ppermute | solution.py:704
  15.3 7.6 %collective-permute-start.1 = (f32[16,16,128]{2,1,0:T(8,128)S(1)}, f32[16,16,128]{2,1,0:T(8,128)S(1)}, u32[]{:S(2)}, u32[]{:S(2)}) collective-permute-start(f32[16,16,128]{2,1,0:T(8,128)S(1)} %bitcast.22), channel_id=1, source_target_pairs={{0,127},{1,2},{2,1},{3,4},{4,3},{5,6},{6,5},{7,8},{8,7},{9,10},{10... | collective-permute-start | bytes 393224 | tf_op jit(solution)/shard_map/ppermute | solution.py:704
  18.2 4.7 %collective-permute-start = (f32[16,16,128]{2,1,0:T(8,128)S(1)}, f32[16,16,128]{2,1,0:T(8,128)S(1)}, u32[]{:S(2)}, u32[]{:S(2)}) collective-permute-start(f32[16,16,128]{2,1,0:T(8,128)S(1)} %bitcast.23), channel_id=1, source_target_pairs={{0,1},{1,0},{2,3},{3,2},{4,5},{5,4},{6,7},{7,6},{8,9},{9,8},{10,11... | collective-permute-start | bytes 393224 | tf_op jit(solution)/shard_map/ppermute | solution.py:704
  18.6 4.3 %copy-start = (bf16[3,3,256,128]{3,2,1,0:T(8,128)(2,1)S(1)}, bf16[3,3,256,128]{3,2,1,0:T(8,128)(2,1)}, u32[]{:S(2)}) copy-start(bf16[3,3,256,128]{3,2,1,0:T(8,128)(2,1)} %param.21) | copy-start | bytes 1769476
  18.6 4.3 %copy-start.1 = (bf16[3,3,128,256]{3,2,1,0:T(8,128)(2,1)S(1)}, bf16[3,3,128,256]{3,2,1,0:T(8,128)(2,1)}, u32[]{:S(2)}) copy-start(bf16[3,3,128,256]{3,2,1,0:T(8,128)(2,1)} %param.22) | copy-start | bytes 1769476
  18.6 4.3 %copy-start.2 = (bf16[3,3,128,20]{2,3,1,0:T(8,128)(2,1)S(1)}, bf16[3,3,128,20]{2,3,1,0:T(8,128)(2,1)}, u32[]{:S(2)}) copy-start(bf16[3,3,128,20]{2,3,1,0:T(8,128)(2,1)} %param.20) | copy-start | bytes 138244
  18.6 4.4 %copy-start.3 = (bf16[3,3,4,128]{3,2,1,0:T(4,128)(2,1)S(1)}, bf16[3,3,4,128]{3,2,1,0:T(4,128)(2,1)}, u32[]{:S(2)}) copy-start(bf16[3,3,4,128]{3,2,1,0:T(4,128)(2,1)} %refs_9_.1) | copy-start | bytes 27652
  32.4 7.0 %collective-permute-start.4 = (bf16[2560,128]{1,0:T(8,128)(2,1)S(1)}, bf16[2560,128]{1,0:T(8,128)(2,1)S(1)}, u32[]{:S(2)}, u32[]{:S(2)}) collective-permute-start(bf16[2560,128]{1,0:T(8,128)(2,1)S(1)} %get-tuple-element.18), channel_id=1, source_target_pairs={{0,8},{8,0},{1,9},{9,1},{2,10},{10,2},{3,11},{11,3},{4,12},{12,4},... | collective-permute-start | bytes 1966088 | tf_op jit(solution)/shard_map/ppermute | solution.py:704
  78.2 4.7 %collective-permute-start.5 = (bf16[2560,128]{1,0:T(8,128)(2,1)S(1)}, bf16[2560,128]{1,0:T(8,128)(2,1)S(1)}, u32[]{:S(2)}, u32[]{:S(2)}) collective-permute-start(bf16[2560,128]{1,0:T(8,128)(2,1)S(1)} %bitcast.18), channel_id=1, source_target_pairs={{0,8},{8,0},{1,9},{9,1},{2,10},{10,2},{3,11},{11,3},{4,12},{12,4},... | collective-permute-start | bytes 1966088 | tf_op jit(solution)/shard_map/ppermute | solution.py:704

commit v10 on v9

--- a/solution.py
+++ b/solution.py
@@ -35,7 +35,7 @@
 HALF_ROWS = 2560
 CELL_ROWS = 8
 CHUNK = {
-    "gather": 8,
+    "gather": 16,
     "first": (8, 2),
     "second": (4, 2),
     "taps": 8,
@@ -136,11 +136,14 @@
     lax.fori_loop(0, count, step, 0, unroll=unroll)
 
 
-def pack_kernel(level, target_far, noise_far, mask_far, packed, target, noise, land_mask, sems):
+def pack_kernel(
+    level, target_far, noise_far, mask_far, coarse_far, packed, strip, target, noise, land_mask, coarse, sems
+):
     arrive = [
         pltpu.make_async_copy(target_far, target, sems.at[0]),
         pltpu.make_async_copy(noise_far, noise, sems.at[1]),
         pltpu.make_async_copy(mask_far, land_mask, sems.at[2]),
+        pltpu.make_async_copy(coarse_far, coarse, sems.at[3]),
     ]
     for copy in arrive:
         copy.start()
@@ -158,6 +161,8 @@
             packed[p, r, 4:8] = target[:, r, lanes]
             packed[p, r, 8:12] = jnp.zeros((4, OWN), F32)
             packed[p, r, 12:16] = noise[:, r, lanes]
+    rows = jnp.transpose(coarse[...].astype(F32), (1, 0, 2))
+    strip[...] = jnp.concatenate([rows, jnp.zeros((ROWS, 4, OWN), F32)], axis=1).astype(BF)
 
 
 def stack_inputs(ref, weight, room):
@@ -573,21 +578,26 @@
     return pl.BlockSpec(memory_space=pltpu.MemorySpace.SMEM)
 
 
-def pack(target, noise, land_mask, level_index):
+def pack(target, noise, land_mask, coarse, level_index):
     lats = target.shape[2] // OWN
     return pl.pallas_call(
         pack_kernel,
-        out_shape=jax.ShapeDtypeStruct((lats, 2, 16, OWN), F32),
-        in_specs=[in_smem(), *in_hbm(3)],
-        out_specs=in_vmem(1)[0],
+        out_shape=(
+            jax.ShapeDtypeStruct((lats, 2, 16, OWN), F32),
+            jax.ShapeDtypeStruct((ROWS, 16, OWN), BF),
+        ),
+        in_specs=[in_smem(), *in_hbm(4)],
+        out_specs=tuple(in_vmem(2)),
         scratch_shapes=[
             pltpu.VMEM(target.shape, F32),
             pltpu.VMEM(noise.shape, F32),
             pltpu.VMEM(land_mask.shape, jnp.int32),
-            pltpu.SemaphoreType.DMA((3,)),
+            pltpu.VMEM(coarse.shape, BF),
+            pltpu.SemaphoreType.DMA((4,)),
         ],
+        compiler_params=pltpu.CompilerParams(vmem_limit_bytes=8 * 2**20),
         name="pack",
-    )(level_index, target, noise, land_mask)
+    )(level_index, in_place(target), in_place(noise), in_place(land_mask), in_place(coarse))
 
 
 def regress(*operands):
@@ -721,9 +731,8 @@
     scale = 1.0 / (target.shape[0] * math.sqrt(target.shape[1] * target.shape[2] * lax.axis_size(STRIPS)))
     place = jnp.stack([lax.axis_index("core"), lax.axis_index("z") % 2])
     place = place.astype(jnp.int32)
-    packed = pack(target, noise, land_mask, level_index)
+    packed, strip = pack(target, noise, land_mask, coarse, level_index)
     packed = all_to_all(packed, LAT).reshape(ROWS, 16, OWN)
-    strip = jnp.pad(coarse.transpose(1, 0, 2), ((0, 0), (0, 4), (0, 0)))
     strip_across = swap(strip, STRIPS, 1)
     strip_pair = swap(strip, STRIPS, 0)
     across = swap(packed, STRIPS, 1)

time: 85.4 us -> 85 us (level)
  starting transfers between devices: 22.7 us -> 21.7 us
    ppermute x6, starting transfers between devices: 15.9 us -> 14.9 us  [swap(): return lax.ppermute(value, axes, sorted(set(pairs)))]
  transfers between devices with their start and end apart: 7 -> 7, of which waited for: 3 -> 3; matrix products, arithmetic and copies ran while one was open for 1% -> 0% of each run, Pallas kernels for 5% -> 6%
where the time goes in v10:
time: 85 us; the launch traced here: 84.7 us
  blocking collectives  38.8 us (46%)
  starting transfers between devices  21.7 us (26%)
  Pallas kernels  18 us (21%)
  waiting for transfers between devices  4.09 us (5%)
  between operations  1.43 us (2%)
    all_to_all x2, blocking collectives, all_to_all(): return lax.all_to_all(value, axes, split_axis=0, concat_axis=0, tiled=True)  38.8 us
    ppermute x6, starting transfers between devices, swap(): return lax.ppermute(value, axes, sorted(set(pairs)))  14.9 us
    pallas_call x1, Pallas kernels, step(): pl.pallas_call(kernel, out_shape=(jax.ShapeDtypeStruct((HALF_ROWS, OWN),...  9.39 us
    all_to_all x1, starting transfers between devices, all_to_all(): return lax.all_to_all(value, axes, split_axis=0, concat_axis=0, tiled=True)  6.79 us
    pallas_call x1, Pallas kernels, regress(): pl.pallas_call(regression_kernel, out_shape=(jax.ShapeDtypeStruct((ROWS,...  4.88 us
    ppermute x6, waiting for transfers between devices, swap(): return lax.ppermute(value, axes, sorted(set(pairs)))  3.41 us
    pallas_call x1, Pallas kernels, unpack(): pl.pallas_call(unpack_kernel, out_shape=tuple((jax.ShapeDtypeStruct(shape...  2.11 us
  transfers between devices with their start and end apart: 7, of which 3 were waited for; matrix products, arithmetic and copies ran while one was open for 0% of the time, Pallas kernels for 6%

profile of v10, /device:TPU:1, one launch (start us, length us, event | category | flops | bytes accessed | tf_op | source)
XLA Modules:
  0.0 84.7 jit_solution(17737960729409225877)
XLA Ops:
  1.3 1.6 %pack.1 = (f32[8,2,16,128]{3,2,1,0:T(8,128)}, bf16[16,16,128]{2,1,0:T(8,128)(2,1)S(1)}) custom-call(s32[1,1]{1,0:T(1,128)S(6)} %copy.17.level, f32[4,2,1024]{2,1,0:T(2,128)} %target_far.1, f32[4,2,1024]{2,1,0:T(2,128)} %noise_far.1, s32[2,1024]{1,0:T(2,128)} %mask_far.1, bf16[12,16,128]{2,1,0:T(8,128)(2,1)} %coarse_far.1), custom_call_target="tpu_custom_call" | custom-call | tf_op jit(solution)/shard_map/pack/pallas_call | solution.py:583
  2.9 6.8 %all-to-all-start = ((f32[8,2,16,128]{3,2,1,0:T(8,128)}), f32[8,2,16,128]{3,2,1,0:T(8,128)S(1)}, u32[]{:S(2)}, u32[]{:S(2)}) async-start(f32[8,2,16,128]{3,2,1,0:T(8,128)} %get-tuple-element.17), calls=%async_computation | async-start | bytes 262144 | tf_op jit(solution)/shard_map/all_to_all | solution.py:701
  9.7 4.7 %collective-permute-start.3 = (bf16[16,16,128]{2,1,0:T(8,128)(2,1)S(1)}, bf16[16,16,128]{2,1,0:T(8,128)(2,1)S(1)}, u32[]{:S(2)}, u32[]{:S(2)}) collective-permute-start(bf16[16,16,128]{2,1,0:T(8,128)(2,1)S(1)} %get-tuple-element.18.own), channel_id=1, source_target_pairs={{0,127},{1,2},{2,1},{3,4},{4,3},{5,6},{6,5},{7,8},{8,7},{9,10},{10... | collective-permute-start | bytes 196616 | tf_op jit(solution)/shard_map/ppermute | solution.py:714
  14.4 0.0 collective-permute-start.2
  14.4 0.1 pad_add_fusion.place.refs_0_
  14.5 0.7 all-to-all-done
  15.1 3.2 %collective-permute-start.1 = (f32[16,16,128]{2,1,0:T(8,128)S(1)}, f32[16,16,128]{2,1,0:T(8,128)S(1)}, u32[]{:S(2)}, u32[]{:S(2)}) collective-permute-start(f32[16,16,128]{2,1,0:T(8,128)S(1)} %bitcast.19), channel_id=1, source_target_pairs={{0,127},{1,2},{2,1},{3,4},{4,3},{5,6},{6,5},{7,8},{8,7},{9,10},{10... | collective-permute-start | bytes 393224 | tf_op jit(solution)/shard_map/ppermute | solution.py:714
  18.3 0.0 collective-permute-start
  18.3 0.0 collective-permute-done.3.across
  18.3 0.0 collective-permute-done.2.pair
  18.3 0.0 copy-start
  18.3 0.0 copy-start.1
  18.3 0.0 copy-start.2
  18.3 0.0 copy-start.3
  18.3 4.9 %regress.1 = (f32[16,8,256]{2,1,0:T(8,128)S(1)}, f32[16,16,256]{2,1,0:T(8,128)S(1)}) custom-call(s32[2]{0:T(128)S(1)} %pad_add_fusion.place.refs_0_, bf16[16,16,128]{2,1,0:T(8,128)(2,1)S(1)} %get-tuple-element.18.own, bf16[16,16,128]{2,1,0:T(8,128)(2,1)S(1)} %collective-permute-done.2.pair, bf16[16,16,128]{2,1,0:T(8,128)(2,1)S(1)} %collective-permute-done.3.across, ...), custom_call_target="tpu_custom_call" | custom-call | flops 2000000000 | bytes 2000000 | tf_op jit(solution)/shard_map/regress/pallas_call | solution.py:604
  23.2 0.0 collective-permute-done.1.refs_3_
  23.2 0.0 collective-permute-done.refs_2_
  23.2 0.0 copy-done
  23.3 0.0 copy-done.1
  23.3 0.0 copy-done.2
  23.3 9.4 %step.1 = (bf16[2560,128]{1,0:T(8,128)(2,1)S(1)}, bf16[2560,128]{1,0:T(8,128)(2,1)S(1)}, bf16[8,8,128]{2,1,0:T(8,128)(2,1)S(1)}) custom-call(s32[2]{0:T(128)S(1)} %pad_add_fusion.place.refs_0_, f32[16,16,128]{2,1,0:T(8,128)S(1)} %bitcast.21, f32[16,16,128]{2,1,0:T(8,128)S(1)} %collective-permute-done.refs_2_, ...), custom_call_target="tpu_custom_call" | custom-call | tf_op jit(solution)/shard_map/step/pallas_call | solution.py:633
  32.7 4.1 %collective-permute-start.4 = (bf16[2560,128]{1,0:T(8,128)(2,1)S(1)}, bf16[2560,128]{1,0:T(8,128)(2,1)S(1)}, u32[]{:S(2)}, u32[]{:S(2)}) collective-permute-start(bf16[2560,128]{1,0:T(8,128)(2,1)S(1)} %get-tuple-element.22), channel_id=1, source_target_pairs={{0,8},{8,0},{1,9},{9,1},{2,10},{10,2},{3,11},{11,3},{4,12},{12,4},... | collective-permute-start | bytes 1966088 | tf_op jit(solution)/shard_map/ppermute | solution.py:714
  36.8 1.7 %collective-permute-done.4 = bf16[2560,128]{1,0:T(8,128)(2,1)S(1)} collective-permute-done((bf16[2560,128]{1,0:T(8,128)(2,1)S(1)}, bf16[2560,128]{1,0:T(8,128)(2,1)S(1)}, u32[]{:S(2)}, u32[]{:S(2)}) %collective-permute-start.4) | collective-permute-done | bytes 655392 | tf_op jit(solution)/shard_map/ppermute | solution.py:714
  38.5 0.2 add_convert_fusion
  38.7 0.1 pad_maximum_fusion
  38.8 21.6 %all_to_all.15 = bf16[64,48,128]{2,1,0:T(8,128)(2,1)S(1)} all-to-all(bf16[64,48,128]{2,1,0:T(8,128)(2,1)S(1)} %pad_maximum_fusion), channel_id=1, replica_groups=mesh['y'=4,'x_hi'=2,'core'=2,'x_lo'=2,'z'=4] {'y','x_hi','x_lo','z'}, dimensions={0} | all-to-all | bytes 1572864 | tf_op jit(solution)/shard_map/all_to_all | solution.py:701
  60.4 0.1 slice_reduce_fusion
  60.5 0.1 broadcast_in_dim.5
  60.6 17.3 %all_to_all.16 = bf16[64,40,128]{2,1,0:T(8,128)(2,1)S(1)} all-to-all(bf16[64,40,128]{2,1,0:T(8,128)(2,1)S(1)} %broadcast_in_dim.5), channel_id=1, replica_groups=mesh['y'=4,'x_hi'=2,'core'=2,'x_lo'=2,'z'=4] {'y','x_hi','x_lo','z'}, dimensions={0} | all-to-all | bytes 1310720 | tf_op jit(solution)/shard_map/all_to_all | solution.py:701
  77.9 3.0 %collective-permute-start.5 = (bf16[2560,128]{1,0:T(8,128)(2,1)S(1)}, bf16[2560,128]{1,0:T(8,128)(2,1)S(1)}, u32[]{:S(2)}, u32[]{:S(2)}) collective-permute-start(bf16[2560,128]{1,0:T(8,128)(2,1)S(1)} %bitcast.15), channel_id=1, source_target_pairs={{0,8},{8,0},{1,9},{9,1},{2,10},{10,2},{3,11},{11,3},{4,12},{12,4},... | collective-permute-start | bytes 1966088 | tf_op jit(solution)/shard_map/ppermute | solution.py:714
  80.9 1.7 %collective-permute-done.5.other = bf16[2560,128]{1,0:T(8,128)(2,1)S(1)} collective-permute-done((bf16[2560,128]{1,0:T(8,128)(2,1)S(1)}, bf16[2560,128]{1,0:T(8,128)(2,1)S(1)}, u32[]{:S(2)}, u32[]{:S(2)}) %collective-permute-start.5) | collective-permute-done | bytes 655392 | tf_op jit(solution)/shard_map/ppermute | solution.py:714
  82.5 2.1 %unpack.1 = (f32[4,2,1024]{2,1,0:T(2,128)}, f32[3,3,20,128]{3,2,1,0:T(8,128)}, f32[3,3,256,128]{3,2,1,0:T(8,128)}, f32[3,3,128,256]{3,2,1,0:T(8,128)}, f32[3,3,4,128]{3,2,1,0:T(4,128)}) custom-call(s32[2]{0:T(128)S(1)} %pad_add_fusion.place.refs_0_, bf16[2560,128]{1,0:T(8,128)(2,1)S(1)} %bitcast.16, bf16[2560,128]{1,0:T(8,128)(2,1)S(1)} %collective-permute-done.5.other, ...), custom_call_target="tpu_custom_call" | custom-call | tf_op jit(solution)/shard_map/unpack/pallas_call | solution.py:686
  (4 shorter events, 0.1 us)
Async XLA Ops:
  2.9 12.2 %all-to-all-start = ((f32[8,2,16,128]{3,2,1,0:T(8,128)}), f32[8,2,16,128]{3,2,1,0:T(8,128)S(1)}, u32[]{:S(2)}, u32[]{:S(2)}) async-start(f32[8,2,16,128]{3,2,1,0:T(8,128)} %get-tuple-element.17), calls=%async_computation | async-start | bytes 262144 | tf_op jit(solution)/shard_map/all_to_all | solution.py:701
  9.7 8.6 %collective-permute-start.3 = (bf16[16,16,128]{2,1,0:T(8,128)(2,1)S(1)}, bf16[16,16,128]{2,1,0:T(8,128)(2,1)S(1)}, u32[]{:S(2)}, u32[]{:S(2)}) collective-permute-start(bf16[16,16,128]{2,1,0:T(8,128)(2,1)S(1)} %get-tuple-element.18.own), channel_id=1, source_target_pairs={{0,127},{1,2},{2,1},{3,4},{4,3},{5,6},{6,5},{7,8},{8,7},{9,10},{10... | collective-permute-start | bytes 196616 | tf_op jit(solution)/shard_map/ppermute | solution.py:714
  14.4 3.9 %collective-permute-start.2 = (bf16[16,16,128]{2,1,0:T(8,128)(2,1)S(1)}, bf16[16,16,128]{2,1,0:T(8,128)(2,1)S(1)}, u32[]{:S(2)}, u32[]{:S(2)}) collective-permute-start(bf16[16,16,128]{2,1,0:T(8,128)(2,1)S(1)} %get-tuple-element.18.own), channel_id=1, source_target_pairs={{0,1},{1,0},{2,3},{3,2},{4,5},{5,4},{6,7},{7,6},{8,9},{9,8},{10,11... | collective-permute-start | bytes 196616 | tf_op jit(solution)/shard_map/ppermute | solution.py:714
  15.1 8.1 %collective-permute-start.1 = (f32[16,16,128]{2,1,0:T(8,128)S(1)}, f32[16,16,128]{2,1,0:T(8,128)S(1)}, u32[]{:S(2)}, u32[]{:S(2)}) collective-permute-start(f32[16,16,128]{2,1,0:T(8,128)S(1)} %bitcast.19), channel_id=1, source_target_pairs={{0,127},{1,2},{2,1},{3,4},{4,3},{5,6},{6,5},{7,8},{8,7},{9,10},{10... | collective-permute-start | bytes 393224 | tf_op jit(solution)/shard_map/ppermute | solution.py:714
  18.3 5.0 %collective-permute-start = (f32[16,16,128]{2,1,0:T(8,128)S(1)}, f32[16,16,128]{2,1,0:T(8,128)S(1)}, u32[]{:S(2)}, u32[]{:S(2)}) collective-permute-start(f32[16,16,128]{2,1,0:T(8,128)S(1)} %bitcast.20), channel_id=1, source_target_pairs={{0,1},{1,0},{2,3},{3,2},{4,5},{5,4},{6,7},{7,6},{8,9},{9,8},{10,11... | collective-permute-start | bytes 393224 | tf_op jit(solution)/shard_map/ppermute | solution.py:714
  18.3 5.0 %copy-start = (bf16[3,3,256,128]{3,2,1,0:T(8,128)(2,1)S(1)}, bf16[3,3,256,128]{3,2,1,0:T(8,128)(2,1)}, u32[]{:S(2)}) copy-start(bf16[3,3,256,128]{3,2,1,0:T(8,128)(2,1)} %param.21) | copy-start | bytes 1769476
  18.3 5.0 %copy-start.1 = (bf16[3,3,128,256]{3,2,1,0:T(8,128)(2,1)S(1)}, bf16[3,3,128,256]{3,2,1,0:T(8,128)(2,1)}, u32[]{:S(2)}) copy-start(bf16[3,3,128,256]{3,2,1,0:T(8,128)(2,1)} %param.22) | copy-start | bytes 1769476
  18.3 5.0 %copy-start.2 = (bf16[3,3,128,20]{2,3,1,0:T(8,128)(2,1)S(1)}, bf16[3,3,128,20]{2,3,1,0:T(8,128)(2,1)}, u32[]{:S(2)}) copy-start(bf16[3,3,128,20]{2,3,1,0:T(8,128)(2,1)} %param.20) | copy-start | bytes 138244
  18.3 4.9 %copy-start.3 = (bf16[3,3,4,128]{3,2,1,0:T(4,128)(2,1)S(1)}, bf16[3,3,4,128]{3,2,1,0:T(4,128)(2,1)}, u32[]{:S(2)}) copy-start(bf16[3,3,4,128]{3,2,1,0:T(4,128)(2,1)} %refs_9_.1) | copy-start | bytes 27652
  32.7 5.8 %collective-permute-start.4 = (bf16[2560,128]{1,0:T(8,128)(2,1)S(1)}, bf16[2560,128]{1,0:T(8,128)(2,1)S(1)}, u32[]{:S(2)}, u32[]{:S(2)}) collective-permute-start(bf16[2560,128]{1,0:T(8,128)(2,1)S(1)} %get-tuple-element.22), channel_id=1, source_target_pairs={{0,8},{8,0},{1,9},{9,1},{2,10},{10,2},{3,11},{11,3},{4,12},{12,4},... | collective-permute-start | bytes 1966088 | tf_op jit(solution)/shard_map/ppermute | solution.py:714
  77.9 4.7 %collective-permute-start.5 = (bf16[2560,128]{1,0:T(8,128)(2,1)S(1)}, bf16[2560,128]{1,0:T(8,128)(2,1)S(1)}, u32[]{:S(2)}, u32[]{:S(2)}) collective-permute-start(bf16[2560,128]{1,0:T(8,128)(2,1)S(1)} %bitcast.15), channel_id=1, source_target_pairs={{0,8},{8,0},{1,9},{9,1},{2,10},{10,2},{3,11},{11,3},{4,12},{12,4},... | collective-permute-start | bytes 1966088 | tf_op jit(solution)/shard_map/ppermute | solution.py:714

commit v11 on v10

--- a/solution.py
+++ b/solution.py
@@ -35,7 +35,7 @@
 HALF_ROWS = 2560
 CELL_ROWS = 8
 CHUNK = {
-    "gather": 16,
+    "gather": 8,
     "first": (8, 2),
     "second": (4, 2),
     "taps": 8,
@@ -46,8 +46,8 @@
     "three": 2,
     "loss": 8,
     "last": 16,
-    "back_three": (8, 1),
-    "blocks": 4,
+    "back_three": (16, 1),
+    "blocks": 8,
     "back_two": (4, 2),
     "back_one": 4,
 }

time: 85 us -> 84.2 us (level)
  Pallas kernels: 18 us -> 17.1 us
  transfers between devices with their start and end apart: 7 -> 7, of which waited for: 3 -> 3; matrix products, arithmetic and copies ran while one was open for 0% -> 0% of each run, Pallas kernels for 6% -> 5%
where the time goes in v11:
time: 84.2 us; the launch traced here: 83.8 us
  blocking collectives  38.2 us (45%)
  starting transfers between devices  22.3 us (26%)
  Pallas kernels  17.1 us (20%)
  waiting for transfers between devices  4.09 us (5%)
  between operations  1.43 us (2%)
    all_to_all x2, blocking collectives, all_to_all(): return lax.all_to_all(value, axes, split_axis=0, concat_axis=0, tiled=True)  38.2 us
    ppermute x6, starting transfers between devices, swap(): return lax.ppermute(value, axes, sorted(set(pairs)))  15.5 us
    pallas_call x1, Pallas kernels, step(): pl.pallas_call(kernel, out_shape=(jax.ShapeDtypeStruct((HALF_ROWS, OWN),...  9.14 us
    all_to_all x1, starting transfers between devices, all_to_all(): return lax.all_to_all(value, axes, split_axis=0, concat_axis=0, tiled=True)  6.79 us
    pallas_call x1, Pallas kernels, regress(): pl.pallas_call(regression_kernel, out_shape=(jax.ShapeDtypeStruct((ROWS,...  4.27 us
    ppermute x6, waiting for transfers between devices, swap(): return lax.ppermute(value, axes, sorted(set(pairs)))  3.41 us
    pallas_call x1, Pallas kernels, unpack(): pl.pallas_call(unpack_kernel, out_shape=tuple((jax.ShapeDtypeStruct(shape...  2.11 us
  transfers between devices with their start and end apart: 7, of which 3 were waited for; matrix products, arithmetic and copies ran while one was open for 0% of the time, Pallas kernels for 5%

profile of v11, /device:TPU:1, one launch (start us, length us, event | category | flops | bytes accessed | tf_op | source)
XLA Modules:
  0.0 83.8 jit_solution(5197715763203656545)
XLA Ops:
  1.3 1.6 %pack.1 = (f32[8,2,16,128]{3,2,1,0:T(8,128)}, bf16[16,16,128]{2,1,0:T(8,128)(2,1)S(1)}) custom-call(s32[1,1]{1,0:T(1,128)S(6)} %copy.17.level, f32[4,2,1024]{2,1,0:T(2,128)} %target_far.1, f32[4,2,1024]{2,1,0:T(2,128)} %noise_far.1, s32[2,1024]{1,0:T(2,128)} %mask_far.1, bf16[12,16,128]{2,1,0:T(8,128)(2,1)} %coarse_far.1), custom_call_target="tpu_custom_call" | custom-call | tf_op jit(solution)/shard_map/pack/pallas_call | solution.py:583
  2.9 6.8 %all-to-all-start = ((f32[8,2,16,128]{3,2,1,0:T(8,128)}), f32[8,2,16,128]{3,2,1,0:T(8,128)S(1)}, u32[]{:S(2)}, u32[]{:S(2)}) async-start(f32[8,2,16,128]{3,2,1,0:T(8,128)} %get-tuple-element.17), calls=%async_computation | async-start | bytes 262144 | tf_op jit(solution)/shard_map/all_to_all | solution.py:701
  9.7 4.7 %collective-permute-start.3 = (bf16[16,16,128]{2,1,0:T(8,128)(2,1)S(1)}, bf16[16,16,128]{2,1,0:T(8,128)(2,1)S(1)}, u32[]{:S(2)}, u32[]{:S(2)}) collective-permute-start(bf16[16,16,128]{2,1,0:T(8,128)(2,1)S(1)} %get-tuple-element.18.own), channel_id=1, source_target_pairs={{0,127},{1,2},{2,1},{3,4},{4,3},{5,6},{6,5},{7,8},{8,7},{9,10},{10... | collective-permute-start | bytes 196616 | tf_op jit(solution)/shard_map/ppermute | solution.py:714
  14.4 0.0 collective-permute-start.2
  14.4 0.1 pad_add_fusion.place.refs_0_
  14.5 0.7 all-to-all-done
  15.1 3.2 %collective-permute-start.1 = (f32[16,16,128]{2,1,0:T(8,128)S(1)}, f32[16,16,128]{2,1,0:T(8,128)S(1)}, u32[]{:S(2)}, u32[]{:S(2)}) collective-permute-start(f32[16,16,128]{2,1,0:T(8,128)S(1)} %bitcast.19), channel_id=1, source_target_pairs={{0,127},{1,2},{2,1},{3,4},{4,3},{5,6},{6,5},{7,8},{8,7},{9,10},{10... | collective-permute-start | bytes 393224 | tf_op jit(solution)/shard_map/ppermute | solution.py:714
  18.3 0.0 collective-permute-start
  18.3 0.0 collective-permute-done.3.across
  18.3 0.0 collective-permute-done.2.pair
  18.3 0.0 copy-start
  18.3 0.0 copy-start.1
  18.3 0.0 copy-start.2
  18.3 0.0 copy-start.3
  18.3 4.3 %regress.1 = (f32[16,8,256]{2,1,0:T(8,128)S(1)}, f32[16,16,256]{2,1,0:T(8,128)S(1)}) custom-call(s32[2]{0:T(128)S(1)} %pad_add_fusion.place.refs_0_, bf16[16,16,128]{2,1,0:T(8,128)(2,1)S(1)} %get-tuple-element.18.own, bf16[16,16,128]{2,1,0:T(8,128)(2,1)S(1)} %collective-permute-done.2.pair, bf16[16,16,128]{2,1,0:T(8,128)(2,1)S(1)} %collective-permute-done.3.across, ...), custom_call_target="tpu_custom_call" | custom-call | flops 2000000000 | bytes 2000000 | tf_op jit(solution)/shard_map/regress/pallas_call | solution.py:604
  22.6 0.0 collective-permute-done.1.refs_3_
  22.6 0.0 collective-permute-done.refs_2_
  22.6 0.0 copy-done
  22.7 0.0 copy-done.1
  22.7 0.0 copy-done.2
  22.7 9.1 %step.1 = (bf16[2560,128]{1,0:T(8,128)(2,1)S(1)}, bf16[2560,128]{1,0:T(8,128)(2,1)S(1)}, bf16[8,8,128]{2,1,0:T(8,128)(2,1)S(1)}) custom-call(s32[2]{0:T(128)S(1)} %pad_add_fusion.place.refs_0_, f32[16,16,128]{2,1,0:T(8,128)S(1)} %bitcast.21, f32[16,16,128]{2,1,0:T(8,128)S(1)} %collective-permute-done.refs_2_, ...), custom_call_target="tpu_custom_call" | custom-call | tf_op jit(solution)/shard_map/step/pallas_call | solution.py:633
  31.8 4.7 %collective-permute-start.4 = (bf16[2560,128]{1,0:T(8,128)(2,1)S(1)}, bf16[2560,128]{1,0:T(8,128)(2,1)S(1)}, u32[]{:S(2)}, u32[]{:S(2)}) collective-permute-start(bf16[2560,128]{1,0:T(8,128)(2,1)S(1)} %get-tuple-element.22), channel_id=1, source_target_pairs={{0,8},{8,0},{1,9},{9,1},{2,10},{10,2},{3,11},{11,3},{4,12},{12,4},... | collective-permute-start | bytes 1966088 | tf_op jit(solution)/shard_map/ppermute | solution.py:714
  36.5 1.7 %collective-permute-done.4 = bf16[2560,128]{1,0:T(8,128)(2,1)S(1)} collective-permute-done((bf16[2560,128]{1,0:T(8,128)(2,1)S(1)}, bf16[2560,128]{1,0:T(8,128)(2,1)S(1)}, u32[]{:S(2)}, u32[]{:S(2)}) %collective-permute-start.4) | collective-permute-done | bytes 655392 | tf_op jit(solution)/shard_map/ppermute | solution.py:714
  38.3 0.2 add_convert_fusion
  38.5 0.1 pad_maximum_fusion
  38.6 21.0 %all_to_all.15 = bf16[64,48,128]{2,1,0:T(8,128)(2,1)S(1)} all-to-all(bf16[64,48,128]{2,1,0:T(8,128)(2,1)S(1)} %pad_maximum_fusion), channel_id=1, replica_groups=mesh['y'=4,'x_hi'=2,'core'=2,'x_lo'=2,'z'=4] {'y','x_hi','x_lo','z'}, dimensions={0} | all-to-all | bytes 1572864 | tf_op jit(solution)/shard_map/all_to_all | solution.py:701
  59.6 0.1 slice_reduce_fusion
  59.7 0.1 broadcast_in_dim.5
  59.8 17.2 %all_to_all.16 = bf16[64,40,128]{2,1,0:T(8,128)(2,1)S(1)} all-to-all(bf16[64,40,128]{2,1,0:T(8,128)(2,1)S(1)} %broadcast_in_dim.5), channel_id=1, replica_groups=mesh['y'=4,'x_hi'=2,'core'=2,'x_lo'=2,'z'=4] {'y','x_hi','x_lo','z'}, dimensions={0} | all-to-all | bytes 1310720 | tf_op jit(solution)/shard_map/all_to_all | solution.py:701
  77.0 3.0 %collective-permute-start.5 = (bf16[2560,128]{1,0:T(8,128)(2,1)S(1)}, bf16[2560,128]{1,0:T(8,128)(2,1)S(1)}, u32[]{:S(2)}, u32[]{:S(2)}) collective-permute-start(bf16[2560,128]{1,0:T(8,128)(2,1)S(1)} %bitcast.15), channel_id=1, source_target_pairs={{0,8},{8,0},{1,9},{9,1},{2,10},{10,2},{3,11},{11,3},{4,12},{12,4},... | collective-permute-start | bytes 1966088 | tf_op jit(solution)/shard_map/ppermute | solution.py:714
  80.0 1.7 %collective-permute-done.5.other = bf16[2560,128]{1,0:T(8,128)(2,1)S(1)} collective-permute-done((bf16[2560,128]{1,0:T(8,128)(2,1)S(1)}, bf16[2560,128]{1,0:T(8,128)(2,1)S(1)}, u32[]{:S(2)}, u32[]{:S(2)}) %collective-permute-start.5) | collective-permute-done | bytes 655392 | tf_op jit(solution)/shard_map/ppermute | solution.py:714
  81.7 2.1 %unpack.1 = (f32[4,2,1024]{2,1,0:T(2,128)}, f32[3,3,20,128]{3,2,1,0:T(8,128)}, f32[3,3,256,128]{3,2,1,0:T(8,128)}, f32[3,3,128,256]{3,2,1,0:T(8,128)}, f32[3,3,4,128]{3,2,1,0:T(4,128)}) custom-call(s32[2]{0:T(128)S(1)} %pad_add_fusion.place.refs_0_, bf16[2560,128]{1,0:T(8,128)(2,1)S(1)} %bitcast.16, bf16[2560,128]{1,0:T(8,128)(2,1)S(1)} %collective-permute-done.5.other, ...), custom_call_target="tpu_custom_call" | custom-call | tf_op jit(solution)/shard_map/unpack/pallas_call | solution.py:686
  (4 shorter events, 0.1 us)
Async XLA Ops:
  2.9 12.2 %all-to-all-start = ((f32[8,2,16,128]{3,2,1,0:T(8,128)}), f32[8,2,16,128]{3,2,1,0:T(8,128)S(1)}, u32[]{:S(2)}, u32[]{:S(2)}) async-start(f32[8,2,16,128]{3,2,1,0:T(8,128)} %get-tuple-element.17), calls=%async_computation | async-start | bytes 262144 | tf_op jit(solution)/shard_map/all_to_all | solution.py:701
  9.7 8.6 %collective-permute-start.3 = (bf16[16,16,128]{2,1,0:T(8,128)(2,1)S(1)}, bf16[16,16,128]{2,1,0:T(8,128)(2,1)S(1)}, u32[]{:S(2)}, u32[]{:S(2)}) collective-permute-start(bf16[16,16,128]{2,1,0:T(8,128)(2,1)S(1)} %get-tuple-element.18.own), channel_id=1, source_target_pairs={{0,127},{1,2},{2,1},{3,4},{4,3},{5,6},{6,5},{7,8},{8,7},{9,10},{10... | collective-permute-start | bytes 196616 | tf_op jit(solution)/shard_map/ppermute | solution.py:714
  14.4 3.9 %collective-permute-start.2 = (bf16[16,16,128]{2,1,0:T(8,128)(2,1)S(1)}, bf16[16,16,128]{2,1,0:T(8,128)(2,1)S(1)}, u32[]{:S(2)}, u32[]{:S(2)}) collective-permute-start(bf16[16,16,128]{2,1,0:T(8,128)(2,1)S(1)} %get-tuple-element.18.own), channel_id=1, source_target_pairs={{0,1},{1,0},{2,3},{3,2},{4,5},{5,4},{6,7},{7,6},{8,9},{9,8},{10,11... | collective-permute-start | bytes 196616 | tf_op jit(solution)/shard_map/ppermute | solution.py:714
  15.1 7.5 %collective-permute-start.1 = (f32[16,16,128]{2,1,0:T(8,128)S(1)}, f32[16,16,128]{2,1,0:T(8,128)S(1)}, u32[]{:S(2)}, u32[]{:S(2)}) collective-permute-start(f32[16,16,128]{2,1,0:T(8,128)S(1)} %bitcast.19), channel_id=1, source_target_pairs={{0,127},{1,2},{2,1},{3,4},{4,3},{5,6},{6,5},{7,8},{8,7},{9,10},{10... | collective-permute-start | bytes 393224 | tf_op jit(solution)/shard_map/ppermute | solution.py:714
  18.3 4.4 %collective-permute-start = (f32[16,16,128]{2,1,0:T(8,128)S(1)}, f32[16,16,128]{2,1,0:T(8,128)S(1)}, u32[]{:S(2)}, u32[]{:S(2)}) collective-permute-start(f32[16,16,128]{2,1,0:T(8,128)S(1)} %bitcast.20), channel_id=1, source_target_pairs={{0,1},{1,0},{2,3},{3,2},{4,5},{5,4},{6,7},{7,6},{8,9},{9,8},{10,11... | collective-permute-start | bytes 393224 | tf_op jit(solution)/shard_map/ppermute | solution.py:714
  18.3 4.3 %copy-start = (bf16[3,3,256,128]{3,2,1,0:T(8,128)(2,1)S(1)}, bf16[3,3,256,128]{3,2,1,0:T(8,128)(2,1)}, u32[]{:S(2)}) copy-start(bf16[3,3,256,128]{3,2,1,0:T(8,128)(2,1)} %param.21) | copy-start | bytes 1769476
  18.3 4.3 %copy-start.1 = (bf16[3,3,128,256]{3,2,1,0:T(8,128)(2,1)S(1)}, bf16[3,3,128,256]{3,2,1,0:T(8,128)(2,1)}, u32[]{:S(2)}) copy-start(bf16[3,3,128,256]{3,2,1,0:T(8,128)(2,1)} %param.22) | copy-start | bytes 1769476
  18.3 4.3 %copy-start.2 = (bf16[3,3,128,20]{2,3,1,0:T(8,128)(2,1)S(1)}, bf16[3,3,128,20]{2,3,1,0:T(8,128)(2,1)}, u32[]{:S(2)}) copy-start(bf16[3,3,128,20]{2,3,1,0:T(8,128)(2,1)} %param.20) | copy-start | bytes 138244
  18.3 4.3 %copy-start.3 = (bf16[3,3,4,128]{3,2,1,0:T(4,128)(2,1)S(1)}, bf16[3,3,4,128]{3,2,1,0:T(4,128)(2,1)}, u32[]{:S(2)}) copy-start(bf16[3,3,4,128]{3,2,1,0:T(4,128)(2,1)} %refs_9_.1) | copy-start | bytes 27652
  31.8 6.4 %collective-permute-start.4 = (bf16[2560,128]{1,0:T(8,128)(2,1)S(1)}, bf16[2560,128]{1,0:T(8,128)(2,1)S(1)}, u32[]{:S(2)}, u32[]{:S(2)}) collective-permute-start(bf16[2560,128]{1,0:T(8,128)(2,1)S(1)} %get-tuple-element.22), channel_id=1, source_target_pairs={{0,8},{8,0},{1,9},{9,1},{2,10},{10,2},{3,11},{11,3},{4,12},{12,4},... | collective-permute-start | bytes 1966088 | tf_op jit(solution)/shard_map/ppermute | solution.py:714
  77.0 4.7 %collective-permute-start.5 = (bf16[2560,128]{1,0:T(8,128)(2,1)S(1)}, bf16[2560,128]{1,0:T(8,128)(2,1)S(1)}, u32[]{:S(2)}, u32[]{:S(2)}) collective-permute-start(bf16[2560,128]{1,0:T(8,128)(2,1)S(1)} %bitcast.15), channel_id=1, source_target_pairs={{0,8},{8,0},{1,9},{9,1},{2,10},{10,2},{3,11},{11,3},{4,12},{12,4},... | collective-permute-start | bytes 1966088 | tf_op jit(solution)/shard_map/ppermute | solution.py:714
